TPU v7x, 256 devices: a whole 4x4x8 slice. The times are simulated.
256 devices in a mesh: dom: 8 (over y, core), shard: 32 (over x, z).
Axes of the slice: x: 4, y: 4, z: 8, core: 2. Of those that a mesh axis runs over, the one named last changes fastest.
Arguments:
- features: bfloat16 [65536, 512], P(('dom', 'shard')), may hold values from -6 to 6
- w_self: bfloat16 [512, 512], replicated, may hold values from -0.25 to 0.25
- w_neigh: bfloat16 [512, 512], replicated, may hold values from -0.25 to 0.25
- cotangent: bfloat16 [65536, 512], P(('dom', 'shard')), may hold values from -6 to 6
- neighbours: int32 [65536, 32], P(('dom', 'shard')), may hold values from 0 to 640, as said below
- hub_slots: int32 [256], P(('dom', 'shard')), may hold values from 0 to 255, as said below
- send_rows: int32 [256, 32, 4], P(('dom', 'shard')), may hold values from 0 to 255, as said below
- send_counts: int32 [256, 32], P(('dom', 'shard')), may hold values from 1 to 4, as said below
Outputs:
- hidden: bfloat16 [65536, 512], P(('dom', 'shard'))
- grad_features: float32 [65536, 512], P(('dom', 'shard'))
- grad_self: float32 [512, 512], replicated
- grad_neigh: float32 [512, 512], replicated
Inputs may be any that keep to these rules, and one draw needn't show every extreme that they name: `neighbours`: padding slots (640) come after a vertex's live slots; each vertex has 4 to 32 live slots. A slot at or above 512 names peer p and position k with k below send_counts of that peer for this device. Hub indices are skewed: some hubs are read far more than others. `hub_slots`: the 1 entries of one device are distinct local rows. `send_rows`: rows may repeat; entries at or past a peer's count are not live. `send_counts`: in every partition group one shard index receives 4 rows from every peer.
All inputs are finite; a program needn't handle non-finite values.
Results may differ from a plain program's by a relative error of at most 0.0052.
Values may be sent and summed in bfloat16 or wider, within the bound.
No kernel may reach another device: no remote copies, remote signals or barrier semaphores. Data moves between devices by JAX's collectives and lax.ppermute only.
A program may use at most 64 MiB of HBM per device.

v0:
```python
import jax
import jax.numpy as jnp
from jax import lax
from jax.sharding import PartitionSpec as P

row_block = 128


def contract_rows(left, right):
    return lax.dot_general(
        left, right, (((0,), (0,)), ((), ())), preferred_element_type=jnp.float32
    )


def contract_cols(left, right):
    return lax.dot_general(
        left, right, (((1,), (1,)), ((), ())), preferred_element_type=jnp.float32
    )


def body(features, w_self, w_neigh, cotangent, neighbours, hub_slots, send_rows, send_counts):
    verts, width = features.shape
    slots = neighbours.shape[1]
    peers = lax.axis_size("shard")
    routes = send_rows[0]
    counts = send_counts[0]
    cap = routes.shape[1]
    live = jnp.arange(cap)[None, :] < counts[:, None]
    hub_local = features[hub_slots]
    hubs = lax.all_gather(hub_local, ("dom", "shard"), axis=0, tiled=True)
    outgoing = jnp.where(live[:, :, None], features[routes], jnp.zeros((), jnp.bfloat16))
    incoming = lax.all_to_all(outgoing, "shard", split_axis=0, concat_axis=0, tiled=True)
    hub_count = hubs.shape[0]
    table_size = verts + hub_count + peers * cap
    table = jnp.concatenate(
        [features, hubs, incoming.reshape(peers * cap, width), jnp.zeros((1, width), jnp.bfloat16)],
        axis=0,
    )
    degree = jnp.sum(neighbours < table_size, axis=1).astype(jnp.float32)
    blocks = neighbours.reshape(verts // row_block, row_block, slots)
    sums = lax.map(lambda blk: jnp.sum(table[blk], axis=1, dtype=jnp.float32), blocks).reshape(
        verts, width
    )
    agg = (sums / degree[:, None]).astype(jnp.bfloat16)
    z = jnp.dot(features, w_self, preferred_element_type=jnp.float32) + jnp.dot(
        agg, w_neigh, preferred_element_type=jnp.float32
    )
    sig = jax.nn.sigmoid(z)
    hidden = (z * sig).astype(jnp.bfloat16)
    dz = (cotangent.astype(jnp.float32) * sig * (1.0 + z * (1.0 - sig))).astype(jnp.bfloat16)
    grad_self, grad_neigh = lax.psum(
        (contract_rows(features, dz), contract_rows(agg, dz)), ("dom", "shard")
    )
    edge_grad = contract_cols(dz, w_neigh) / degree[:, None]
    grads = edge_grad.reshape(verts // row_block, row_block, width)

    def add_block(acc, pair):
        blk, grad = pair
        spread = jnp.broadcast_to(grad[:, None, :], (row_block, slots, width)).reshape(-1, width)
        return (acc.at[blk.reshape(-1)].add(spread), None)

    start = jnp.zeros((table_size + 1, width), jnp.float32)
    accum, _ = lax.scan(add_block, start, (blocks, grads))
    hub_part = accum[verts : verts + hub_count]
    hub_back = lax.psum_scatter(hub_part, ("dom", "shard"), scatter_dimension=0, tiled=True)
    recv_part = accum[verts + hub_count : table_size].reshape(peers, cap, width)
    returned = lax.all_to_all(
        recv_part.astype(jnp.bfloat16), "shard", split_axis=0, concat_axis=0, tiled=True
    ).astype(recv_part.dtype)
    returned = jnp.where(live[:, :, None], returned, 0.0)
    grad_features = contract_cols(dz, w_self) + accum[:verts]
    grad_features = grad_features.at[hub_slots].add(hub_back)
    grad_features = grad_features.at[routes.reshape(-1)].add(returned.reshape(-1, width))
    return (hidden, grad_features, grad_self, grad_neigh)


def solution(mesh):
    return jax.shard_map(
        body,
        mesh=mesh,
        in_specs=(
            P(("dom", "shard"), None),
            P(),
            P(),
            P(("dom", "shard"), None),
            P(("dom", "shard"), None),
            P(("dom", "shard")),
            P(("dom", "shard"), None, None),
            P(("dom", "shard"), None),
        ),
        out_specs=(P(("dom", "shard"), None), P(("dom", "shard"), None), P(), P()),
        check_vma=False,
    )
```

profile of v0, /device:TPU:1, one launch (start us, length us, event | category | flops | bytes accessed | tf_op | source)
XLA Modules:
  0.0 479.4 jit_solution(18046370803552838058)
XLA Ops:
  8.2 1.9 gather_fusion.1
  11.0 11.9 %all-to-all-start = ((bf16[32,4,512]{2,1,0:T(4,128)(2,1)}), bf16[32,4,512]{2,1,0:T(4,128)(2,1)S(1)}, u32[]{:S(2)}, u32[]{:S(2)}) async-start(bf16[32,4,512]{2,1,0:T(4,128)(2,1)} %broadcast_select_fusion), calls=%async_computation | async-start | bytes 262144 | tf_op jit(solution)/shard_map/all_to_all | solution.py:32
  23.7 70.5 %all-gather = bf16[256,1,512]{2,1,0:T(2,128)(2,1)S(1)} all-gather(bf16[1,1,512]{2,1,0:T(2,128)(2,1)S(1)} %dynamic-slice_bitcast_fusion.1), channel_id=1, replica_groups=mesh['dom'=8,'shard'=32] {'dom','shard'}, dimensions={0}, use_global_device_ids=true | all-gather | bytes 263168 | tf_op jit(solution)/shard_map/all_gather | solution.py:30
  94.9 42.3 %while.22 = (s32[]{:T(128)}, f32[2,128,512]{2,1,0:T(8,128)S(1)}, s32[2,128,32]{2,1,0:T(8,128)S(1)}, bf16[641,512]{1,0:T(8,128)(2,1)S(1)}, s32[]{:T(128)}) while((s32[]{:T(128)}, f32[2,128,512]{2,1,0:T(8,128)S(1)}, s32[2,128,32]{2,1,0:T(8,128)S(1)}, bf16[641,512]{1,0:T(8,128)(2,1)S(1)}, s32[]{:T(128)}) %tuple.59), condition=%wide.region_2.3_spmd, body=%wide.region_0.0_spmd.sunk | while | flops 4145154 | bytes 13484109 | solution.py:41
  95.0 17.3 %gather_fusion = bf16[4096,512]{1,0:T(8,128)(2,1)} fusion(bf16[641,512]{1,0:T(8,128)(2,1)S(1)} %get-tuple-element.173, s32[4096]{0:T(1024)S(1)} %broadcast_clamp_fusion.2), kind=kCustom, calls=%fused_computation.clone.1 | custom fusion | bytes 8404992 | tf_op jit(solution)/shard_map/while/body/eval_jaxpr/gather | solution.py:41
  112.3 3.7 convert_reduce_fusion.3
  116.2 17.3 %gather_fusion = bf16[4096,512]{1,0:T(8,128)(2,1)} fusion(bf16[641,512]{1,0:T(8,128)(2,1)S(1)} %get-tuple-element.173, s32[4096]{0:T(1024)S(1)} %broadcast_clamp_fusion.2), kind=kCustom, calls=%fused_computation.clone.1 | custom fusion | bytes 8404992 | tf_op jit(solution)/shard_map/while/body/eval_jaxpr/gather | solution.py:41
  133.5 3.7 convert_reduce_fusion.3
  137.4 1.2 multiply_convert_fusion
  138.9 1.3 convolution_bitcast_fusion
  140.2 1.3 fusion.3
  141.7 61.5 %while.23 = (s32[]{:T(128)}, f32[641,512]{1,0:T(8,128)S(1)}, s32[2,128,32]{2,1,0:T(8,128)S(1)}, f32[2,128,512]{2,1,0:T(8,128)S(1)}, s32[]{:T(128)}) while((s32[]{:T(128)}, f32[641,512]{1,0:T(8,128)S(1)}, s32[2,128,32]{2,1,0:T(8,128)S(1)}, f32[2,128,512]{2,1,0:T(8,128)S(1)}, s32[]{:T(128)}) %tuple.61), condition=%wide.region_6.7_spmd, body=%wide.region_4.6_spmd.sunk | while | flops 2109442 | bytes 34455628 | solution.py:63
  141.9 4.3 broadcast_in_dim.68
  146.2 26.3 %scatter_fusion = f32[641,512]{1,0:T(8,128)S(1)} fusion(f32[641,512]{1,0:T(8,128)S(1)} %get-tuple-element.181, s32[4096]{0:T(1024)S(1)} %bitcast.62, f32[4096,512]{1,0:T(8,128)} %bitcast.59), kind=kCustom, calls=%fused_computation.2.clone.1 | custom fusion | flops 2097152 | bytes 25182208 | tf_op jit(solution)/shard_map/while/body/eval_jaxpr/scatter-add | solution.py:60
  172.6 4.3 broadcast_in_dim.68
  177.0 26.3 %scatter_fusion = f32[641,512]{1,0:T(8,128)S(1)} fusion(f32[641,512]{1,0:T(8,128)S(1)} %get-tuple-element.181, s32[4096]{0:T(1024)S(1)} %bitcast.62, f32[4096,512]{1,0:T(8,128)} %bitcast.59), kind=kCustom, calls=%fused_computation.2.clone.1 | custom fusion | flops 2097152 | bytes 25182208 | tf_op jit(solution)/shard_map/while/body/eval_jaxpr/scatter-add | solution.py:60
  203.2 0.8 slice.25
  206.4 6.9 %all-to-all-start.1 = ((bf16[32,4,512]{2,1,0:T(4,128)(2,1)}), bf16[32,4,512]{2,1,0:T(4,128)(2,1)S(1)}, u32[]{:S(2)}, u32[]{:S(2)}) async-start(bf16[32,4,512]{2,1,0:T(4,128)(2,1)} %convert_element_type.38), calls=%async_computation.1 | async-start | bytes 262144 | tf_op jit(solution)/shard_map/all_to_all | solution.py:67
  213.7 9.2 %all-to-all-done.1 = bf16[32,4,512]{2,1,0:T(4,128)(2,1)S(1)} async-done(((bf16[32,4,512]{2,1,0:T(4,128)(2,1)}), bf16[32,4,512]{2,1,0:T(4,128)(2,1)S(1)}, u32[]{:S(2)}, u32[]{:S(2)}) %all-to-all-start.1) | async-done | bytes 131104 | tf_op jit(solution)/shard_map/all_to_all | solution.py:67
  223.2 242.8 %all-reduce.4.cloned.1.call-done = (f32[256,512]{1,0:T(8,128)}, f32[512,512]{0,1:T(8,128)}, f32[512,512]{1,0:T(8,128)}) async-done(((f32[256,512]{1,0:T(8,128)}, f32[512,512]{0,1:T(8,128)}, f32[512,512]{1,0:T(8,128)}), (f32[256,512]{1,0:T(8,128)}, f32[512,512]{0,1:T(8,128)}, f32[512,512]{1,0:T(8,128)})) %all-reduce.4.cloned.1.call-update) | async-done | bytes 2621456
  465.9 1.3 broadcast_select_fusion.1
  467.3 2.5 copy.27
  469.9 1.5 scatter_fusion.1
  471.4 1.0 copy.51
  (79 shorter events, 6.8 us)
Async XLA Ops:
  7.2 130.2 %copy-start = (bf16[512,512]{1,0:T(8,128)(2,1)S(1)}, bf16[512,512]{1,0:T(8,128)(2,1)}, u32[]{:S(2)}) copy-start(bf16[512,512]{1,0:T(8,128)(2,1)} %param.16) | copy-start | bytes 1572868
  7.2 16.5 %copy-start.2 = (bf16[256,512]{1,0:T(8,128)(2,1)S(1)}, bf16[256,512]{1,0:T(8,128)(2,1)}, u32[]{:S(2)}) copy-start(bf16[256,512]{1,0:T(8,128)(2,1)} %param.14) | copy-start | bytes 786436
  7.2 2.9 copy-start.12
  7.2 15.7 %copy-start.8 = (s32[256,32]{0,1:T(8,128)S(1)}, s32[256,32]{0,1:T(8,128)}, u32[]{:S(2)}) copy-start(s32[256,32]{0,1:T(8,128)} %param.18) | copy-start | bytes 98308
  10.0 84.3 %copy-start.5 = (bf16[512,512]{1,0:T(8,128)(2,1)S(1)}, bf16[512,512]{1,0:T(8,128)(2,1)}, u32[]{:S(2)}) copy-start(bf16[512,512]{1,0:T(8,128)(2,1)} %param.15) | copy-start | bytes 1572868
  10.2 0.8 copy-start.9
  11.0 83.7 %all-to-all-start = ((bf16[32,4,512]{2,1,0:T(4,128)(2,1)}), bf16[32,4,512]{2,1,0:T(4,128)(2,1)S(1)}, u32[]{:S(2)}, u32[]{:S(2)}) async-start(bf16[32,4,512]{2,1,0:T(4,128)(2,1)} %broadcast_select_fusion), calls=%async_computation | async-start | bytes 262144 | tf_op jit(solution)/shard_map/all_to_all | solution.py:32
  22.8 443.1 %all-reduce.4.cloned.1.call-start = ((), (), s32[]{:S(2)}) async-start(), calls=%async_computation.2 | async-start | bytes 5242880
  94.9 42.5 %copy-start.14 = (bf16[256,512]{1,0:T(8,128)(2,1)S(1)}, bf16[256,512]{1,0:T(8,128)(2,1)}, u32[]{:S(2)}) copy-start(bf16[256,512]{1,0:T(8,128)(2,1)} %param.17) | copy-start | bytes 786436
  138.6 1.6 copy-start.3
  204.1 0.7 copy-start.11
  204.1 0.9 copy-start.13
  204.1 9.3 %copy-start.4 = (bf16[256,512]{1,0:T(8,128)(2,1)S(1)}, bf16[256,512]{1,0:T(8,128)(2,1)}, u32[]{:S(2)}) copy-start(bf16[256,512]{1,0:T(8,128)(2,1)} %copy-done.3) | copy-start | bytes 786436
  204.1 9.3 %copy-start.6 = (bf16[512,512]{1,0:T(8,128)(2,1)S(1)}, bf16[512,512]{1,0:T(8,128)(2,1)}, u32[]{:S(2)}) copy-start(bf16[512,512]{1,0:T(8,128)(2,1)} %param.15) | copy-start | bytes 1572868
  204.8 18.1 %copy-start.10 = (pred[32,4]{1,0:T(8,128)(4,1)S(1)}, pred[32,4]{1,0:T(8,128)(4,1)}, u32[]{:S(2)}) copy-start(pred[32,4]{1,0:T(8,128)(4,1)} %copy-done.9) | copy-start | bytes 388
  206.4 16.5 %all-to-all-start.1 = ((bf16[32,4,512]{2,1,0:T(4,128)(2,1)}), bf16[32,4,512]{2,1,0:T(4,128)(2,1)S(1)}, u32[]{:S(2)}, u32[]{:S(2)}) async-start(bf16[32,4,512]{2,1,0:T(4,128)(2,1)} %convert_element_type.38), calls=%async_computation.1 | async-start | bytes 262144 | tf_op jit(solution)/shard_map/all_to_all | solution.py:67
  469.9 1.6 copy-start.7
  471.4 1.1 copy-start.1
Sparse Core Ops, SparseCore 0:
  204.2 261.6 all-reduce.3
where the time goes:
time: 481 us; the launch traced here: 479 us
  waiting for transfers between devices  252 us (52%)
  blocking collectives  70.5 us (15%)
  other arithmetic  65.7 us (14%)
  local copies, waits for them, and re-layouts  52.4 us (11%)
  starting transfers between devices  18.8 us (4%)
  between operations  15 us (3%)
    unnamed x2, waiting for transfers between devices  243 us
    all_gather x1, blocking collectives, body(): hubs = lax.all_gather(hub_local, ('dom', 'shard'), axis=0, tiled=True)  70.5 us
    scatter-add x2, other arithmetic, add_block(): return (acc.at[blk.reshape(-1)].add(spread), None)  52.5 us
    gather x2, local copies, waits for them, and re-layouts, body(): table[blk]  34.6 us
    all_to_all x1, starting transfers between devices, body(): lax.all_to_all(outgoing, 'shard', split_axis=0, concat_axis=0, tiled=True)  11.9 us
  transfers between devices with their start and end apart: 3, of which 2 were waited for; matrix products, arithmetic and copies ran while one was open for 1% of the time, Pallas kernels for 0%

commit v1 on v0

v1 whole, which is shorter than its diff:
```python
import functools

import jax
import jax.numpy as jnp
from jax import lax
from jax.experimental import pallas as pl
from jax.experimental.pallas import tpu as pltpu
from jax.sharding import PartitionSpec as P

BF = jnp.bfloat16
F32 = jnp.float32
I32 = jnp.int32
PACK = 8
HUB_ROW = 4


def dot(a, b, ca=1, cb=0):
    return lax.dot_general(a, b, (((ca,), (cb,)), ((), ())), preferred_element_type=F32)


def call(kernel, outs, name, flops=0, nbytes=0, vmem=None):
    outs = [jax.ShapeDtypeStruct(s, d) for s, d in outs]
    spec = pl.BlockSpec(memory_space=pltpu.VMEM)

    def run(*args):
        return pl.pallas_call(
            kernel,
            out_shape=outs,
            in_specs=[spec] * len(args),
            out_specs=[spec] * len(outs),
            name=name,
            compiler_params=pltpu.CompilerParams(vmem_limit_bytes=vmem or (32 << 20)),
            cost_estimate=pl.CostEstimate(
                flops=flops or 1 << 20, bytes_accessed=nbytes or 1 << 20, transcendentals=0
            ),
        )(*args)

    return run


def place():
    dom = lax.axis_index("dom")
    return dom // 2, dom % 2


def iota(shape, dim):
    return lax.broadcasted_iota(I32, shape, dim)


def count_kernel(nb_ref, feat_ref, ws_ref, ct_ref, c_ref, deg_ref, zs_ref, s1_ref, *, table):
    verts, slots = nb_ref.shape
    packed = ct_ref.shape[0] - verts - 256
    y, c = place()
    nb = nb_ref[...]
    deg_ref[...] = jnp.sum((nb < table).astype(F32), axis=1, keepdims=True)
    nbt = nb.astype(F32).T.astype(I32)
    step = 64
    for t in range(0, ct_ref.shape[0], step):
        r = iota((step, verts), 0) + t
        if t < verts:
            want = r
        elif t < verts + packed:
            b = r - verts
            k = lax.rem(b, PACK)
            want = jnp.where(k < 4, verts + 256 + (b // PACK) * 4 + k, -1)
        else:
            block = (t - verts - packed) // 64
            i = r - (verts + packed + block * 64)
            dom = lax.rem(y - block + 4, 4) * 2
            want = verts + jnp.where(i < 32, (dom + c) * 32 + i, (dom + 1 - c) * 32 + i - 32)
        acc = jnp.zeros((step, verts), F32)
        for j in range(slots):
            acc = acc + jnp.where(nbt[j : j + 1, :] == want, 1.0, 0.0)
        ct_ref[t : t + step, :] = acc.astype(BF)
        c_ref[:, t : t + step] = acc.T.astype(BF)
    feat = feat_ref[...]
    zs_ref[...] = dot(feat, ws_ref[...])
    s1_ref[...] = dot(c_ref[:, :verts], feat)


def forward_kernel(
    feat_ref, cot_ref, wn_ref, c_ref, deg_ref, zs_ref, s1_ref, bnd_ref, h0_ref, hp_ref, h1_ref, h2_ref, h3_ref,
    hid_ref, dz_ref, send_ref, keep_ref,
):
    verts, width = feat_ref.shape
    _, c = place()
    packed = bnd_ref.shape[0] * PACK
    bnd = bnd_ref[...].reshape(packed, width)
    hubs = jnp.concatenate([h0_ref[...], hp_ref[...], h1_ref[...], h2_ref[...], h3_ref[...]], axis=0)
    sums = s1_ref[...] + dot(c_ref[:, verts : verts + packed], bnd) + dot(c_ref[:, verts + packed :], hubs)
    agg = (sums / deg_ref[...]).astype(BF)
    z = zs_ref[...] + dot(agg, wn_ref[...])
    sig = jax.nn.sigmoid(z)
    hid_ref[...] = (z * sig).astype(BF)
    dz = (cot_ref[...].astype(F32) * sig * (1.0 + z * (1.0 - sig))).astype(BF)
    dz_ref[...] = dz
    feat = feat_ref[...]
    first = c == 0
    send_ref[...] = dot(jnp.where(first, agg, feat), dz, 0, 0).astype(BF)
    keep_ref[...] = dot(jnp.where(first, feat, agg), dz, 0, 0)


def backward_kernel(dz_ref, wn_ref, ws_ref, deg_ref, ct_ref, base_ref, bnd_ref, hsend_ref, hkeep_ref):
    verts, width = dz_ref.shape
    packed = bnd_ref.shape[0]
    dz = dz_ref[...]
    edge = (dot(dz, wn_ref[...], 1, 1) / deg_ref[...]).astype(BF)
    base_ref[...] = dot(dz, ws_ref[...], 1, 1) + dot(ct_ref[:verts, :], edge)
    bnd_ref[...] = dot(ct_ref[verts : verts + packed, :], edge).astype(BF)
    hub = dot(ct_ref[verts + packed :, :], edge)
    for k in range(4):
        hkeep_ref[k] = hub[k * 64 : k * 64 + 32]
        hsend_ref[k] = hub[k * 64 + 32 : k * 64 + 64].astype(BF)


def half_kernel(keep_ref, got_ref, own_ref, s1_ref, s2_ref, s3_ref):
    y, _ = place()
    own_ref[...] = keep_ref[y] + got_ref[y].astype(F32)
    for k, ref in ((1, s1_ref), (2, s2_ref), (3, s3_ref)):
        j = lax.rem(y + k, 4)
        ref[...] = (keep_ref[j] + got_ref[j].astype(F32)).astype(BF)


def hub_half_kernel(keep_ref, got_ref, own_ref, s1_ref, s2_ref, s3_ref):
    own_ref[...] = keep_ref[0] + got_ref[0].astype(F32)
    for k, ref in ((1, s1_ref), (2, s2_ref), (3, s3_ref)):
        ref[...] = (keep_ref[k] + got_ref[k].astype(F32)).astype(BF)


def spread(rows, packed, first, per):
    r = iota((packed, rows), 0)
    k = lax.rem(r, PACK) - first
    pick = jnp.where((k >= 0) & (k < per), (r // PACK) * per + k, -1)
    return (pick == iota((packed, rows), 1)).astype(BF)


def second_pack_kernel(own_ref, r1_ref, r2_ref, r3_ref, bnd_ref, out_ref):
    w = own_ref[...] + r1_ref[...].astype(F32) + r2_ref[...].astype(F32) + r3_ref[...].astype(F32)
    packed, width = bnd_ref.shape
    out = bnd_ref[...].astype(F32) + dot(spread(w.shape[0], packed, 4, 4), w.astype(BF))
    out_ref[...] = out.astype(BF).reshape(out_ref.shape)


def third_pack_kernel(got_ref, own_ref, r1_ref, r2_ref, r3_ref, out_ref):
    peers, pack, width = got_ref.shape
    packed = peers * pack
    hub = own_ref[...] + r1_ref[...].astype(F32) + r2_ref[...].astype(F32) + r3_ref[...].astype(F32)
    rows = dot(spread(hub.shape[0], packed, HUB_ROW, 1), hub.astype(BF)).astype(BF)
    total = jnp.sum(got_ref[...].astype(F32), axis=0)
    low = jnp.concatenate([total[4:], jnp.zeros((4, width), F32)], axis=0)
    out_ref[...] = (rows.astype(F32).reshape(peers, pack, width) + low[None]).astype(BF)


def unpack_kernel(got_ref, out_ref):
    peers, pack, width = got_ref.shape
    packed = peers * pack
    rows = out_ref.shape[0]
    r = iota((rows, packed), 0)
    pick = (r // 4) * PACK + lax.rem(r, 4)
    sel = (pick == iota((rows, packed), 1)).astype(BF)
    out_ref[...] = dot(sel, got_ref[...].reshape(packed, width)).astype(BF)


def grad_kernel(base_ref, sel_ref, second_ref, third_ref, out_ref):
    peers, pack, width = second_ref.shape
    packed = peers * pack
    k = lax.rem(iota((packed, width), 0), PACK)
    second = second_ref[...].reshape(packed, width)
    third = third_ref[...].reshape(packed, width)
    zero = jnp.zeros_like(second)
    both = jnp.where(k < 4, second, jnp.where(k == HUB_ROW, third, zero))
    out_ref[...] = base_ref[...] + dot(sel_ref[...], both, 0, 0)


def weight_kernel(a0, a1, a2, a3, b0, b1, b2, b3, self_ref, neigh_ref):
    y, c = place()
    first = c == 0
    for k, (a, b) in enumerate(((a0, b0), (a1, b1), (a2, b2), (a3, b3))):
        j = lax.rem(y - k + 4, 4)
        mine, other = a[...].astype(F32), b[...].astype(F32)
        self_ref[j] = jnp.where(first, mine, other)
        neigh_ref[j] = jnp.where(first, other, mine)


def swap_core(x):
    return lax.ppermute(x, "dom", [(i, i ^ 1) for i in range(8)])


def shift_y(x, k):
    return lax.ppermute(x, "dom", [(i, ((i // 2 + k) % 4) * 2 + i % 2) for i in range(8)])


def exchange(x):
    return lax.all_to_all(x, "shard", split_axis=0, concat_axis=0, tiled=True)


def body(features, w_self, w_neigh, cotangent, neighbours, hub_slots, send_rows, send_counts):
    verts, width = features.shape
    peers, cap = send_rows.shape[1:]
    hubs = 256
    packed = peers * PACK
    table = verts + hubs + peers * cap
    rows = verts + packed + hubs

    slot = jnp.arange(PACK)[None, :]
    routes = jnp.pad(send_rows[0], ((0, 0), (0, PACK - cap)), constant_values=-1)
    index = jnp.where(slot < send_counts[0][:, None], routes, -1)
    index = jnp.where(slot == HUB_ROW, hub_slots[0], index)
    sel = (index[:, :, None] == jnp.arange(verts)).astype(BF).reshape(packed, verts)
    outgoing = dot(sel, features).astype(BF).reshape(peers, PACK, width)
    first = exchange(outgoing)

    ct, cm, degree, z_self, s_local = call(
        functools.partial(count_kernel, table=table),
        [((rows, verts), BF), ((verts, rows), BF), ((verts, 1), F32), ((verts, width), F32), ((verts, width), F32)],
        "count",
    )(neighbours, features, w_self)

    hub_own = first[:, HUB_ROW]
    hub_other = swap_core(hub_own)
    hub_pair = jnp.concatenate([hub_own, hub_other], axis=0)
    hub_far = [shift_y(hub_pair, k) for k in (1, 2, 3)]

    hidden, dz, w_send, w_keep = call(
        forward_kernel,
        [((verts, width), BF), ((verts, width), BF), ((width, width), BF), ((width, width), F32)],
        "forward",
    )(features, cotangent, w_neigh, cm, degree, z_self, s_local, first, hub_own, hub_other, *hub_far)

    w_got = swap_core(w_send)
    base, bnd_back, hub_send, hub_keep = call(
        backward_kernel,
        [((verts, width), F32), ((packed, width), BF), ((4, 32, width), BF), ((4, 32, width), F32)],
        "backward",
    )(dz, w_neigh, w_self, degree, ct)

    chunk = width // 4
    w_own, *w_out = call(half_kernel, [((chunk, width), F32)] + [((chunk, width), BF)] * 3, "half")(
        w_keep.reshape(4, chunk, width), w_got.reshape(4, chunk, width)
    )
    w_in = [shift_y(w_out[k - 1], k) for k in (1, 2, 3)]

    hub_got = swap_core(hub_send)
    h_own, *h_out = call(hub_half_kernel, [((32, width), F32)] + [((32, width), BF)] * 3, "hubhalf")(
        hub_keep, hub_got
    )
    h_in = [shift_y(h_out[k - 1], -k) for k in (1, 2, 3)]

    pack = call(second_pack_kernel, [((peers, PACK, width), BF)], "pack")(w_own, *w_in, bnd_back)[0]
    second = exchange(pack)
    pack = call(third_pack_kernel, [((peers, PACK, width), BF)], "pack2")(second, h_own, *h_in)[0]
    third = exchange(pack)
    w_part = call(unpack_kernel, [((chunk, width), BF)], "unpack")(third)[0]

    mine = [w_part] + [shift_y(w_part, k) for k in (1, 2, 3)]
    other = [swap_core(x) for x in mine]
    grad_features = call(grad_kernel, [((verts, width), F32)], "grad")(base, sel, second, third)[0]
    grad_self, grad_neigh = call(weight_kernel, [((4, chunk, width), F32)] * 2, "weights")(*mine, *other)
    return (hidden, grad_features, grad_self.reshape(width, width), grad_neigh.reshape(width, width))


def solution(mesh):
    vertex = P(("dom", "shard"), None)
    return jax.shard_map(
        body,
        mesh=mesh,
        in_specs=(
            vertex,
            P(),
            P(),
            vertex,
            vertex,
            P(("dom", "shard")),
            P(("dom", "shard"), None, None),
            vertex,
        ),
        out_specs=(vertex, vertex, P(), P()),
        check_vma=False,
    )
```

time: 481 us -> 101 us (0.21)
  waiting for transfers between devices: 252 us -> 11.4 us
  other arithmetic: 65.7 us -> 0.18 us
  local copies, waits for them, and re-layouts: 52.4 us -> 1.04 us
  blocking collectives: 70.5 us -> 39.9 us
  starting transfers between devices: 18.8 us -> 35.5 us
  between operations: 15 us -> 1.49 us
  Pallas kernels: 0 us -> 9.45 us
    unnamed x2 -> x0, waiting for transfers between devices: 243 us -> none
    all_gather x1 -> x0, blocking collectives: 70.5 us -> none  [body(): hubs = lax.all_gather(hub_local, ('dom', 'shard'), axis=0, tiled=True)]
    scatter-add x3 -> x0, other arithmetic: 54.1 us -> none  [the longest x2 52.5 us: add_block(): return (acc.at[blk.reshape(-1)].add(spread), None)]
    all_to_all x0 -> x2, blocking collectives: none -> 39.9 us  [exchange(): return lax.all_to_all(x, 'shard', split_axis=0, concat_axis=0, tiled=True)]
    gather x4 -> x0, local copies, waits for them, and re-layouts: 36.5 us -> none  [the longest x2 34.6 us: body(): table[blk]]
    ppermute x0 -> x19, starting transfers between devices: none -> 31.4 us  [the longest x7 16.2 us: swap_core(): return lax.ppermute(x, 'dom', [(i, i ^ 1) for i in range(8)])]
    all_to_all x2 -> x1, starting transfers between devices: 18.8 us -> 4.12 us  [exchange(): return lax.all_to_all(x, 'shard', split_axis=0, concat_axis=0, tiled=True)]
    ppermute x0 -> x19, waiting for transfers between devices: none -> 10.9 us  [the longest x12 7.5 us: shift_y(): lax.ppermute(x, 'dom', [(i, (i // 2 + k) % 4 * 2 + i % 2) for i in range(...]
  transfers between devices with their start and end apart: 3 -> 20, of which waited for: 2 -> 9; matrix products, arithmetic and copies ran while one was open for 1% -> 0% of each run, Pallas kernels for 0% -> 5%
where the time goes in v1:
time: 101 us; the launch traced here: 100 us
  blocking collectives  39.9 us (40%)
  starting transfers between devices  35.5 us (35%)
  waiting for transfers between devices  11.4 us (11%)
  Pallas kernels  9.45 us (9%)
  between operations  1.49 us (1%)
  matrix products  1.22 us (1%)
  local copies, waits for them, and re-layouts  1.04 us (1%)
    all_to_all x2, blocking collectives, exchange(): return lax.all_to_all(x, 'shard', split_axis=0, concat_axis=0, tiled=True)  39.9 us
    ppermute x7, starting transfers between devices, swap_core(): return lax.ppermute(x, 'dom', [(i, i ^ 1) for i in range(8)])  16.2 us
    ppermute x12, starting transfers between devices, shift_y(): lax.ppermute(x, 'dom', [(i, (i // 2 + k) % 4 * 2 + i % 2) for i in range(...  15.2 us
    pallas_call x10, Pallas kernels, run(): pl.pallas_call(kernel, out_shape=outs, in_specs=[spec] * len(args), out_s...  9.45 us
    ppermute x12, waiting for transfers between devices, shift_y(): lax.ppermute(x, 'dom', [(i, (i // 2 + k) % 4 * 2 + i % 2) for i in range(...  7.5 us
    all_to_all x1, starting transfers between devices, exchange(): return lax.all_to_all(x, 'shard', split_axis=0, concat_axis=0, tiled=True)  4.12 us
    ppermute x7, waiting for transfers between devices, swap_core(): return lax.ppermute(x, 'dom', [(i, i ^ 1) for i in range(8)])  3.39 us
  transfers between devices with their start and end apart: 20, of which 9 were waited for; matrix products, arithmetic and copies ran while one was open for 0% of the time, Pallas kernels for 5%

profile of v1, /device:TPU:1, one launch (start us, length us, event | category | flops | bytes accessed | tf_op | source)
XLA Modules:
  0.0 100.2 jit_solution(16529590301778417439)
XLA Ops:
  2.2 1.2 %fusion = bf16[32,8,512]{2,1,0:T(8,128)(2,1)S(1)} fusion(bf16[256,512]{1,0:T(8,128)(2,1)} %feat_ref.3, s32[256]{0:T(256)S(1)} %eq.26), kind=kOutput, calls=%fused_computation.1 | convolution fusion | flops 67305472 | bytes 525312 | tf_op jit(solution)/shard_map/dot_general | solution.py:18
  3.5 21.5 %all_to_all.15.bnd_ref = bf16[32,8,512]{2,1,0:T(8,128)(2,1)S(1)} all-to-all(bf16[32,8,512]{2,1,0:T(8,128)(2,1)S(1)} %fusion), channel_id=1, replica_groups=mesh['dom'=8,'shard'=32] {'shard'}, dimensions={0} | all-to-all | bytes 524288 | tf_op jit(solution)/shard_map/all_to_all | solution.py:194
  25.0 3.8 %collective-permute-start = (bf16[32,512]{1,0:T(8,128)(2,1)S(1)}, bf16[32,512]{1,0:T(8,128)(2,1)S(1)}, u32[]{:S(2)}, u32[]{:S(2)}) collective-permute-start(bf16[32,512]{1,0:T(8,128)(2,1)S(1)} %bitcast.16), channel_id=1, source_target_pairs={{0,32},{32,0},{64,96},{96,64},{128,160},{160,128},{192,224},{224,1... | collective-permute-start | bytes 98312 | tf_op jit(solution)/shard_map/ppermute | solution.py:186
  29.7 1.3 %collective-permute-start.1 = (bf16[64,512]{1,0:T(8,128)(2,1)S(1)}, bf16[64,512]{1,0:T(8,128)(2,1)S(1)}, u32[]{:S(2)}, u32[]{:S(2)}) collective-permute-start(bf16[64,512]{1,0:T(8,128)(2,1)S(1)} %pad_maximum_fusion), channel_id=1, source_target_pairs={{0,64},{32,96},{64,128},{96,160},{128,192},{160,224},{192,0},{224,... | collective-permute-start | bytes 196616 | tf_op jit(solution)/shard_map/ppermute | solution.py:190
  31.1 2.6 %collective-permute-start.2 = (bf16[64,512]{1,0:T(8,128)(2,1)S(1)}, bf16[64,512]{1,0:T(8,128)(2,1)S(1)}, u32[]{:S(2)}, u32[]{:S(2)}) collective-permute-start(bf16[64,512]{1,0:T(8,128)(2,1)S(1)} %pad_maximum_fusion), channel_id=1, source_target_pairs={{0,128},{32,160},{64,192},{96,224},{128,0},{160,32},{192,64},{224,... | collective-permute-start | bytes 196616 | tf_op jit(solution)/shard_map/ppermute | solution.py:190
  33.7 1.1 %collective-permute-start.3 = (bf16[64,512]{1,0:T(8,128)(2,1)S(1)}, bf16[64,512]{1,0:T(8,128)(2,1)S(1)}, u32[]{:S(2)}, u32[]{:S(2)}) collective-permute-start(bf16[64,512]{1,0:T(8,128)(2,1)S(1)} %pad_maximum_fusion), channel_id=1, source_target_pairs={{0,192},{32,224},{64,0},{96,32},{128,64},{160,96},{192,128},{224,1... | collective-permute-start | bytes 196616 | tf_op jit(solution)/shard_map/ppermute | solution.py:190
  34.9 3.2 %count.1 = (bf16[768,256]{1,0:T(8,128)(2,1)S(1)}, bf16[256,768]{1,0:T(8,128)(2,1)S(1)}, f32[256,1]{1,0:T(8,128)S(1)}, f32[256,512]{1,0:T(8,128)S(1)}, f32[256,512]{1,0:T(8,128)S(1)}) custom-call(s32[256,32]{1,0:T(8,128)S(1)} %copy.18.nb_ref, bf16[256,512]{1,0:T(8,128)(2,1)S(1)} %copy-done, bf16[512,512]{1,0:T(8,128)(2,1)S(1)} %copy-done.1), custom_call_target="tpu_custom_call" | custom-call | flops 1048576 | bytes 1048576 | tf_op jit(solution)/shard_map/count/pallas_call | solution.py:26
  38.1 1.4 %forward.1 = (bf16[256,512]{1,0:T(8,128)(2,1)}, bf16[256,512]{1,0:T(8,128)(2,1)S(1)}, bf16[512,512]{1,0:T(8,128)(2,1)S(1)}, f32[512,512]{1,0:T(8,128)S(1)}) custom-call(bf16[256,512]{1,0:T(8,128)(2,1)S(1)} %copy-done, bf16[256,512]{1,0:T(8,128)(2,1)S(1)} %copy-done.3, bf16[512,512]{1,0:T(8,128)(2,1)S(1)} %copy-done.2, ...), custom_call_target="tpu_custom_call" | custom-call | flops 1048576 | bytes 1048576 | tf_op jit(solution)/shard_map/forward/pallas_call | solution.py:26
  39.5 1.2 %collective-permute-start.4 = (bf16[512,512]{1,0:T(8,128)(2,1)S(1)}, bf16[512,512]{1,0:T(8,128)(2,1)S(1)}, u32[]{:S(2)}, u32[]{:S(2)}) collective-permute-start(bf16[512,512]{1,0:T(8,128)(2,1)S(1)} %get-tuple-element.36), channel_id=1, source_target_pairs={{0,32},{32,0},{64,96},{96,64},{128,160},{160,128},{192,224},{224,1... | collective-permute-start | bytes 1572872 | tf_op jit(solution)/shard_map/ppermute | solution.py:186
  40.7 1.5 %collective-permute-done.4 = bf16[512,512]{1,0:T(8,128)(2,1)S(1)} collective-permute-done((bf16[512,512]{1,0:T(8,128)(2,1)S(1)}, bf16[512,512]{1,0:T(8,128)(2,1)S(1)}, u32[]{:S(2)}, u32[]{:S(2)}) %collective-permute-start.4) | collective-permute-done | bytes 524320 | tf_op jit(solution)/shard_map/ppermute | solution.py:186
  42.8 2.6 %collective-permute-start.6 = (bf16[128,512]{1,0:T(8,128)(2,1)S(1)}, bf16[128,512]{1,0:T(8,128)(2,1)S(1)}, u32[]{:S(2)}, u32[]{:S(2)}) collective-permute-start(bf16[128,512]{1,0:T(8,128)(2,1)S(1)} %get-tuple-element.39), channel_id=1, source_target_pairs={{0,128},{32,160},{64,192},{96,224},{128,0},{160,32},{192,64},{224,... | collective-permute-start | bytes 393224 | tf_op jit(solution)/shard_map/ppermute | solution.py:190
  46.4 2.0 %collective-permute-done.5.r1_ref = bf16[128,512]{1,0:T(8,128)(2,1)S(1)} collective-permute-done((bf16[128,512]{1,0:T(8,128)(2,1)S(1)}, bf16[128,512]{1,0:T(8,128)(2,1)S(1)}, u32[]{:S(2)}, u32[]{:S(2)}) %collective-permute-start.5) | collective-permute-done | bytes 131104 | tf_op jit(solution)/shard_map/ppermute | solution.py:190
  48.4 3.1 %collective-permute-done.6.r2_ref = bf16[128,512]{1,0:T(8,128)(2,1)S(1)} collective-permute-done((bf16[128,512]{1,0:T(8,128)(2,1)S(1)}, bf16[128,512]{1,0:T(8,128)(2,1)S(1)}, u32[]{:S(2)}, u32[]{:S(2)}) %collective-permute-start.6) | collective-permute-done | bytes 131104 | tf_op jit(solution)/shard_map/ppermute | solution.py:190
  52.5 4.1 %all-to-all-start.1 = ((bf16[32,8,512]{2,1,0:T(8,128)(2,1)}), bf16[32,8,512]{2,1,0:T(8,128)(2,1)S(1)}, u32[]{:S(2)}, u32[]{:S(2)}) async-start(bf16[32,8,512]{2,1,0:T(8,128)(2,1)} %pack.1), calls=%async_computation.1 | async-start | bytes 524288 | tf_op jit(solution)/shard_map/all_to_all | solution.py:194
  56.6 2.0 %collective-permute-start.8 = (bf16[4,32,512]{2,1,0:T(8,128)(2,1)S(1)}, bf16[4,32,512]{2,1,0:T(8,128)(2,1)S(1)}, u32[]{:S(2)}, u32[]{:S(2)}) collective-permute-start(bf16[4,32,512]{2,1,0:T(8,128)(2,1)S(1)} %get-tuple-element.43), channel_id=1, source_target_pairs={{0,32},{32,0},{64,96},{96,64},{128,160},{160,128},{192,224},{224,1... | collective-permute-start | bytes 393224 | tf_op jit(solution)/shard_map/ppermute | solution.py:186
  59.6 1.1 %collective-permute-start.10 = (bf16[32,512]{1,0:T(8,128)(2,1)S(1)}, bf16[32,512]{1,0:T(8,128)(2,1)S(1)}, u32[]{:S(2)}, u32[]{:S(2)}) collective-permute-start(bf16[32,512]{1,0:T(8,128)(2,1)S(1)} %get-tuple-element.46), channel_id=1, source_target_pairs={{0,128},{32,160},{64,192},{96,224},{128,0},{160,32},{192,64},{224,... | collective-permute-start | bytes 98312 | tf_op jit(solution)/shard_map/ppermute | solution.py:190
  60.7 1.9 %collective-permute-start.11 = (bf16[32,512]{1,0:T(8,128)(2,1)S(1)}, bf16[32,512]{1,0:T(8,128)(2,1)S(1)}, u32[]{:S(2)}, u32[]{:S(2)}) collective-permute-start(bf16[32,512]{1,0:T(8,128)(2,1)S(1)} %get-tuple-element.47), channel_id=1, source_target_pairs={{0,64},{32,96},{64,128},{96,160},{128,192},{160,224},{192,0},{224,... | collective-permute-start | bytes 98312 | tf_op jit(solution)/shard_map/ppermute | solution.py:190
  64.3 1.1 %collective-permute-done.11.r3_ref = bf16[32,512]{1,0:T(8,128)(2,1)S(1)} collective-permute-done((bf16[32,512]{1,0:T(8,128)(2,1)S(1)}, bf16[32,512]{1,0:T(8,128)(2,1)S(1)}, u32[]{:S(2)}, u32[]{:S(2)}) %collective-permute-start.11) | collective-permute-done | bytes 32800 | tf_op jit(solution)/shard_map/ppermute | solution.py:190
  66.5 18.4 %all_to_all.16.third_ref.got_ref = bf16[32,8,512]{2,1,0:T(8,128)(2,1)S(1)} all-to-all(bf16[32,8,512]{2,1,0:T(8,128)(2,1)S(1)} %pack2.1), channel_id=1, replica_groups=mesh['dom'=8,'shard'=32] {'shard'}, dimensions={0} | all-to-all | bytes 524288 | tf_op jit(solution)/shard_map/all_to_all | solution.py:194
  85.2 3.0 %collective-permute-start.13 = (bf16[128,512]{1,0:T(8,128)(2,1)S(1)}, bf16[128,512]{1,0:T(8,128)(2,1)S(1)}, u32[]{:S(2)}, u32[]{:S(2)}) collective-permute-start(bf16[128,512]{1,0:T(8,128)(2,1)S(1)} %unpack.1.a0), channel_id=1, source_target_pairs={{0,128},{32,160},{64,192},{96,224},{128,0},{160,32},{192,64},{224,... | collective-permute-start | bytes 393224 | tf_op jit(solution)/shard_map/ppermute | solution.py:190
  88.3 4.5 %collective-permute-start.15 = (bf16[128,512]{1,0:T(8,128)(2,1)S(1)}, bf16[128,512]{1,0:T(8,128)(2,1)S(1)}, u32[]{:S(2)}, u32[]{:S(2)}) collective-permute-start(bf16[128,512]{1,0:T(8,128)(2,1)S(1)} %unpack.1.a0), channel_id=1, source_target_pairs={{0,32},{32,0},{64,96},{96,64},{128,160},{160,128},{192,224},{224,1... | collective-permute-start | bytes 393224 | tf_op jit(solution)/shard_map/ppermute | solution.py:186
  92.8 2.2 %collective-permute-start.16 = (bf16[128,512]{1,0:T(8,128)(2,1)S(1)}, bf16[128,512]{1,0:T(8,128)(2,1)S(1)}, u32[]{:S(2)}, u32[]{:S(2)}) collective-permute-start(bf16[128,512]{1,0:T(8,128)(2,1)S(1)} %collective-permute-done.12.a1), channel_id=1, source_target_pairs={{0,32},{32,0},{64,96},{96,64},{128,160},{160,128},{192,224},{224,1... | collective-permute-start | bytes 393224 | tf_op jit(solution)/shard_map/ppermute | solution.py:186
  95.0 1.9 %collective-permute-start.17 = (bf16[128,512]{1,0:T(8,128)(2,1)S(1)}, bf16[128,512]{1,0:T(8,128)(2,1)S(1)}, u32[]{:S(2)}, u32[]{:S(2)}) collective-permute-start(bf16[128,512]{1,0:T(8,128)(2,1)S(1)} %collective-permute-done.13.a2), channel_id=1, source_target_pairs={{0,32},{32,0},{64,96},{96,64},{128,160},{160,128},{192,224},{224,1... | collective-permute-start | bytes 393224 | tf_op jit(solution)/shard_map/ppermute | solution.py:186
  98.7 1.5 %weights.1 = (f32[4,128,512]{2,1,0:T(8,128)}, f32[4,128,512]{2,1,0:T(8,128)}) custom-call(bf16[128,512]{1,0:T(8,128)(2,1)S(1)} %unpack.1.a0, bf16[128,512]{1,0:T(8,128)(2,1)S(1)} %collective-permute-done.12.a1, bf16[128,512]{1,0:T(8,128)(2,1)S(1)} %collective-permute-done.13.a2, bf16[128,512]{1,0:T(8,128)(2,1)S(1)} %collective-permute-done.14.a3, ...), custom_call_target="tpu_custom_call" | custom-call | flops 1048576 | bytes 1048576 | tf_op jit(solution)/shard_map/weights/pallas_call | solution.py:26
  (52 shorter events, 10.3 us)
Async XLA Ops:
  3.4 31.4 %copy-start.1 = (bf16[512,512]{1,0:T(8,128)(2,1)S(1)}, bf16[512,512]{1,0:T(8,128)(2,1)}, u32[]{:S(2)}) copy-start(bf16[512,512]{1,0:T(8,128)(2,1)} %ws_ref.3) | copy-start | bytes 1572868
  24.9 9.9 %copy-start = (bf16[256,512]{1,0:T(8,128)(2,1)S(1)}, bf16[256,512]{1,0:T(8,128)(2,1)}, u32[]{:S(2)}) copy-start(bf16[256,512]{1,0:T(8,128)(2,1)} %feat_ref.3) | copy-start | bytes 786436
  25.0 9.7 %copy-start.4 = (s32[256,32]{0,1:T(8,128)S(1)}, s32[256,32]{0,1:T(8,128)}, u32[]{:S(2)}) copy-start(s32[256,32]{0,1:T(8,128)} %param.12) | copy-start | bytes 98308
  25.0 4.7 %collective-permute-start = (bf16[32,512]{1,0:T(8,128)(2,1)S(1)}, bf16[32,512]{1,0:T(8,128)(2,1)S(1)}, u32[]{:S(2)}, u32[]{:S(2)}) collective-permute-start(bf16[32,512]{1,0:T(8,128)(2,1)S(1)} %bitcast.16), channel_id=1, source_target_pairs={{0,32},{32,0},{64,96},{96,64},{128,160},{160,128},{192,224},{224,1... | collective-permute-start | bytes 98312 | tf_op jit(solution)/shard_map/ppermute | solution.py:186
  29.7 8.4 %copy-start.2 = (bf16[512,512]{1,0:T(8,128)(2,1)S(1)}, bf16[512,512]{1,0:T(8,128)(2,1)}, u32[]{:S(2)}) copy-start(bf16[512,512]{1,0:T(8,128)(2,1)} %wn_ref.3) | copy-start | bytes 1572868
  29.7 8.3 %collective-permute-start.1 = (bf16[64,512]{1,0:T(8,128)(2,1)S(1)}, bf16[64,512]{1,0:T(8,128)(2,1)S(1)}, u32[]{:S(2)}, u32[]{:S(2)}) collective-permute-start(bf16[64,512]{1,0:T(8,128)(2,1)S(1)} %pad_maximum_fusion), channel_id=1, source_target_pairs={{0,64},{32,96},{64,128},{96,160},{128,192},{160,224},{192,0},{224,... | collective-permute-start | bytes 196616 | tf_op jit(solution)/shard_map/ppermute | solution.py:190
  31.1 7.0 %collective-permute-start.2 = (bf16[64,512]{1,0:T(8,128)(2,1)S(1)}, bf16[64,512]{1,0:T(8,128)(2,1)S(1)}, u32[]{:S(2)}, u32[]{:S(2)}) collective-permute-start(bf16[64,512]{1,0:T(8,128)(2,1)S(1)} %pad_maximum_fusion), channel_id=1, source_target_pairs={{0,128},{32,160},{64,192},{96,224},{128,0},{160,32},{192,64},{224,... | collective-permute-start | bytes 196616 | tf_op jit(solution)/shard_map/ppermute | solution.py:190
  33.7 4.4 %collective-permute-start.3 = (bf16[64,512]{1,0:T(8,128)(2,1)S(1)}, bf16[64,512]{1,0:T(8,128)(2,1)S(1)}, u32[]{:S(2)}, u32[]{:S(2)}) collective-permute-start(bf16[64,512]{1,0:T(8,128)(2,1)S(1)} %pad_maximum_fusion), channel_id=1, source_target_pairs={{0,192},{32,224},{64,0},{96,32},{128,64},{160,96},{192,128},{224,1... | collective-permute-start | bytes 196616 | tf_op jit(solution)/shard_map/ppermute | solution.py:190
  39.5 2.8 %collective-permute-start.4 = (bf16[512,512]{1,0:T(8,128)(2,1)S(1)}, bf16[512,512]{1,0:T(8,128)(2,1)S(1)}, u32[]{:S(2)}, u32[]{:S(2)}) collective-permute-start(bf16[512,512]{1,0:T(8,128)(2,1)S(1)} %get-tuple-element.36), channel_id=1, source_target_pairs={{0,32},{32,0},{64,96},{96,64},{128,160},{160,128},{192,224},{224,1... | collective-permute-start | bytes 1572872 | tf_op jit(solution)/shard_map/ppermute | solution.py:186
  42.4 6.0 %collective-permute-start.5 = (bf16[128,512]{1,0:T(8,128)(2,1)S(1)}, bf16[128,512]{1,0:T(8,128)(2,1)S(1)}, u32[]{:S(2)}, u32[]{:S(2)}) collective-permute-start(bf16[128,512]{1,0:T(8,128)(2,1)S(1)} %get-tuple-element.38), channel_id=1, source_target_pairs={{0,64},{32,96},{64,128},{96,160},{128,192},{160,224},{192,0},{224,... | collective-permute-start | bytes 393224 | tf_op jit(solution)/shard_map/ppermute | solution.py:190
  42.8 8.7 %collective-permute-start.6 = (bf16[128,512]{1,0:T(8,128)(2,1)S(1)}, bf16[128,512]{1,0:T(8,128)(2,1)S(1)}, u32[]{:S(2)}, u32[]{:S(2)}) collective-permute-start(bf16[128,512]{1,0:T(8,128)(2,1)S(1)} %get-tuple-element.39), channel_id=1, source_target_pairs={{0,128},{32,160},{64,192},{96,224},{128,0},{160,32},{192,64},{224,... | collective-permute-start | bytes 393224 | tf_op jit(solution)/shard_map/ppermute | solution.py:190
  45.5 6.1 %collective-permute-start.7 = (bf16[128,512]{1,0:T(8,128)(2,1)S(1)}, bf16[128,512]{1,0:T(8,128)(2,1)S(1)}, u32[]{:S(2)}, u32[]{:S(2)}) collective-permute-start(bf16[128,512]{1,0:T(8,128)(2,1)S(1)} %get-tuple-element.40), channel_id=1, source_target_pairs={{0,192},{32,224},{64,0},{96,32},{128,64},{160,96},{192,128},{224,1... | collective-permute-start | bytes 393224 | tf_op jit(solution)/shard_map/ppermute | solution.py:190
  52.5 13.8 %all-to-all-start.1 = ((bf16[32,8,512]{2,1,0:T(8,128)(2,1)}), bf16[32,8,512]{2,1,0:T(8,128)(2,1)S(1)}, u32[]{:S(2)}, u32[]{:S(2)}) async-start(bf16[32,8,512]{2,1,0:T(8,128)(2,1)} %pack.1), calls=%async_computation.1 | async-start | bytes 524288 | tf_op jit(solution)/shard_map/all_to_all | solution.py:194
  56.6 3.0 %collective-permute-start.8 = (bf16[4,32,512]{2,1,0:T(8,128)(2,1)S(1)}, bf16[4,32,512]{2,1,0:T(8,128)(2,1)S(1)}, u32[]{:S(2)}, u32[]{:S(2)}) collective-permute-start(bf16[4,32,512]{2,1,0:T(8,128)(2,1)S(1)} %get-tuple-element.43), channel_id=1, source_target_pairs={{0,32},{32,0},{64,96},{96,64},{128,160},{160,128},{192,224},{224,1... | collective-permute-start | bytes 393224 | tf_op jit(solution)/shard_map/ppermute | solution.py:186
  59.6 4.7 %collective-permute-start.10 = (bf16[32,512]{1,0:T(8,128)(2,1)S(1)}, bf16[32,512]{1,0:T(8,128)(2,1)S(1)}, u32[]{:S(2)}, u32[]{:S(2)}) collective-permute-start(bf16[32,512]{1,0:T(8,128)(2,1)S(1)} %get-tuple-element.46), channel_id=1, source_target_pairs={{0,128},{32,160},{64,192},{96,224},{128,0},{160,32},{192,64},{224,... | collective-permute-start | bytes 98312 | tf_op jit(solution)/shard_map/ppermute | solution.py:190
  60.7 4.6 %collective-permute-start.11 = (bf16[32,512]{1,0:T(8,128)(2,1)S(1)}, bf16[32,512]{1,0:T(8,128)(2,1)S(1)}, u32[]{:S(2)}, u32[]{:S(2)}) collective-permute-start(bf16[32,512]{1,0:T(8,128)(2,1)S(1)} %get-tuple-element.47), channel_id=1, source_target_pairs={{0,64},{32,96},{64,128},{96,160},{128,192},{160,224},{192,0},{224,... | collective-permute-start | bytes 98312 | tf_op jit(solution)/shard_map/ppermute | solution.py:190
  62.7 3.1 %collective-permute-start.9 = (bf16[32,512]{1,0:T(8,128)(2,1)S(1)}, bf16[32,512]{1,0:T(8,128)(2,1)S(1)}, u32[]{:S(2)}, u32[]{:S(2)}) collective-permute-start(bf16[32,512]{1,0:T(8,128)(2,1)S(1)} %get-tuple-element.45), channel_id=1, source_target_pairs={{0,192},{32,224},{64,0},{96,32},{128,64},{160,96},{192,128},{224,1... | collective-permute-start | bytes 98312 | tf_op jit(solution)/shard_map/ppermute | solution.py:190
  85.1 7.7 %collective-permute-start.12 = (bf16[128,512]{1,0:T(8,128)(2,1)S(1)}, bf16[128,512]{1,0:T(8,128)(2,1)S(1)}, u32[]{:S(2)}, u32[]{:S(2)}) collective-permute-start(bf16[128,512]{1,0:T(8,128)(2,1)S(1)} %unpack.1.a0), channel_id=1, source_target_pairs={{0,64},{32,96},{64,128},{96,160},{128,192},{160,224},{192,0},{224,... | collective-permute-start | bytes 393224 | tf_op jit(solution)/shard_map/ppermute | solution.py:190
  85.2 9.8 %collective-permute-start.13 = (bf16[128,512]{1,0:T(8,128)(2,1)S(1)}, bf16[128,512]{1,0:T(8,128)(2,1)S(1)}, u32[]{:S(2)}, u32[]{:S(2)}) collective-permute-start(bf16[128,512]{1,0:T(8,128)(2,1)S(1)} %unpack.1.a0), channel_id=1, source_target_pairs={{0,128},{32,160},{64,192},{96,224},{128,0},{160,32},{192,64},{224,... | collective-permute-start | bytes 393224 | tf_op jit(solution)/shard_map/ppermute | solution.py:190
  88.2 8.7 %collective-permute-start.14 = (bf16[128,512]{1,0:T(8,128)(2,1)S(1)}, bf16[128,512]{1,0:T(8,128)(2,1)S(1)}, u32[]{:S(2)}, u32[]{:S(2)}) collective-permute-start(bf16[128,512]{1,0:T(8,128)(2,1)S(1)} %unpack.1.a0), channel_id=1, source_target_pairs={{0,192},{32,224},{64,0},{96,32},{128,64},{160,96},{192,128},{224,1... | collective-permute-start | bytes 393224 | tf_op jit(solution)/shard_map/ppermute | solution.py:190
  88.3 10.4 %collective-permute-start.15 = (bf16[128,512]{1,0:T(8,128)(2,1)S(1)}, bf16[128,512]{1,0:T(8,128)(2,1)S(1)}, u32[]{:S(2)}, u32[]{:S(2)}) collective-permute-start(bf16[128,512]{1,0:T(8,128)(2,1)S(1)} %unpack.1.a0), channel_id=1, source_target_pairs={{0,32},{32,0},{64,96},{96,64},{128,160},{160,128},{192,224},{224,1... | collective-permute-start | bytes 393224 | tf_op jit(solution)/shard_map/ppermute | solution.py:186
  92.8 5.9 %collective-permute-start.16 = (bf16[128,512]{1,0:T(8,128)(2,1)S(1)}, bf16[128,512]{1,0:T(8,128)(2,1)S(1)}, u32[]{:S(2)}, u32[]{:S(2)}) collective-permute-start(bf16[128,512]{1,0:T(8,128)(2,1)S(1)} %collective-permute-done.12.a1), channel_id=1, source_target_pairs={{0,32},{32,0},{64,96},{96,64},{128,160},{160,128},{192,224},{224,1... | collective-permute-start | bytes 393224 | tf_op jit(solution)/shard_map/ppermute | solution.py:186
  95.0 3.6 %collective-permute-start.17 = (bf16[128,512]{1,0:T(8,128)(2,1)S(1)}, bf16[128,512]{1,0:T(8,128)(2,1)S(1)}, u32[]{:S(2)}, u32[]{:S(2)}) collective-permute-start(bf16[128,512]{1,0:T(8,128)(2,1)S(1)} %collective-permute-done.13.a2), channel_id=1, source_target_pairs={{0,32},{32,0},{64,96},{96,64},{128,160},{160,128},{192,224},{224,1... | collective-permute-start | bytes 393224 | tf_op jit(solution)/shard_map/ppermute | solution.py:186
  96.9 1.8 %collective-permute-start.18 = (bf16[128,512]{1,0:T(8,128)(2,1)S(1)}, bf16[128,512]{1,0:T(8,128)(2,1)S(1)}, u32[]{:S(2)}, u32[]{:S(2)}) collective-permute-start(bf16[128,512]{1,0:T(8,128)(2,1)S(1)} %collective-permute-done.14.a3), channel_id=1, source_target_pairs={{0,32},{32,0},{64,96},{96,64},{128,160},{160,128},{192,224},{224,1... | collective-permute-start | bytes 393224 | tf_op jit(solution)/shard_map/ppermute | solution.py:186
  (3 other events, 4.6 us)

commit v2 on v1

v2 whole, which is shorter than its diff:
```python
import functools

import jax
import jax.numpy as jnp
from jax import lax
from jax.experimental import pallas as pl
from jax.experimental.pallas import tpu as pltpu
from jax.sharding import Mesh
from jax.sharding import PartitionSpec as P

BF = jnp.bfloat16
F32 = jnp.float32
I32 = jnp.int32
PACK = 8
HUB_ROW = 4
NY, NX, NZ = 4, 4, 8


def dot(a, b, ca=1, cb=0):
    return lax.dot_general(a, b, (((ca,), (cb,)), ((), ())), preferred_element_type=F32)


def call(kernel, outs, name, flops=1 << 22, nbytes=1 << 20, smem=()):
    outs = [jax.ShapeDtypeStruct(s, d) for s, d in outs]
    spec = pl.BlockSpec(memory_space=pltpu.VMEM)
    scalar = pl.BlockSpec(memory_space=pltpu.SMEM)

    def run(*args):
        return pl.pallas_call(
            kernel,
            out_shape=outs,
            in_specs=[scalar if i in smem else spec for i in range(len(args))],
            out_specs=[spec] * len(outs),
            name=name,
            compiler_params=pltpu.CompilerParams(vmem_limit_bytes=32 << 20),
            cost_estimate=pl.CostEstimate(flops=flops, bytes_accessed=nbytes, transcendentals=0),
        )(*args)

    return run


def place():
    dom = lax.axis_index("dom")
    return dom // 2, dom % 2


def iota(shape, dim):
    return lax.broadcasted_iota(I32, shape, dim)


def outgoing_kernel(slot_ref, feat_ref, route_ref, count_ref, out_ref, sel_ref):
    verts, width = feat_ref.shape
    cap, peers = route_ref.shape
    packed = peers * PACK
    live = iota((cap, peers), 0) < count_ref[...]
    routes = jnp.where(live, route_ref[...], -1).astype(F32).astype(BF)
    owner = (iota((packed, peers), 0) // PACK == iota((packed, peers), 1)).astype(BF)
    every = dot(owner, routes, 1, 1)
    k = lax.rem(iota((packed, cap), 0), PACK)
    index = jnp.sum(jnp.where(k == iota((packed, cap), 1), every, 0.0), axis=1, keepdims=True).astype(I32)
    k = lax.rem(iota((packed, 1), 0), PACK)
    index = jnp.where(k < cap, index, jnp.where(k == HUB_ROW, slot_ref[0], -1))
    sel = (index == iota((packed, verts), 1)).astype(BF)
    sel_ref[...] = sel
    out_ref[...] = dot(sel, feat_ref[...]).astype(BF).reshape(out_ref.shape)


def count_kernel(nbt_ref, feat_ref, ws_ref, sel_ref, ct_ref, c_ref, deg_ref, zs_ref, s1_ref, selt_ref, *, hubs, table):
    slots, verts = nbt_ref.shape
    packed = ct_ref.shape[0] // 2 - verts // 2
    far = verts + 2 * packed
    y, c = place()
    nbt = nbt_ref[...]
    degree = jnp.sum((nbt < table).astype(F32), axis=0, keepdims=True)
    deg_ref[...] = jnp.broadcast_to(degree, (8, verts)).T[:, :1]
    step = 128

    def hub(back, core, row):
        return verts + (lax.rem(y - back + NY, NY) * 2 + core) * NX * NZ + row

    for t in range(0, far + 256, step):
        r = iota((step, verts), 0)
        if t < verts:
            want = r + t
        elif t < far:
            mine = t < verts + packed
            b = r + (t - verts if mine else t - verts - packed)
            p, k = b // PACK, lax.rem(b, PACK)
            bound = verts + hubs + p * 4 + k if mine else -1
            want = jnp.where(k < 4, bound, hub(k - 4, c if mine else 1 - c, p))
        else:
            b = r + (t - far)
            i = b - 32
            p = lax.rem(i, 32)
            core = jnp.where(lax.rem(i // 32, 2) == 0, c, 1 - c)
            want = jnp.where(b < 32, hub(0, 1 - c, b), hub(i // 64 + 1, core, p))
            want = jnp.where(b < 224, want, -1)
        acc = jnp.zeros((step, verts), F32)
        for j in range(slots):
            acc = acc + jnp.where(nbt[j : j + 1, :] == want, 1.0, 0.0)
        if t < far:
            ct_ref[t : t + step, :] = acc.astype(BF)
        if t < verts + packed:
            c_ref[:, t : t + step] = acc.T.astype(BF)
        elif t >= far:
            t0 = t - packed
            c_ref[:, t0 : t0 + step] = acc.T.astype(BF)
    feat = feat_ref[...]
    zs_ref[...] = dot(feat, ws_ref[...])
    s1_ref[...] = dot(c_ref[:, :verts], feat)
    selt_ref[...] = sel_ref[...].astype(F32).T.astype(BF)


def forward_kernel(
    feat_ref, cot_ref, wn_ref, c_ref, deg_ref, zs_ref, s1_ref, bnd_ref, hp_ref, h1_ref, h2_ref, h3_ref,
    hid_ref, dz_ref, send_ref, keep_ref,
):
    verts, width = feat_ref.shape
    _, c = place()
    packed = bnd_ref.shape[0] * PACK
    bnd = bnd_ref[...].reshape(packed, width)
    pad = jnp.zeros((32, width), BF)
    hubs = jnp.concatenate([hp_ref[...], h1_ref[...], h2_ref[...], h3_ref[...], pad], axis=0)
    sums = s1_ref[...] + dot(c_ref[:, verts : verts + packed], bnd) + dot(c_ref[:, verts + packed :], hubs)
    agg = (sums / deg_ref[...]).astype(BF)
    z = zs_ref[...] + dot(agg, wn_ref[...])
    sig = jax.nn.sigmoid(z)
    hid_ref[...] = (z * sig).astype(BF)
    dz = (cot_ref[...].astype(F32) * sig * (1.0 + z * (1.0 - sig))).astype(BF)
    dz_ref[...] = dz
    feat = feat_ref[...]
    first = c == 0
    send_ref[...] = dot(jnp.where(first, agg, feat), dz, 0, 0).astype(BF)
    keep_ref[...] = dot(jnp.where(first, feat, agg), dz, 0, 0)


def backward_kernel(dz_ref, wn_ref, ws_ref, deg_ref, ct_ref, base_ref, mine_ref, other_ref):
    verts, width = dz_ref.shape
    packed = mine_ref.shape[0]
    dz = dz_ref[...]
    edge = (dot(dz, wn_ref[...], 1, 1) / deg_ref[...]).astype(BF)
    other_ref[...] = dot(ct_ref[verts + packed :, :], edge).astype(BF)
    mine_ref[...] = dot(ct_ref[verts : verts + packed, :], edge)
    base_ref[...] = dot(dz, ws_ref[...], 1, 1) + dot(ct_ref[:verts, :], edge)


def pair_kernel(mine_ref, got_ref, out_ref):
    out_ref[...] = (mine_ref[...] + got_ref[...].astype(F32)).astype(BF).reshape(out_ref.shape)


def half_kernel(keep_ref, got_ref, own_ref, s1_ref, s2_ref, s3_ref):
    y, _ = place()
    own_ref[...] = keep_ref[y] + got_ref[y].astype(F32)
    for k, ref in ((1, s1_ref), (2, s2_ref), (3, s3_ref)):
        j = lax.rem(y + k, NY)
        ref[...] = (keep_ref[j] + got_ref[j].astype(F32)).astype(BF)


def quarter_kernel(own_ref, r1_ref, r2_ref, r3_ref, out_ref, s1_ref, s2_ref, s3_ref):
    x = lax.axis_index("x")

    def chunk(j):
        return own_ref[j] + r1_ref[j].astype(F32) + r2_ref[j].astype(F32) + r3_ref[j].astype(F32)

    out_ref[...] = chunk(x)
    for k, ref in ((1, s1_ref), (2, s2_ref), (3, s3_ref)):
        ref[...] = chunk(lax.rem(x + k, NX)).astype(BF)


def column_kernel(own_ref, r1_ref, r2_ref, r3_ref, out_ref):
    total = own_ref[...] + r1_ref[...].astype(F32) + r2_ref[...].astype(F32) + r3_ref[...].astype(F32)
    out_ref[...] = jnp.broadcast_to(total.astype(BF)[None], out_ref.shape)


def total_kernel(got_ref, out_ref):
    out_ref[...] = jnp.sum(got_ref[...].astype(F32), axis=0).astype(BF)


def join_kernel(a0, a1, a2, a3, out_ref):
    x = lax.axis_index("x")
    for k, a in enumerate((a0, a1, a2, a3)):
        out_ref[lax.rem(x - k + NX, NX)] = a[...]


def hub_kernel(got_ref, out_ref):
    out_ref[...] = jnp.sum(got_ref[...].astype(F32), axis=0).astype(BF)


def grad_kernel(slot_ref, base_ref, selt_ref, got_ref, r1_ref, r2_ref, r3_ref, out_ref):
    verts, width = base_ref.shape
    got = got_ref[...].reshape(-1, width)
    far = sum(r[...].astype(F32)[HUB_ROW + k : HUB_ROW + k + 1] for k, r in ((1, r1_ref), (2, r2_ref), (3, r3_ref)))
    at = iota((verts, width), 0) == slot_ref[0]
    out_ref[...] = base_ref[...] + dot(selt_ref[...], got) + jnp.where(at, far, 0.0)


def weight_kernel(a0, a1, a2, a3, b0, b1, b2, b3, self_ref, neigh_ref):
    y, c = place()
    first = c == 0
    for k, (a, b) in enumerate(((a0, b0), (a1, b1), (a2, b2), (a3, b3))):
        j = lax.rem(y - k + NY, NY)
        mine, other = a[...].astype(F32), b[...].astype(F32)
        self_ref[j] = jnp.where(first, mine, other)
        neigh_ref[j] = jnp.where(first, other, mine)


def swap_core(v):
    return lax.ppermute(v, "dom", [(i, i ^ 1) for i in range(2 * NY)])


def shift_y(v, k):
    return lax.ppermute(v, "dom", [(i, ((i // 2 + k) % NY) * 2 + i % 2) for i in range(2 * NY)])


def shift_x(v, k):
    return lax.ppermute(v, "x", [(i, (i + k) % NX) for i in range(NX)])


def exchange(v, axis):
    return lax.all_to_all(v, axis, split_axis=0, concat_axis=0, tiled=True)


def body(features, w_self, w_neigh, cotangent, neighbours, hub_slots, send_rows, send_counts):
    verts, width = features.shape
    peers, cap = send_rows.shape[1:]
    hubs = 2 * NY * NX * NZ
    packed = peers * PACK
    table = verts + hubs + peers * cap

    outgoing, sel = call(
        outgoing_kernel, [((peers, PACK, width), BF), ((packed, verts), BF)], "outgoing", smem=(0,)
    )(hub_slots, features, send_rows[0].T, send_counts)
    first = exchange(outgoing, ("x", "z"))

    ct, cm, degree, z_self, s_local, selt = call(
        functools.partial(count_kernel, hubs=hubs, table=table),
        [
            ((verts + 2 * packed, verts), BF),
            ((verts, verts + packed + 256), BF),
            ((verts, 1), F32),
            ((verts, width), F32),
            ((verts, width), F32),
            ((verts, packed), BF),
        ],
        "count",
        flops=1 << 28,
        nbytes=1 << 23,
    )(neighbours.T, features, w_self, sel)

    first, ct, cm = lax.optimization_barrier((first, ct, cm))
    hub_own = first[:, HUB_ROW]
    hub_other = swap_core(hub_own)
    hub_pair = jnp.concatenate([hub_own, hub_other], axis=0)
    hub_far = [shift_y(hub_pair, k) for k in (1, 2, 3)]

    hidden, dz, w_send, w_keep = call(
        forward_kernel,
        [((verts, width), BF), ((verts, width), BF), ((width, width), BF), ((width, width), F32)],
        "forward",
    )(features, cotangent, w_neigh, cm, degree, z_self, s_local, first, hub_other, *hub_far)

    w_got = swap_core(w_send)
    base, mine, other = call(
        backward_kernel,
        [((verts, width), F32), ((packed, width), F32), ((packed, width), BF)],
        "backward",
    )(dz, w_neigh, w_self, degree, ct)
    other_got = swap_core(other)

    chunk = width // NY
    part = chunk // NX
    w_own, *w_out = call(half_kernel, [((chunk, width), F32)] + [((chunk, width), BF)] * 3, "half")(
        w_keep.reshape(NY, chunk, width), w_got.reshape(NY, chunk, width)
    )
    w_in = [shift_y(w_out[k - 1], k) for k in (1, 2, 3)]

    back = call(pair_kernel, [((peers, PACK, width), BF)], "pair")(mine, other_got)[0]
    second = exchange(back, ("x", "z"))

    split = (NX, part, width)
    w_own, *w_out = call(quarter_kernel, [((part, width), F32)] + [((part, width), BF)] * 3, "quarter")(
        w_own.reshape(split), *[w.reshape(split) for w in w_in]
    )
    w_in = [shift_x(w_out[k - 1], k) for k in (1, 2, 3)]
    w_col = call(column_kernel, [((NZ, part, width), BF)], "column")(w_own, *w_in)[0]
    w_sum = call(total_kernel, [((part, width), BF)], "total")(exchange(w_col, "z"))[0]

    hub_sum = call(hub_kernel, [((PACK, width), BF)], "hub")(second)[0]
    hub_in = [shift_y(hub_sum, -k) for k in (1, 2, 3)]
    grad_features = call(grad_kernel, [((verts, width), F32)], "grad", smem=(0,))(
        hub_slots, base, selt, second, *hub_in
    )[0]

    w_x = [w_sum] + [shift_x(w_sum, k) for k in (1, 2, 3)]
    w_part = call(join_kernel, [((NX, part, width), BF)], "join")(*w_x)[0].reshape(chunk, width)
    mine = [w_part] + [shift_y(w_part, k) for k in (1, 2, 3)]
    other = [swap_core(v) for v in mine]
    grad_self, grad_neigh = call(weight_kernel, [((NY, chunk, width), F32)] * 2, "weights")(*mine, *other)
    return (hidden, grad_features, grad_self.reshape(width, width), grad_neigh.reshape(width, width))


def solution(mesh):
    fine = Mesh(mesh.devices.reshape(2 * NY, NX, NZ), ("dom", "x", "z"))
    every = ("dom", "x", "z")
    vertex = P(every, None)
    return jax.shard_map(
        body,
        mesh=fine,
        in_specs=(vertex, P(), P(), vertex, vertex, P(every), P(every, None, None), vertex),
        out_specs=(vertex, vertex, P(), P()),
        check_vma=False,
    )
```

time: 101 us -> 115 us (1.14)
  blocking collectives: 39.9 us -> 0 us
  waiting for transfers between devices: 11.4 us -> 39.1 us
  starting transfers between devices: 35.5 us -> 57.5 us
  local copies, waits for them, and re-layouts: 1.04 us -> 4.06 us
  Pallas kernels: 9.45 us -> 11.3 us
  matrix products: 1.22 us -> 0 us
    all_to_all x2 -> x0, blocking collectives: 39.9 us -> none  [exchange(): return lax.all_to_all(x, 'shard', split_axis=0, concat_axis=0, tiled=True)]
    ppermute x19 -> x25, waiting for transfers between devices: 10.9 us -> 31.2 us  [the longest x12 21.8 us: shift_y(): lax.ppermute(v, 'dom', [(i, (i // 2 + k) % NY * 2 + i % 2) for i in range...]
    all_to_all x1 -> x3, starting transfers between devices: 4.12 us -> 21.5 us  [exchange(): return lax.all_to_all(v, axis, split_axis=0, concat_axis=0, tiled=True)]
    all_to_all x1 -> x3, waiting for transfers between devices: 0.54 us -> 7.92 us  [exchange(): return lax.all_to_all(v, axis, split_axis=0, concat_axis=0, tiled=True)]
    ppermute x19 -> x25, starting transfers between devices: 31.4 us -> 36 us  [the longest x7 19.3 us: swap_core(): return lax.ppermute(v, 'dom', [(i, i ^ 1) for i in range(2 * NY)])]
    unnamed x16 -> x24, local copies, waits for them, and re-layouts: 0.8 us -> 3.97 us
    pallas_call x10 -> x13, Pallas kernels: 9.45 us -> 11.3 us  [run(): pl.pallas_call(kernel, out_shape=outs, in_specs=[scalar if i in smem else...]
    dot_general x1 -> x0, matrix products: 1.22 us -> none  [dot(): lax.dot_general(a, b, (((ca,), (cb,)), ((), ())), preferred_element_type=...]
  transfers between devices with their start and end apart: 20 -> 28, of which waited for: 9 -> 18; matrix products, arithmetic and copies ran while one was open for 0% -> 0% of each run, Pallas kernels for 5% -> 6%
where the time goes in v2:
time: 115 us; the launch traced here: 113 us
  starting transfers between devices  57.5 us (50%)
  waiting for transfers between devices  39.1 us (34%)
  Pallas kernels  11.3 us (10%)
  local copies, waits for them, and re-layouts  4.06 us (4%)
  between operations  1.5 us (1%)
    ppermute x12, waiting for transfers between devices, shift_y(): lax.ppermute(v, 'dom', [(i, (i // 2 + k) % NY * 2 + i % 2) for i in range...  21.8 us
    all_to_all x3, starting transfers between devices, exchange(): return lax.all_to_all(v, axis, split_axis=0, concat_axis=0, tiled=True)  21.5 us
    ppermute x7, starting transfers between devices, swap_core(): return lax.ppermute(v, 'dom', [(i, i ^ 1) for i in range(2 * NY)])  19.3 us
    pallas_call x13, Pallas kernels, run(): pl.pallas_call(kernel, out_shape=outs, in_specs=[scalar if i in smem else...  11.3 us
    ppermute x12, starting transfers between devices, shift_y(): lax.ppermute(v, 'dom', [(i, (i // 2 + k) % NY * 2 + i % 2) for i in range...  9.74 us
    all_to_all x3, waiting for transfers between devices, exchange(): return lax.all_to_all(v, axis, split_axis=0, concat_axis=0, tiled=True)  7.92 us
    ppermute x6, starting transfers between devices, shift_x(): return lax.ppermute(v, 'x', [(i, (i + k) % NX) for i in range(NX)])  7 us
    ppermute x6, waiting for transfers between devices, shift_x(): return lax.ppermute(v, 'x', [(i, (i + k) % NX) for i in range(NX)])  5.76 us
  transfers between devices with their start and end apart: 28, of which 18 were waited for; matrix products, arithmetic and copies ran while one was open for 0% of the time, Pallas kernels for 6%

profile of v2, /device:TPU:1, one launch (start us, length us, event | category | flops | bytes accessed | tf_op | source)
XLA Modules:
  0.0 113.5 jit_solution(8747418528380061032)
XLA Ops:
  4.0 12.0 %all-to-all-start = ((bf16[32,8,512]{2,1,0:T(8,128)(2,1)}), bf16[32,8,512]{2,1,0:T(8,128)(2,1)S(1)}, u32[]{:S(2)}, u32[]{:S(2)}) async-start(bf16[32,8,512]{2,1,0:T(8,128)(2,1)} %get-tuple-element.32), calls=%async_computation | async-start | bytes 524288 | tf_op jit(solution)/shard_map/all_to_all | solution.py:220
  16.8 3.8 %count.1 = (bf16[768,256]{1,0:T(8,128)(2,1)S(1)}, bf16[256,768]{1,0:T(8,128)(2,1)S(1)}, f32[256,1]{1,0:T(8,128)S(1)}, f32[256,512]{1,0:T(8,128)S(1)}, f32[256,51...) custom-call(s32[32,256]{1,0:T(8,128)S(1)} %bitcast.27, bf16[256,512]{1,0:T(8,128)(2,1)S(1)} %copy-done.2, ...), custom_call_target="tpu_custom_call" | custom-call | flops 268435456 | bytes 8388608 | tf_op jit(solution)/shard_map/count/pallas_call | solution.py:29
  21.2 4.5 %all-to-all-done.bnd_ref = bf16[32,8,512]{2,1,0:T(8,128)(2,1)S(1)} async-done(((bf16[32,8,512]{2,1,0:T(8,128)(2,1)}), bf16[32,8,512]{2,1,0:T(8,128)(2,1)S(1)}, u32[]{:S(2)}, u32[]{:S(2)}) %all-to-all-start) | async-done | bytes 262176 | tf_op jit(solution)/shard_map/all_to_all | solution.py:220
  25.8 3.8 %collective-permute-start = (bf16[32,512]{1,0:T(8,128)(2,1)S(1)}, bf16[32,512]{1,0:T(8,128)(2,1)S(1)}, u32[]{:S(2)}, u32[]{:S(2)}) collective-permute-start(bf16[32,512]{1,0:T(8,128)(2,1)S(1)} %slice_bitcast_fusion), channel_id=1, source_target_pairs={{0,32},{32,0},{64,96},{96,64},{128,160},{160,128},{192,224},{224,1... | collective-permute-start | bytes 98312 | tf_op jit(solution)/shard_map/ppermute | solution.py:208
  30.5 2.7 %collective-permute-start.3 = (bf16[64,512]{1,0:T(8,128)(2,1)S(1)}, bf16[64,512]{1,0:T(8,128)(2,1)S(1)}, u32[]{:S(2)}, u32[]{:S(2)}) collective-permute-start(bf16[64,512]{1,0:T(8,128)(2,1)S(1)} %pad_maximum_fusion), channel_id=1, source_target_pairs={{0,192},{32,224},{64,0},{96,32},{128,64},{160,96},{192,128},{224,1... | collective-permute-start | bytes 196616 | tf_op jit(solution)/shard_map/ppermute | solution.py:212
  34.6 3.4 %collective-permute-done.2.h2_ref = bf16[64,512]{1,0:T(8,128)(2,1)S(1)} collective-permute-done((bf16[64,512]{1,0:T(8,128)(2,1)S(1)}, bf16[64,512]{1,0:T(8,128)(2,1)S(1)}, u32[]{:S(2)}, u32[]{:S(2)}) %collective-permute-start.2) | collective-permute-done | bytes 65568 | tf_op jit(solution)/shard_map/ppermute | solution.py:212
  37.9 1.7 %collective-permute-done.1.h1_ref = bf16[64,512]{1,0:T(8,128)(2,1)S(1)} collective-permute-done((bf16[64,512]{1,0:T(8,128)(2,1)S(1)}, bf16[64,512]{1,0:T(8,128)(2,1)S(1)}, u32[]{:S(2)}, u32[]{:S(2)}) %collective-permute-start.1) | collective-permute-done | bytes 65568 | tf_op jit(solution)/shard_map/ppermute | solution.py:212
  43.0 1.5 %collective-permute-done.8 = bf16[512,512]{1,0:T(8,128)(2,1)S(1)} collective-permute-done((bf16[512,512]{1,0:T(8,128)(2,1)S(1)}, bf16[512,512]{1,0:T(8,128)(2,1)S(1)}, u32[]{:S(2)}, u32[]{:S(2)}) %collective-permute-start.8) | collective-permute-done | bytes 524320 | tf_op jit(solution)/shard_map/ppermute | solution.py:208
  47.5 5.9 %collective-permute-done.9 = bf16[128,512]{1,0:T(8,128)(2,1)S(1)} collective-permute-done((bf16[128,512]{1,0:T(8,128)(2,1)S(1)}, bf16[128,512]{1,0:T(8,128)(2,1)S(1)}, u32[]{:S(2)}, u32[]{:S(2)}) %collective-permute-start.9) | collective-permute-done | bytes 131104 | tf_op jit(solution)/shard_map/ppermute | solution.py:212
  54.3 1.7 %collective-permute-start.13 = (bf16[32,512]{1,0:T(8,128)(2,1)S(1)}, bf16[32,512]{1,0:T(8,128)(2,1)S(1)}, u32[]{:S(2)}, u32[]{:S(2)}) collective-permute-start(bf16[32,512]{1,0:T(8,128)(2,1)S(1)} %get-tuple-element.56), channel_id=1, source_target_pairs={{0,16},{8,24},{16,0},{24,8},{1,17},{9,25},{17,1},{25,9},{2,18},{10... | collective-permute-start | bytes 98312 | tf_op jit(solution)/shard_map/ppermute | solution.py:216
  59.6 3.5 %all-to-all-start.2 = ((bf16[8,32,512]{2,1,0:T(8,128)(2,1)}), bf16[8,32,512]{2,1,0:T(8,128)(2,1)S(1)}, u32[]{:S(2)}, u32[]{:S(2)}) async-start(bf16[8,32,512]{2,1,0:T(8,128)(2,1)} %column.1), calls=%async_computation.2 | async-start | bytes 524288 | tf_op jit(solution)/shard_map/all_to_all | solution.py:220
  63.9 3.2 %collective-permute-start.4 = (bf16[256,512]{1,0:T(8,128)(2,1)S(1)}, bf16[256,512]{1,0:T(8,128)(2,1)S(1)}, u32[]{:S(2)}, u32[]{:S(2)}) collective-permute-start(bf16[256,512]{1,0:T(8,128)(2,1)S(1)} %get-tuple-element.47), channel_id=1, source_target_pairs={{0,32},{32,0},{64,96},{96,64},{128,160},{160,128},{192,224},{224,1... | collective-permute-start | bytes 786440 | tf_op jit(solution)/shard_map/ppermute | solution.py:208
  69.1 3.4 %all-to-all-done.2.got_ref = bf16[8,32,512]{2,1,0:T(8,128)(2,1)S(1)} async-done(((bf16[8,32,512]{2,1,0:T(8,128)(2,1)}), bf16[8,32,512]{2,1,0:T(8,128)(2,1)S(1)}, u32[]{:S(2)}, u32[]{:S(2)}) %all-to-all-start.2) | async-done | bytes 262176 | tf_op jit(solution)/shard_map/all_to_all | solution.py:220
  72.5 5.9 %all-to-all-start.1 = ((bf16[32,8,512]{2,1,0:T(8,128)(2,1)}), bf16[32,8,512]{2,1,0:T(8,128)(2,1)S(1)}, u32[]{:S(2)}, u32[]{:S(2)}) async-start(bf16[32,8,512]{2,1,0:T(8,128)(2,1)} %pair.1), calls=%async_computation.1 | async-start | bytes 524288 | tf_op jit(solution)/shard_map/all_to_all | solution.py:220
  78.5 2.6 %collective-permute-start.17 = (bf16[32,512]{1,0:T(8,128)(2,1)S(1)}, bf16[32,512]{1,0:T(8,128)(2,1)S(1)}, u32[]{:S(2)}, u32[]{:S(2)}) collective-permute-start(bf16[32,512]{1,0:T(8,128)(2,1)S(1)} %total.1.a0), channel_id=1, source_target_pairs={{0,24},{8,0},{16,8},{24,16},{1,25},{9,1},{17,9},{25,17},{2,26},{10... | collective-permute-start | bytes 98312 | tf_op jit(solution)/shard_map/ppermute | solution.py:216
  82.1 3.2 %collective-permute-done.16.a2 = bf16[32,512]{1,0:T(8,128)(2,1)S(1)} collective-permute-done((bf16[32,512]{1,0:T(8,128)(2,1)S(1)}, bf16[32,512]{1,0:T(8,128)(2,1)S(1)}, u32[]{:S(2)}, u32[]{:S(2)}) %collective-permute-start.16) | collective-permute-done | bytes 32800 | tf_op jit(solution)/shard_map/ppermute | solution.py:216
  86.3 2.3 %collective-permute-start.20 = (bf16[128,512]{1,0:T(8,128)(2,1)S(1)}, bf16[128,512]{1,0:T(8,128)(2,1)S(1)}, u32[]{:S(2)}, u32[]{:S(2)}) collective-permute-start(bf16[128,512]{1,0:T(8,128)(2,1)S(1)} %bitcast.17), channel_id=1, source_target_pairs={{0,192},{32,224},{64,0},{96,32},{128,64},{160,96},{192,128},{224,1... | collective-permute-start | bytes 393224 | tf_op jit(solution)/shard_map/ppermute | solution.py:212
  89.3 4.6 %collective-permute-start.21 = (bf16[128,512]{1,0:T(8,128)(2,1)S(1)}, bf16[128,512]{1,0:T(8,128)(2,1)S(1)}, u32[]{:S(2)}, u32[]{:S(2)}) collective-permute-start(bf16[128,512]{1,0:T(8,128)(2,1)S(1)} %bitcast.20), channel_id=1, source_target_pairs={{0,32},{32,0},{64,96},{96,64},{128,160},{160,128},{192,224},{224,1... | collective-permute-start | bytes 393224 | tf_op jit(solution)/shard_map/ppermute | solution.py:208
  93.9 3.0 %collective-permute-start.24 = (bf16[128,512]{1,0:T(8,128)(2,1)S(1)}, bf16[128,512]{1,0:T(8,128)(2,1)S(1)}, u32[]{:S(2)}, u32[]{:S(2)}) collective-permute-start(bf16[128,512]{1,0:T(8,128)(2,1)S(1)} %collective-permute-done.20.a3), channel_id=1, source_target_pairs={{0,32},{32,0},{64,96},{96,64},{128,160},{160,128},{192,224},{224,1... | collective-permute-start | bytes 393224 | tf_op jit(solution)/shard_map/ppermute | solution.py:208
  96.9 2.6 %collective-permute-start.23 = (bf16[128,512]{1,0:T(8,128)(2,1)S(1)}, bf16[128,512]{1,0:T(8,128)(2,1)S(1)}, u32[]{:S(2)}, u32[]{:S(2)}) collective-permute-start(bf16[128,512]{1,0:T(8,128)(2,1)S(1)} %collective-permute-done.19.a2), channel_id=1, source_target_pairs={{0,32},{32,0},{64,96},{96,64},{128,160},{160,128},{192,224},{224,1... | collective-permute-start | bytes 393224 | tf_op jit(solution)/shard_map/ppermute | solution.py:208
  100.7 3.7 %collective-permute-done.7.r3_ref = bf16[8,512]{1,0:T(8,128)(2,1)S(1)} collective-permute-done((bf16[8,512]{1,0:T(8,128)(2,1)S(1)}, bf16[8,512]{1,0:T(8,128)(2,1)S(1)}, u32[]{:S(2)}, u32[]{:S(2)}) %collective-permute-start.7) | collective-permute-done | bytes 8224 | tf_op jit(solution)/shard_map/ppermute | solution.py:212
  104.4 4.0 %collective-permute-done.6.r2_ref = bf16[8,512]{1,0:T(8,128)(2,1)S(1)} collective-permute-done((bf16[8,512]{1,0:T(8,128)(2,1)S(1)}, bf16[8,512]{1,0:T(8,128)(2,1)S(1)}, u32[]{:S(2)}, u32[]{:S(2)}) %collective-permute-start.6) | collective-permute-done | bytes 8224 | tf_op jit(solution)/shard_map/ppermute | solution.py:212
  108.4 2.5 %collective-permute-done.5.r1_ref = bf16[8,512]{1,0:T(8,128)(2,1)S(1)} collective-permute-done((bf16[8,512]{1,0:T(8,128)(2,1)S(1)}, bf16[8,512]{1,0:T(8,128)(2,1)S(1)}, u32[]{:S(2)}, u32[]{:S(2)}) %collective-permute-start.5) | collective-permute-done | bytes 8224 | tf_op jit(solution)/shard_map/ppermute | solution.py:212
  111.9 1.5 %weights.1 = (f32[4,128,512]{2,1,0:T(8,128)}, f32[4,128,512]{2,1,0:T(8,128)}) custom-call(bf16[128,512]{1,0:T(8,128)(2,1)S(1)} %bitcast.21, bf16[128,512]{1,0:T(8,128)(2,1)S(1)} %collective-permute-done.18.a1, bf16[128,512]{1,0:T(8,128)(2,1)S(1)} %collective-permute-done.19.a2, bf16[128,512]{1,0:T(8,128)(2,1)S(1)} %collective-permute-done.20.a3, ...), custom_call_target="tpu_custom_call" | custom-call | flops 4194304 | bytes 1048576 | tf_op jit(solution)/shard_map/weights/pallas_call | solution.py:29
  (72 shorter events, 24.8 us)
Async XLA Ops:
  4.0 21.7 %all-to-all-start = ((bf16[32,8,512]{2,1,0:T(8,128)(2,1)}), bf16[32,8,512]{2,1,0:T(8,128)(2,1)S(1)}, u32[]{:S(2)}, u32[]{:S(2)}) async-start(bf16[32,8,512]{2,1,0:T(8,128)(2,1)} %get-tuple-element.32), calls=%async_computation | async-start | bytes 524288 | tf_op jit(solution)/shard_map/all_to_all | solution.py:220
  25.8 4.7 %collective-permute-start = (bf16[32,512]{1,0:T(8,128)(2,1)S(1)}, bf16[32,512]{1,0:T(8,128)(2,1)S(1)}, u32[]{:S(2)}, u32[]{:S(2)}) collective-permute-start(bf16[32,512]{1,0:T(8,128)(2,1)S(1)} %slice_bitcast_fusion), channel_id=1, source_target_pairs={{0,32},{32,0},{64,96},{96,64},{128,160},{160,128},{192,224},{224,1... | collective-permute-start | bytes 98312 | tf_op jit(solution)/shard_map/ppermute | solution.py:208
  30.5 4.1 %collective-permute-start.3 = (bf16[64,512]{1,0:T(8,128)(2,1)S(1)}, bf16[64,512]{1,0:T(8,128)(2,1)S(1)}, u32[]{:S(2)}, u32[]{:S(2)}) collective-permute-start(bf16[64,512]{1,0:T(8,128)(2,1)S(1)} %pad_maximum_fusion), channel_id=1, source_target_pairs={{0,192},{32,224},{64,0},{96,32},{128,64},{160,96},{192,128},{224,1... | collective-permute-start | bytes 196616 | tf_op jit(solution)/shard_map/ppermute | solution.py:212
  33.2 4.7 %collective-permute-start.2 = (bf16[64,512]{1,0:T(8,128)(2,1)S(1)}, bf16[64,512]{1,0:T(8,128)(2,1)S(1)}, u32[]{:S(2)}, u32[]{:S(2)}) collective-permute-start(bf16[64,512]{1,0:T(8,128)(2,1)S(1)} %pad_maximum_fusion), channel_id=1, source_target_pairs={{0,128},{32,160},{64,192},{96,224},{128,0},{160,32},{192,64},{224,... | collective-permute-start | bytes 196616 | tf_op jit(solution)/shard_map/ppermute | solution.py:212
  33.6 6.1 %collective-permute-start.1 = (bf16[64,512]{1,0:T(8,128)(2,1)S(1)}, bf16[64,512]{1,0:T(8,128)(2,1)S(1)}, u32[]{:S(2)}, u32[]{:S(2)}) collective-permute-start(bf16[64,512]{1,0:T(8,128)(2,1)S(1)} %pad_maximum_fusion), channel_id=1, source_target_pairs={{0,64},{32,96},{64,128},{96,160},{128,192},{160,224},{192,0},{224,... | collective-permute-start | bytes 196616 | tf_op jit(solution)/shard_map/ppermute | solution.py:212
  44.6 8.8 %collective-permute-start.9 = (bf16[128,512]{1,0:T(8,128)(2,1)S(1)}, bf16[128,512]{1,0:T(8,128)(2,1)S(1)}, u32[]{:S(2)}, u32[]{:S(2)}) collective-permute-start(bf16[128,512]{1,0:T(8,128)(2,1)S(1)} %get-tuple-element.51), channel_id=1, source_target_pairs={{0,64},{32,96},{64,128},{96,160},{128,192},{160,224},{192,0},{224,... | collective-permute-start | bytes 393224 | tf_op jit(solution)/shard_map/ppermute | solution.py:212
  44.7 8.7 %collective-permute-start.10 = (bf16[128,512]{1,0:T(8,128)(2,1)S(1)}, bf16[128,512]{1,0:T(8,128)(2,1)S(1)}, u32[]{:S(2)}, u32[]{:S(2)}) collective-permute-start(bf16[128,512]{1,0:T(8,128)(2,1)S(1)} %get-tuple-element.52), channel_id=1, source_target_pairs={{0,128},{32,160},{64,192},{96,224},{128,0},{160,32},{192,64},{224,... | collective-permute-start | bytes 393224 | tf_op jit(solution)/shard_map/ppermute | solution.py:212
  46.2 7.6 %collective-permute-start.11 = (bf16[128,512]{1,0:T(8,128)(2,1)S(1)}, bf16[128,512]{1,0:T(8,128)(2,1)S(1)}, u32[]{:S(2)}, u32[]{:S(2)}) collective-permute-start(bf16[128,512]{1,0:T(8,128)(2,1)S(1)} %get-tuple-element.53), channel_id=1, source_target_pairs={{0,192},{32,224},{64,0},{96,32},{128,64},{160,96},{192,128},{224,1... | collective-permute-start | bytes 393224 | tf_op jit(solution)/shard_map/ppermute | solution.py:212
  53.9 4.1 %collective-permute-start.12 = (bf16[32,512]{1,0:T(8,128)(2,1)S(1)}, bf16[32,512]{1,0:T(8,128)(2,1)S(1)}, u32[]{:S(2)}, u32[]{:S(2)}) collective-permute-start(bf16[32,512]{1,0:T(8,128)(2,1)S(1)} %get-tuple-element.55), channel_id=1, source_target_pairs={{0,8},{8,16},{16,24},{24,0},{1,9},{9,17},{17,25},{25,1},{2,10},{10... | collective-permute-start | bytes 98312 | tf_op jit(solution)/shard_map/ppermute | solution.py:216
  54.3 4.3 %collective-permute-start.13 = (bf16[32,512]{1,0:T(8,128)(2,1)S(1)}, bf16[32,512]{1,0:T(8,128)(2,1)S(1)}, u32[]{:S(2)}, u32[]{:S(2)}) collective-permute-start(bf16[32,512]{1,0:T(8,128)(2,1)S(1)} %get-tuple-element.56), channel_id=1, source_target_pairs={{0,16},{8,24},{16,0},{24,8},{1,17},{9,25},{17,1},{25,9},{2,18},{10... | collective-permute-start | bytes 98312 | tf_op jit(solution)/shard_map/ppermute | solution.py:216
  59.6 12.9 %all-to-all-start.2 = ((bf16[8,32,512]{2,1,0:T(8,128)(2,1)}), bf16[8,32,512]{2,1,0:T(8,128)(2,1)S(1)}, u32[]{:S(2)}, u32[]{:S(2)}) async-start(bf16[8,32,512]{2,1,0:T(8,128)(2,1)} %column.1), calls=%async_computation.2 | async-start | bytes 524288 | tf_op jit(solution)/shard_map/all_to_all | solution.py:220
  63.9 4.4 %collective-permute-start.4 = (bf16[256,512]{1,0:T(8,128)(2,1)S(1)}, bf16[256,512]{1,0:T(8,128)(2,1)S(1)}, u32[]{:S(2)}, u32[]{:S(2)}) collective-permute-start(bf16[256,512]{1,0:T(8,128)(2,1)S(1)} %get-tuple-element.47), channel_id=1, source_target_pairs={{0,32},{32,0},{64,96},{96,64},{128,160},{160,128},{192,224},{224,1... | collective-permute-start | bytes 786440 | tf_op jit(solution)/shard_map/ppermute | solution.py:208
  72.5 28.0 %all-to-all-start.1 = ((bf16[32,8,512]{2,1,0:T(8,128)(2,1)}), bf16[32,8,512]{2,1,0:T(8,128)(2,1)S(1)}, u32[]{:S(2)}, u32[]{:S(2)}) async-start(bf16[32,8,512]{2,1,0:T(8,128)(2,1)} %pair.1), calls=%async_computation.1 | async-start | bytes 524288 | tf_op jit(solution)/shard_map/all_to_all | solution.py:220
  81.0 4.3 %collective-permute-start.16 = (bf16[32,512]{1,0:T(8,128)(2,1)S(1)}, bf16[32,512]{1,0:T(8,128)(2,1)S(1)}, u32[]{:S(2)}, u32[]{:S(2)}) collective-permute-start(bf16[32,512]{1,0:T(8,128)(2,1)S(1)} %total.1.a0), channel_id=1, source_target_pairs={{0,16},{8,24},{16,0},{24,8},{1,17},{9,25},{17,1},{25,9},{2,18},{10... | collective-permute-start | bytes 98312 | tf_op jit(solution)/shard_map/ppermute | solution.py:216
  81.5 4.7 %collective-permute-start.15 = (bf16[32,512]{1,0:T(8,128)(2,1)S(1)}, bf16[32,512]{1,0:T(8,128)(2,1)S(1)}, u32[]{:S(2)}, u32[]{:S(2)}) collective-permute-start(bf16[32,512]{1,0:T(8,128)(2,1)S(1)} %total.1.a0), channel_id=1, source_target_pairs={{0,8},{8,16},{16,24},{24,0},{1,9},{9,17},{17,25},{25,1},{2,10},{10... | collective-permute-start | bytes 98312 | tf_op jit(solution)/shard_map/ppermute | solution.py:216
  86.3 7.6 %collective-permute-start.20 = (bf16[128,512]{1,0:T(8,128)(2,1)S(1)}, bf16[128,512]{1,0:T(8,128)(2,1)S(1)}, u32[]{:S(2)}, u32[]{:S(2)}) collective-permute-start(bf16[128,512]{1,0:T(8,128)(2,1)S(1)} %bitcast.17), channel_id=1, source_target_pairs={{0,192},{32,224},{64,0},{96,32},{128,64},{160,96},{192,128},{224,1... | collective-permute-start | bytes 393224 | tf_op jit(solution)/shard_map/ppermute | solution.py:212
  88.6 8.3 %collective-permute-start.19 = (bf16[128,512]{1,0:T(8,128)(2,1)S(1)}, bf16[128,512]{1,0:T(8,128)(2,1)S(1)}, u32[]{:S(2)}, u32[]{:S(2)}) collective-permute-start(bf16[128,512]{1,0:T(8,128)(2,1)S(1)} %bitcast.18), channel_id=1, source_target_pairs={{0,128},{32,160},{64,192},{96,224},{128,0},{160,32},{192,64},{224,... | collective-permute-start | bytes 393224 | tf_op jit(solution)/shard_map/ppermute | solution.py:212
  88.6 10.9 %collective-permute-start.18 = (bf16[128,512]{1,0:T(8,128)(2,1)S(1)}, bf16[128,512]{1,0:T(8,128)(2,1)S(1)}, u32[]{:S(2)}, u32[]{:S(2)}) collective-permute-start(bf16[128,512]{1,0:T(8,128)(2,1)S(1)} %bitcast.19), channel_id=1, source_target_pairs={{0,64},{32,96},{64,128},{96,160},{128,192},{160,224},{192,0},{224,... | collective-permute-start | bytes 393224 | tf_op jit(solution)/shard_map/ppermute | solution.py:212
  89.3 22.6 %collective-permute-start.21 = (bf16[128,512]{1,0:T(8,128)(2,1)S(1)}, bf16[128,512]{1,0:T(8,128)(2,1)S(1)}, u32[]{:S(2)}, u32[]{:S(2)}) collective-permute-start(bf16[128,512]{1,0:T(8,128)(2,1)S(1)} %bitcast.20), channel_id=1, source_target_pairs={{0,32},{32,0},{64,96},{96,64},{128,160},{160,128},{192,224},{224,1... | collective-permute-start | bytes 393224 | tf_op jit(solution)/shard_map/ppermute | solution.py:208
  93.9 18.0 %collective-permute-start.24 = (bf16[128,512]{1,0:T(8,128)(2,1)S(1)}, bf16[128,512]{1,0:T(8,128)(2,1)S(1)}, u32[]{:S(2)}, u32[]{:S(2)}) collective-permute-start(bf16[128,512]{1,0:T(8,128)(2,1)S(1)} %collective-permute-done.20.a3), channel_id=1, source_target_pairs={{0,32},{32,0},{64,96},{96,64},{128,160},{160,128},{192,224},{224,1... | collective-permute-start | bytes 393224 | tf_op jit(solution)/shard_map/ppermute | solution.py:208
  96.9 15.0 %collective-permute-start.23 = (bf16[128,512]{1,0:T(8,128)(2,1)S(1)}, bf16[128,512]{1,0:T(8,128)(2,1)S(1)}, u32[]{:S(2)}, u32[]{:S(2)}) collective-permute-start(bf16[128,512]{1,0:T(8,128)(2,1)S(1)} %collective-permute-done.19.a2), channel_id=1, source_target_pairs={{0,32},{32,0},{64,96},{96,64},{128,160},{160,128},{192,224},{224,1... | collective-permute-start | bytes 393224 | tf_op jit(solution)/shard_map/ppermute | solution.py:208
  99.5 12.4 %collective-permute-start.22 = (bf16[128,512]{1,0:T(8,128)(2,1)S(1)}, bf16[128,512]{1,0:T(8,128)(2,1)S(1)}, u32[]{:S(2)}, u32[]{:S(2)}) collective-permute-start(bf16[128,512]{1,0:T(8,128)(2,1)S(1)} %collective-permute-done.18.a1), channel_id=1, source_target_pairs={{0,32},{32,0},{64,96},{96,64},{128,160},{160,128},{192,224},{224,1... | collective-permute-start | bytes 393224 | tf_op jit(solution)/shard_map/ppermute | solution.py:208
  100.6 3.8 %collective-permute-start.7 = (bf16[8,512]{1,0:T(8,128)(2,1)S(1)}, bf16[8,512]{1,0:T(8,128)(2,1)S(1)}, u32[]{:S(2)}, u32[]{:S(2)}) collective-permute-start(bf16[8,512]{1,0:T(8,128)(2,1)S(1)} %hub.1), channel_id=1, source_target_pairs={{0,64},{32,96},{64,128},{96,160},{128,192},{160,224},{192,0},{224,... | collective-permute-start | bytes 24584 | tf_op jit(solution)/shard_map/ppermute | solution.py:212
  104.4 4.0 %collective-permute-start.6 = (bf16[8,512]{1,0:T(8,128)(2,1)S(1)}, bf16[8,512]{1,0:T(8,128)(2,1)S(1)}, u32[]{:S(2)}, u32[]{:S(2)}) collective-permute-start(bf16[8,512]{1,0:T(8,128)(2,1)S(1)} %hub.1), channel_id=1, source_target_pairs={{0,128},{32,160},{64,192},{96,224},{128,0},{160,32},{192,64},{224,... | collective-permute-start | bytes 24584 | tf_op jit(solution)/shard_map/ppermute | solution.py:212
  (16 other events, 90.6 us)

commit v3 on v1

v3 whole, which is shorter than its diff:
```python
import functools

import jax
import jax.numpy as jnp
from jax import lax
from jax.experimental import pallas as pl
from jax.experimental.pallas import tpu as pltpu
from jax.sharding import PartitionSpec as P

BF = jnp.bfloat16
F32 = jnp.float32
I32 = jnp.int32
PACK = 8
HUB = 4
NY = 4


def dot(a, b, ca=1, cb=0):
    return lax.dot_general(a, b, (((ca,), (cb,)), ((), ())), preferred_element_type=F32)


def call(kernel, outs, name, flops=1 << 22, nbytes=1 << 20, smem=(), hbm=(), hbm_out=False, scratch=(), alias=None):
    outs = [jax.ShapeDtypeStruct(s, d) for s, d in outs]
    vector = pl.BlockSpec(memory_space=pltpu.VMEM)
    scalar = pl.BlockSpec(memory_space=pltpu.SMEM)
    main = pl.BlockSpec(memory_space=pltpu.HBM)

    def run(*args):
        return pl.pallas_call(
            kernel,
            out_shape=outs,
            in_specs=[scalar if i in smem else main if i in hbm else vector for i in range(len(args))],
            out_specs=[main if hbm_out else vector] * len(outs),
            scratch_shapes=list(scratch),
            input_output_aliases=alias or {},
            name=name,
            compiler_params=pltpu.CompilerParams(vmem_limit_bytes=32 << 20),
            cost_estimate=pl.CostEstimate(flops=flops, bytes_accessed=nbytes, transcendentals=0),
        )(*args)

    return run


def place():
    dom = lax.axis_index("dom")
    return dom // 2, dom % 2


def iota(shape, dim):
    return lax.broadcasted_iota(I32, shape, dim)


def outgoing_kernel(sel_ref, feat_ref, r1_ref, r2_ref, r3_ref, out_ref):
    rows = dot(sel_ref[...], feat_ref[...])
    k = lax.rem(iota(rows.shape, 0), PACK)
    for i, ref in ((1, r1_ref), (2, r2_ref), (3, r3_ref)):
        rows = jnp.where(k == HUB + i, ref[...].astype(F32)[:1], rows)
    out_ref[...] = rows.astype(BF).reshape(out_ref.shape)


def packed_index(nb, verts, packed, hubs):
    y, c = place()
    h = nb - verts
    p, dom = lax.rem(h, 32), h // 32
    row = p * PACK + HUB + lax.rem(y - dom // 2 + NY, NY)
    hub = verts + row + jnp.where(lax.rem(dom, 2) == c, 0, packed)
    b = nb - verts - hubs
    bound = verts + (b // 4) * PACK + lax.rem(b, 4)
    far = jnp.where(nb < verts + hubs, hub, jnp.where(b < packed // 2, bound, -1))
    return jnp.where(nb < verts, nb, far)


def count_tile(index, at, step=128):
    slots, verts = index.shape
    rows = iota((step, verts), 0) + at
    acc = jnp.zeros((step, verts), F32)
    for j in range(slots):
        acc = acc + jnp.where(index[j : j + 1, :] == rows, 1.0, 0.0)
    return acc


def count_kernel(slot_ref, nbt_ref, route_ref, count_ref, ct_ref, c_ref, deg_ref, index_ref, sel_ref, *, hubs, table):
    packed, verts = sel_ref.shape
    cap, peers = route_ref.shape
    live = iota((cap, peers), 0) < count_ref[...]
    routes = jnp.where(live, route_ref[...], -1).astype(F32).astype(BF)
    owner = (iota((packed, peers), 0) // PACK == iota((packed, peers), 1)).astype(BF)
    every = dot(owner, routes, 1, 1)
    k = lax.rem(iota((packed, cap), 0), PACK)
    pick = jnp.sum(jnp.where(k == iota((packed, cap), 1), every, 0.0), axis=1, keepdims=True).astype(I32)
    k = lax.rem(iota((packed, 1), 0), PACK)
    pick = jnp.where(k < cap, pick, jnp.where(k == HUB, slot_ref[0], -1))
    sel_ref[...] = (pick == iota((packed, verts), 1)).astype(BF)

    nbt = nbt_ref[...]
    degree = jnp.sum((nbt < table).astype(F32), axis=0, keepdims=True)
    deg_ref[...] = jnp.broadcast_to(degree, (8, verts)).T[:, :1]
    index = packed_index(nbt, verts, packed, hubs)
    index_ref[...] = index
    for t in range(0, verts + packed, 128):
        acc = count_tile(index, t)
        ct_ref[t : t + 128, :] = acc.astype(BF)
        c_ref[:, t : t + 128] = acc.T.astype(BF)


def local_kernel(feat_ref, ws_ref, c_ref, index_ref, ct2_ref, c2_ref, zs_ref, s1_ref):
    feat = feat_ref[...]
    verts = feat.shape[0]
    zs_ref[...] = dot(feat, ws_ref[...])
    s1_ref[...] = dot(c_ref[:, :verts], feat)
    index = index_ref[...]
    for t in range(0, c2_ref.shape[1], 128):
        acc = count_tile(index, c_ref.shape[1] + t)
        ct2_ref[t : t + 128, :] = acc.astype(BF)
        c2_ref[:, t : t + 128] = acc.T.astype(BF)


def forward_kernel(
    feat_ref, cot_ref, wn_ref, c_ref, c2_ref, deg_ref, zs_ref, s1_ref, got_ref, other_ref,
    hid_ref, dz_ref, send_ref, keep_ref,
):
    verts, width = feat_ref.shape
    _, c = place()
    got = got_ref[...].reshape(-1, width)
    other = other_ref[...].reshape(-1, width)
    sums = s1_ref[...] + dot(c_ref[:, verts:], got) + dot(c2_ref[...], other)
    agg = (sums / deg_ref[...]).astype(BF)
    z = zs_ref[...] + dot(agg, wn_ref[...])
    sig = jax.nn.sigmoid(z)
    hid_ref[...] = (z * sig).astype(BF)
    dz = (cot_ref[...].astype(F32) * sig * (1.0 + z * (1.0 - sig))).astype(BF)
    dz_ref[...] = dz
    feat = feat_ref[...]
    first = c == 0
    send_ref[...] = dot(jnp.where(first, agg, feat), dz, 0, 0).astype(BF)
    keep_ref[...] = dot(jnp.where(first, feat, agg), dz, 0, 0)


def backward_kernel(dz_ref, wn_ref, ws_ref, deg_ref, ct_ref, ct2_ref, base_ref, mine_ref, other_ref):
    verts, width = dz_ref.shape
    dz = dz_ref[...]
    edge = (dot(dz, wn_ref[...], 1, 1) / deg_ref[...]).astype(BF)
    other_ref[...] = dot(ct2_ref[...], edge).astype(BF)
    mine_ref[...] = dot(ct_ref[verts:, :], edge)
    base_ref[...] = dot(dz, ws_ref[...], 1, 1) + dot(ct_ref[:verts, :], edge)


def half_kernel(keep_ref, got_ref, own_ref, s1_ref, s2_ref, s3_ref):
    y, _ = place()
    own_ref[...] = keep_ref[y] + got_ref[y].astype(F32)
    for k, ref in ((1, s1_ref), (2, s2_ref), (3, s3_ref)):
        j = lax.rem(y + k, 4)
        ref[...] = (keep_ref[j] + got_ref[j].astype(F32)).astype(BF)


def spread(rows, packed, first, per):
    r = iota((packed, rows), 0)
    k = lax.rem(r, PACK) - first
    pick = jnp.where((k >= 0) & (k < per), (r // PACK) * per + k, -1)
    return (pick == iota((packed, rows), 1)).astype(BF)


def second_pack_kernel(own_ref, r1_ref, r2_ref, r3_ref, mine_ref, out_ref):
    w = own_ref[...] + r1_ref[...].astype(F32) + r2_ref[...].astype(F32) + r3_ref[...].astype(F32)
    mine = mine_ref[...]
    packed = mine.shape[0]
    rows = dot(spread(w.shape[0], packed, HUB, 4), w.astype(BF))
    k = lax.rem(iota(mine.shape, 0), PACK)
    out_ref[...] = jnp.where(k < HUB, mine, rows).astype(BF).reshape(out_ref.shape)


def third_pack_kernel(got_ref, mine_ref, other_ref, out_ref):
    peers, pack, width = got_ref.shape
    hub = (mine_ref[...] + other_ref[...].astype(F32)).reshape(peers, pack, width)
    total = jnp.sum(got_ref[...].astype(F32), axis=0)
    total = jnp.concatenate([total[HUB:], total[HUB:]], axis=0)
    k = iota((peers, pack, width), 1)
    out_ref[...] = jnp.where(k < HUB, total[None], hub).astype(BF)


def unpack_kernel(got_ref, out_ref):
    peers, pack, width = got_ref.shape
    packed = peers * pack
    rows = out_ref.shape[0] - pack
    r = iota((rows, packed), 0)
    pick = (r // 4) * PACK + lax.rem(r, 4)
    sel = (pick == iota((rows, packed), 1)).astype(BF)
    got = got_ref[...]
    out_ref[:rows, :] = dot(sel, got.reshape(packed, width)).astype(BF)
    out_ref[rows:, :] = jnp.sum(got.astype(F32), axis=0).astype(BF)


def grad_kernel(slot_ref, base_ref, sel_ref, got_ref, own_ref, r1_ref, r2_ref, r3_ref, out_ref):
    verts, width = base_ref.shape
    got = got_ref[...].reshape(-1, width)
    k = lax.rem(iota(got.shape, 0), PACK)
    got = jnp.where(k < HUB, got, jnp.zeros_like(got))
    hub = jnp.zeros((1, width), F32)
    for i, ref in ((0, own_ref), (3, r1_ref), (2, r2_ref), (1, r3_ref)):
        tail = ref[ref.shape[0] - PACK :, :].astype(F32)
        hub = hub + tail[HUB + i : HUB + i + 1]
    at = iota((verts, width), 0) == slot_ref[0]
    out_ref[...] = base_ref[...] + dot(sel_ref[...], got, 0, 0) + jnp.where(at, hub, 0.0)


def weight_kernel(a0, a1, a2, a3, b0, b1, b2, b3, self_ref, neigh_ref):
    y, c = place()
    first = c == 0
    rows = self_ref.shape[1]
    for k, (a, b) in enumerate(((a0, b0), (a1, b1), (a2, b2), (a3, b3))):
        j = lax.rem(y - k + NY, NY)
        mine, other = a[:rows, :].astype(F32), b[:rows, :].astype(F32)
        self_ref[j] = jnp.where(first, mine, other)
        neigh_ref[j] = jnp.where(first, other, mine)


def swap_core(x):
    return lax.ppermute(x, "dom", [(i, i ^ 1) for i in range(8)])


def shift_y(x, k):
    return lax.ppermute(x, "dom", [(i, ((i // 2 + k) % 4) * 2 + i % 2) for i in range(8)])


def exchange(x):
    return lax.all_to_all(x, "shard", split_axis=0, concat_axis=0, tiled=True)


def body(features, w_self, w_neigh, cotangent, neighbours, hub_slots, send_rows, send_counts):
    verts, width = features.shape
    peers, cap = send_rows.shape[1:]
    hubs = 256
    packed = peers * PACK
    table = verts + hubs + peers * cap
    rows = verts + packed

    hub_row = lax.dynamic_slice(features, (hub_slots[0].astype(jnp.uint32), jnp.uint32(0)), (1, width))
    hub_in = [shift_y(hub_row, k) for k in (1, 2, 3)]
    ct, cm, degree, index, sel = call(
        functools.partial(count_kernel, hubs=hubs, table=table),
        [
            ((rows, verts), BF),
            ((verts, rows), BF),
            ((verts, 1), F32),
            (neighbours.shape[::-1], I32),
            ((packed, verts), BF),
        ],
        "count",
        flops=1 << 28,
        smem=(0,),
    )(hub_slots, neighbours.T, send_rows[0].T, send_counts)
    outgoing = call(outgoing_kernel, [((peers, PACK, width), BF)], "outgoing")(sel, features, *hub_in)[0]
    first = exchange(outgoing)
    first_other = swap_core(first)
    ct2, cm2, z_self, s_local = call(
        local_kernel,
        [((packed, verts), BF), ((verts, packed), BF), ((verts, width), F32), ((verts, width), F32)],
        "local",
    )(features, w_self, cm, index)

    hidden, dz, w_send, w_keep = call(
        forward_kernel,
        [((verts, width), BF), ((verts, width), BF), ((width, width), BF), ((width, width), F32)],
        "forward",
    )(features, cotangent, w_neigh, cm, cm2, degree, z_self, s_local, first, first_other)

    w_got = swap_core(w_send)
    base, mine, other = call(
        backward_kernel,
        [((verts, width), F32), ((packed, width), F32), ((packed, width), BF)],
        "backward",
    )(dz, w_neigh, w_self, degree, ct, ct2)

    chunk = width // NY
    w_own, *w_out = call(half_kernel, [((chunk, width), F32)] + [((chunk, width), BF)] * 3, "half")(
        w_keep.reshape(NY, chunk, width), w_got.reshape(NY, chunk, width)
    )
    w_in = [shift_y(w_out[k - 1], k) for k in (1, 2, 3)]

    mine, other = lax.optimization_barrier((mine, swap_core(other)))
    pack = call(second_pack_kernel, [((peers, PACK, width), BF)], "pack")(w_own, *w_in, mine)[0]
    second = exchange(pack)
    pack = call(third_pack_kernel, [((peers, PACK, width), BF)], "pack2")(second, mine, other)[0]
    third = exchange(pack)
    w_part = call(unpack_kernel, [((chunk + PACK, width), BF)], "unpack")(third)[0]

    w_all = [w_part] + [shift_y(w_part, k) for k in (1, 2, 3)]
    w_other = [swap_core(v) for v in w_all]
    grad_features = call(grad_kernel, [((verts, width), F32)], "grad", smem=(0,))(
        hub_slots, base, sel, second, *w_all
    )[0]
    grad_self, grad_neigh = call(weight_kernel, [((NY, chunk, width), F32)] * 2, "weights")(*w_all, *w_other)
    return (hidden, grad_features, grad_self.reshape(width, width), grad_neigh.reshape(width, width))


def solution(mesh):
    vertex = P(("dom", "shard"), None)
    return jax.shard_map(
        body,
        mesh=mesh,
        in_specs=(
            vertex,
            P(),
            P(),
            vertex,
            vertex,
            P(("dom", "shard")),
            P(("dom", "shard"), None, None),
            vertex,
        ),
        out_specs=(vertex, vertex, P(), P()),
        check_vma=False,
    )
```

time: 101 us -> 96.1 us (0.951)
  blocking collectives: 39.9 us -> 49.9 us
  starting transfers between devices: 35.5 us -> 27.8 us
  waiting for transfers between devices: 11.4 us -> 5.73 us
  matrix products: 1.22 us -> 0 us
  local copies, waits for them, and re-layouts: 1.04 us -> 2.14 us
    all_to_all x2 -> x3, blocking collectives: 39.9 us -> 49.9 us  [exchange(): return lax.all_to_all(x, 'shard', split_axis=0, concat_axis=0, tiled=True)]
    all_to_all x1 -> x0, starting transfers between devices: 4.12 us -> none  [exchange(): return lax.all_to_all(x, 'shard', split_axis=0, concat_axis=0, tiled=True)]
    ppermute x7, waiting for transfers between devices: 3.39 us -> 0.6 us  [swap_core(): return lax.ppermute(x, 'dom', [(i, i ^ 1) for i in range(8)])]
    ppermute x12 -> x9, waiting for transfers between devices: 7.5 us -> 5.13 us  [shift_y(): lax.ppermute(x, 'dom', [(i, (i // 2 + k) % 4 * 2 + i % 2) for i in range(...]
    ppermute x12 -> x9, starting transfers between devices: 15.2 us -> 13 us  [shift_y(): lax.ppermute(x, 'dom', [(i, (i // 2 + k) % 4 * 2 + i % 2) for i in range(...]
    ppermute x7, starting transfers between devices: 16.2 us -> 14.8 us  [swap_core(): return lax.ppermute(x, 'dom', [(i, i ^ 1) for i in range(8)])]
    dot_general x1 -> x0, matrix products: 1.22 us -> none  [dot(): lax.dot_general(a, b, (((ca,), (cb,)), ((), ())), preferred_element_type=...]
    pallas_call x10 -> x11, Pallas kernels: 9.45 us -> 8.8 us  [run(): pl.pallas_call(kernel, out_shape=outs, in_specs=[scalar if i in smem else...]
  transfers between devices with their start and end apart: 20 -> 16, of which waited for: 9 -> 4; matrix products, arithmetic and copies ran while one was open for 0% -> 0% of each run, Pallas kernels for 5% -> 5%
where the time goes in v3:
time: 96.1 us; the launch traced here: 95.7 us
  blocking collectives  49.9 us (52%)
  starting transfers between devices  27.8 us (29%)
  Pallas kernels  8.8 us (9%)
  waiting for transfers between devices  5.73 us (6%)
  local copies, waits for them, and re-layouts  2.14 us (2%)
  between operations  1.4 us (1%)
    all_to_all x3, blocking collectives, exchange(): return lax.all_to_all(x, 'shard', split_axis=0, concat_axis=0, tiled=True)  49.9 us
    ppermute x7, starting transfers between devices, swap_core(): return lax.ppermute(x, 'dom', [(i, i ^ 1) for i in range(8)])  14.8 us
    ppermute x9, starting transfers between devices, shift_y(): lax.ppermute(x, 'dom', [(i, (i // 2 + k) % 4 * 2 + i % 2) for i in range(...  13 us
    pallas_call x11, Pallas kernels, run(): pl.pallas_call(kernel, out_shape=outs, in_specs=[scalar if i in smem else...  8.8 us
    ppermute x9, waiting for transfers between devices, shift_y(): lax.ppermute(x, 'dom', [(i, (i // 2 + k) % 4 * 2 + i % 2) for i in range(...  5.13 us
  transfers between devices with their start and end apart: 16, of which 4 were waited for; matrix products, arithmetic and copies ran while one was open for 0% of the time, Pallas kernels for 5%

profile of v3, /device:TPU:1, one launch (start us, length us, event | category | flops | bytes accessed | tf_op | source)
XLA Modules:
  0.0 95.7 jit_solution(6369361997889990934)
XLA Ops:
  1.3 0.7 constant_dynamic-slice_fusion
  2.0 3.6 %collective-permute-start.2 = (bf16[1,512]{1,0:T(2,128)(2,1)S(1)}, bf16[1,512]{1,0:T(2,128)(2,1)S(1)}, u32[]{:S(2)}, u32[]{:S(2)}) collective-permute-start(bf16[1,512]{1,0:T(2,128)(2,1)S(1)} %constant_dynamic-slice_fusion), channel_id=1, source_target_pairs={{0,192},{32,224},{64,0},{96,32},{128,64},{160,96},{192,128},{224,1... | collective-permute-start | bytes 3080 | tf_op jit(solution)/shard_map/ppermute | solution.py:222
  7.2 0.8 copy-done.4
  8.0 2.1 %count.1 = (bf16[512,256]{1,0:T(8,128)(2,1)S(1)}, bf16[256,512]{1,0:T(8,128)(2,1)S(1)}, f32[256,1]{1,0:T(8,128)S(1)}, s32[32,256]{1,0:T(8,128)S(1)}, bf16[256,256]{1,0:T(8,128)(2,1)S(1)}) custom-call(s32[1]{0:T(128)S(6)} %copy.12.slot_ref, s32[32,256]{1,0:T(8,128)S(1)} %bitcast.11, s32[4,32]{1,0:T(4,128)S(1)} %bitcast.12, s32[1,32]{1,0:T(1,128)S(1)} %copy-done.6), custom_call_target="tpu_custom_call" | custom-call | flops 268435456 | bytes 1048576 | tf_op jit(solution)/shard_map/count/pallas_call | solution.py:29
  10.4 20.5 %all_to_all.15.got_ref = bf16[32,8,512]{2,1,0:T(8,128)(2,1)S(1)} all-to-all(bf16[32,8,512]{2,1,0:T(8,128)(2,1)S(1)} %outgoing.1), channel_id=1, replica_groups=mesh['dom'=8,'shard'=32] {'shard'}, dimensions={0} | all-to-all | bytes 524288 | tf_op jit(solution)/shard_map/all_to_all | solution.py:226
  30.9 3.7 %collective-permute-start.3 = (bf16[32,8,512]{2,1,0:T(8,128)(2,1)S(1)}, bf16[32,8,512]{2,1,0:T(8,128)(2,1)S(1)}, u32[]{:S(2)}, u32[]{:S(2)}) collective-permute-start(bf16[32,8,512]{2,1,0:T(8,128)(2,1)S(1)} %all_to_all.15.got_ref), channel_id=1, source_target_pairs={{0,32},{32,0},{64,96},{96,64},{128,160},{160,128},{192,224},{224,1... | collective-permute-start | bytes 786440 | tf_op jit(solution)/shard_map/ppermute | solution.py:218
  34.6 1.1 %local.1 = (bf16[256,256]{1,0:T(8,128)(2,1)S(1)}, bf16[256,256]{1,0:T(8,128)(2,1)S(1)}, f32[256,512]{1,0:T(8,128)S(1)}, f32[256,512]{1,0:T(8,128)S(1)}) custom-call(bf16[256,512]{1,0:T(8,128)(2,1)S(1)} %copy-done, bf16[512,512]{1,0:T(8,128)(2,1)S(1)} %copy-done.1, bf16[256,512]{1,0:T(8,128)(2,1)S(1)} %get-tuple-element.28.c_ref, ...), custom_call_target="tpu_custom_call" | custom-call | flops 4194304 | bytes 1048576 | tf_op jit(solution)/shard_map/local/pallas_call | solution.py:29
  35.7 1.4 %forward.1 = (bf16[256,512]{1,0:T(8,128)(2,1)}, bf16[256,512]{1,0:T(8,128)(2,1)S(1)}, bf16[512,512]{1,0:T(8,128)(2,1)S(1)}, f32[512,512]{1,0:T(8,128)S(1)}) custom-call(bf16[256,512]{1,0:T(8,128)(2,1)S(1)} %copy-done, bf16[256,512]{1,0:T(8,128)(2,1)S(1)} %copy-done.3, bf16[512,512]{1,0:T(8,128)(2,1)S(1)} %copy-done.2, ...), custom_call_target="tpu_custom_call" | custom-call | flops 4194304 | bytes 1048576 | tf_op jit(solution)/shard_map/forward/pallas_call | solution.py:29
  37.5 0.8 backward.1
  39.1 1.6 %collective-permute-start.5 = (bf16[128,512]{1,0:T(8,128)(2,1)S(1)}, bf16[128,512]{1,0:T(8,128)(2,1)S(1)}, u32[]{:S(2)}, u32[]{:S(2)}) collective-permute-start(bf16[128,512]{1,0:T(8,128)(2,1)S(1)} %get-tuple-element.43), channel_id=1, source_target_pairs={{0,64},{32,96},{64,128},{96,160},{128,192},{160,224},{192,0},{224,... | collective-permute-start | bytes 393224 | tf_op jit(solution)/shard_map/ppermute | solution.py:222
  40.7 1.6 %collective-permute-start.6 = (bf16[128,512]{1,0:T(8,128)(2,1)S(1)}, bf16[128,512]{1,0:T(8,128)(2,1)S(1)}, u32[]{:S(2)}, u32[]{:S(2)}) collective-permute-start(bf16[128,512]{1,0:T(8,128)(2,1)S(1)} %get-tuple-element.44), channel_id=1, source_target_pairs={{0,128},{32,160},{64,192},{96,224},{128,0},{160,32},{192,64},{224,... | collective-permute-start | bytes 393224 | tf_op jit(solution)/shard_map/ppermute | solution.py:222
  42.3 0.9 collective-permute-start.7
  43.2 1.9 %collective-permute-done.5.r1_ref = bf16[128,512]{1,0:T(8,128)(2,1)S(1)} collective-permute-done((bf16[128,512]{1,0:T(8,128)(2,1)S(1)}, bf16[128,512]{1,0:T(8,128)(2,1)S(1)}, u32[]{:S(2)}, u32[]{:S(2)}) %collective-permute-start.5) | collective-permute-done | bytes 131104 | tf_op jit(solution)/shard_map/ppermute | solution.py:222
  45.1 3.2 %collective-permute-done.6.r2_ref = bf16[128,512]{1,0:T(8,128)(2,1)S(1)} collective-permute-done((bf16[128,512]{1,0:T(8,128)(2,1)S(1)}, bf16[128,512]{1,0:T(8,128)(2,1)S(1)}, u32[]{:S(2)}, u32[]{:S(2)}) %collective-permute-start.6) | collective-permute-done | bytes 131104 | tf_op jit(solution)/shard_map/ppermute | solution.py:222
  48.6 13.7 %all_to_all.16.got_ref = bf16[32,8,512]{2,1,0:T(8,128)(2,1)S(1)} all-to-all(bf16[32,8,512]{2,1,0:T(8,128)(2,1)S(1)} %pack.1), channel_id=1, replica_groups=mesh['dom'=8,'shard'=32] {'shard'}, dimensions={0} | all-to-all | bytes 524288 | tf_op jit(solution)/shard_map/all_to_all | solution.py:226
  62.4 15.7 %all_to_all.17.got_ref = bf16[32,8,512]{2,1,0:T(8,128)(2,1)S(1)} all-to-all(bf16[32,8,512]{2,1,0:T(8,128)(2,1)S(1)} %pack2.1), channel_id=1, replica_groups=mesh['dom'=8,'shard'=32] {'shard'}, dimensions={0} | all-to-all | bytes 524288 | tf_op jit(solution)/shard_map/all_to_all | solution.py:226
  78.3 2.8 %collective-permute-start.11 = (bf16[136,512]{1,0:T(8,128)(2,1)S(1)}, bf16[136,512]{1,0:T(8,128)(2,1)S(1)}, u32[]{:S(2)}, u32[]{:S(2)}) collective-permute-start(bf16[136,512]{1,0:T(8,128)(2,1)S(1)} %unpack.1.own_ref.a0), channel_id=1, source_target_pairs={{0,192},{32,224},{64,0},{96,32},{128,64},{160,96},{192,128},{224,1... | collective-permute-start | bytes 417800 | tf_op jit(solution)/shard_map/ppermute | solution.py:222
  81.1 1.5 %collective-permute-start.10 = (bf16[136,512]{1,0:T(8,128)(2,1)S(1)}, bf16[136,512]{1,0:T(8,128)(2,1)S(1)}, u32[]{:S(2)}, u32[]{:S(2)}) collective-permute-start(bf16[136,512]{1,0:T(8,128)(2,1)S(1)} %unpack.1.own_ref.a0), channel_id=1, source_target_pairs={{0,128},{32,160},{64,192},{96,224},{128,0},{160,32},{192,64},{224,... | collective-permute-start | bytes 417800 | tf_op jit(solution)/shard_map/ppermute | solution.py:222
  82.6 4.2 %collective-permute-start.12 = (bf16[136,512]{1,0:T(8,128)(2,1)S(1)}, bf16[136,512]{1,0:T(8,128)(2,1)S(1)}, u32[]{:S(2)}, u32[]{:S(2)}) collective-permute-start(bf16[136,512]{1,0:T(8,128)(2,1)S(1)} %unpack.1.own_ref.a0), channel_id=1, source_target_pairs={{0,32},{32,0},{64,96},{96,64},{128,160},{160,128},{192,224},{224,1... | collective-permute-start | bytes 417800 | tf_op jit(solution)/shard_map/ppermute | solution.py:218
  86.8 2.4 %collective-permute-start.15 = (bf16[136,512]{1,0:T(8,128)(2,1)S(1)}, bf16[136,512]{1,0:T(8,128)(2,1)S(1)}, u32[]{:S(2)}, u32[]{:S(2)}) collective-permute-start(bf16[136,512]{1,0:T(8,128)(2,1)S(1)} %collective-permute-done.11.r3_ref.a3), channel_id=1, source_target_pairs={{0,32},{32,0},{64,96},{96,64},{128,160},{160,128},{192,224},{224,1... | collective-permute-start | bytes 417800 | tf_op jit(solution)/shard_map/ppermute | solution.py:218
  89.2 2.5 %collective-permute-start.14 = (bf16[136,512]{1,0:T(8,128)(2,1)S(1)}, bf16[136,512]{1,0:T(8,128)(2,1)S(1)}, u32[]{:S(2)}, u32[]{:S(2)}) collective-permute-start(bf16[136,512]{1,0:T(8,128)(2,1)S(1)} %collective-permute-done.10.r2_ref.a2), channel_id=1, source_target_pairs={{0,32},{32,0},{64,96},{96,64},{128,160},{160,128},{192,224},{224,1... | collective-permute-start | bytes 417800 | tf_op jit(solution)/shard_map/ppermute | solution.py:218
  91.7 1.5 %collective-permute-start.13 = (bf16[136,512]{1,0:T(8,128)(2,1)S(1)}, bf16[136,512]{1,0:T(8,128)(2,1)S(1)}, u32[]{:S(2)}, u32[]{:S(2)}) collective-permute-start(bf16[136,512]{1,0:T(8,128)(2,1)S(1)} %collective-permute-done.9.r1_ref.a1), channel_id=1, source_target_pairs={{0,32},{32,0},{64,96},{96,64},{128,160},{160,128},{192,224},{224,1... | collective-permute-start | bytes 417800 | tf_op jit(solution)/shard_map/ppermute | solution.py:218
  93.1 1.0 %grad.1 = f32[256,512]{1,0:T(8,128)} custom-call(s32[1]{0:T(128)S(6)} %copy.12.slot_ref, f32[256,512]{1,0:T(8,128)S(1)} %get-tuple-element.39.base_ref, bf16[256,256]{1,0:T(8,128)(2,1)S(1)} %get-tuple-element.34.sel_ref, bf16[32,8,512]{2,1,0:T(8,128)(2,1)S(1)} %all_to_all.16.got_ref, bf16[136,512]{1,0:T(8,128)(2,1)S(1)} %unpack.1.own_ref.a0, ...), custom_call_target="tpu_custom_call" | custom-call | flops 4194304 | bytes 1048576 | tf_op jit(solution)/shard_map/grad/pallas_call | solution.py:29
  94.2 1.5 %weights.1 = (f32[4,128,512]{2,1,0:T(8,128)}, f32[4,128,512]{2,1,0:T(8,128)}) custom-call(bf16[136,512]{1,0:T(8,128)(2,1)S(1)} %unpack.1.own_ref.a0, bf16[136,512]{1,0:T(8,128)(2,1)S(1)} %collective-permute-done.9.r1_ref.a1, bf16[136,512]{1,0:T(8,128)(2,1)S(1)} %collective-permute-done.10.r2_ref.a2, bf16[136,512]{1,0:T(8,128)(2,1)S(1)} %collective-permute-done.11.r3_ref.a3, ...), custom_call_target="tpu_custom_call" | custom-call | flops 4194304 | bytes 1048576 | tf_op jit(solution)/shard_map/weights/pallas_call | solution.py:29
  (37 shorter events, 3.8 us)
Async XLA Ops:
  2.0 4.6 %copy-start.5 = (s32[1,32,4]{1,2,0:T(4,128)S(1)}, s32[1,32,4]{1,2,0:T(4,128)}, u32[]{:S(2)}) copy-start(s32[1,32,4]{1,2,0:T(4,128)} %param.14) | copy-start | bytes 1540
  2.0 8.1 %collective-permute-start.2 = (bf16[1,512]{1,0:T(2,128)(2,1)S(1)}, bf16[1,512]{1,0:T(2,128)(2,1)S(1)}, u32[]{:S(2)}, u32[]{:S(2)}) collective-permute-start(bf16[1,512]{1,0:T(2,128)(2,1)S(1)} %constant_dynamic-slice_fusion), channel_id=1, source_target_pairs={{0,192},{32,224},{64,0},{96,32},{128,64},{160,96},{192,128},{224,1... | collective-permute-start | bytes 3080 | tf_op jit(solution)/shard_map/ppermute | solution.py:222
  5.5 4.5 %collective-permute-start.1 = (bf16[1,512]{1,0:T(2,128)(2,1)S(1)}, bf16[1,512]{1,0:T(2,128)(2,1)S(1)}, u32[]{:S(2)}, u32[]{:S(2)}) collective-permute-start(bf16[1,512]{1,0:T(2,128)(2,1)S(1)} %constant_dynamic-slice_fusion), channel_id=1, source_target_pairs={{0,128},{32,160},{64,192},{96,224},{128,0},{160,32},{192,64},{224,... | collective-permute-start | bytes 3080 | tf_op jit(solution)/shard_map/ppermute | solution.py:222
  5.9 4.2 %collective-permute-start = (bf16[1,512]{1,0:T(2,128)(2,1)S(1)}, bf16[1,512]{1,0:T(2,128)(2,1)S(1)}, u32[]{:S(2)}, u32[]{:S(2)}) collective-permute-start(bf16[1,512]{1,0:T(2,128)(2,1)S(1)} %constant_dynamic-slice_fusion), channel_id=1, source_target_pairs={{0,64},{32,96},{64,128},{96,160},{128,192},{160,224},{192,0},{224,... | collective-permute-start | bytes 3080 | tf_op jit(solution)/shard_map/ppermute | solution.py:222
  6.6 0.7 copy-start.6
  7.2 0.8 copy-start.4
  8.0 2.1 %copy-start = (bf16[256,512]{1,0:T(8,128)(2,1)S(1)}, bf16[256,512]{1,0:T(8,128)(2,1)}, u32[]{:S(2)}) copy-start(bf16[256,512]{1,0:T(8,128)(2,1)} %feat_ref.5) | copy-start | bytes 786436
  10.1 24.4 %copy-start.1 = (bf16[512,512]{1,0:T(8,128)(2,1)S(1)}, bf16[512,512]{1,0:T(8,128)(2,1)}, u32[]{:S(2)}) copy-start(bf16[512,512]{1,0:T(8,128)(2,1)} %ws_ref.3) | copy-start | bytes 1572868
  30.9 4.8 %collective-permute-start.3 = (bf16[32,8,512]{2,1,0:T(8,128)(2,1)S(1)}, bf16[32,8,512]{2,1,0:T(8,128)(2,1)S(1)}, u32[]{:S(2)}, u32[]{:S(2)}) collective-permute-start(bf16[32,8,512]{2,1,0:T(8,128)(2,1)S(1)} %all_to_all.15.got_ref), channel_id=1, source_target_pairs={{0,32},{32,0},{64,96},{96,64},{128,160},{160,128},{192,224},{224,1... | collective-permute-start | bytes 786440 | tf_op jit(solution)/shard_map/ppermute | solution.py:218
  34.6 1.2 %copy-start.2 = (bf16[512,512]{1,0:T(8,128)(2,1)S(1)}, bf16[512,512]{1,0:T(8,128)(2,1)}, u32[]{:S(2)}) copy-start(bf16[512,512]{1,0:T(8,128)(2,1)} %wn_ref.3) | copy-start | bytes 1572868
  34.6 1.2 %copy-start.3 = (bf16[256,512]{1,0:T(8,128)(2,1)S(1)}, bf16[256,512]{1,0:T(8,128)(2,1)}, u32[]{:S(2)}) copy-start(bf16[256,512]{1,0:T(8,128)(2,1)} %cot_ref.1) | copy-start | bytes 786436
  37.1 1.9 %collective-permute-start.4 = (bf16[512,512]{1,0:T(8,128)(2,1)S(1)}, bf16[512,512]{1,0:T(8,128)(2,1)S(1)}, u32[]{:S(2)}, u32[]{:S(2)}) collective-permute-start(bf16[512,512]{1,0:T(8,128)(2,1)S(1)} %get-tuple-element.41), channel_id=1, source_target_pairs={{0,32},{32,0},{64,96},{96,64},{128,160},{160,128},{192,224},{224,1... | collective-permute-start | bytes 1572872 | tf_op jit(solution)/shard_map/ppermute | solution.py:218
  38.3 4.9 %collective-permute-start.8 = (bf16[256,512]{1,0:T(8,128)(2,1)S(1)}, bf16[256,512]{1,0:T(8,128)(2,1)S(1)}, u32[]{:S(2)}, u32[]{:S(2)}) collective-permute-start(bf16[256,512]{1,0:T(8,128)(2,1)S(1)} %get-tuple-element.47), channel_id=1, source_target_pairs={{0,32},{32,0},{64,96},{96,64},{128,160},{160,128},{192,224},{224,1... | collective-permute-start | bytes 786440 | tf_op jit(solution)/shard_map/ppermute | solution.py:218
  39.1 6.0 %collective-permute-start.5 = (bf16[128,512]{1,0:T(8,128)(2,1)S(1)}, bf16[128,512]{1,0:T(8,128)(2,1)S(1)}, u32[]{:S(2)}, u32[]{:S(2)}) collective-permute-start(bf16[128,512]{1,0:T(8,128)(2,1)S(1)} %get-tuple-element.43), channel_id=1, source_target_pairs={{0,64},{32,96},{64,128},{96,160},{128,192},{160,224},{192,0},{224,... | collective-permute-start | bytes 393224 | tf_op jit(solution)/shard_map/ppermute | solution.py:222
  40.7 7.6 %collective-permute-start.6 = (bf16[128,512]{1,0:T(8,128)(2,1)S(1)}, bf16[128,512]{1,0:T(8,128)(2,1)S(1)}, u32[]{:S(2)}, u32[]{:S(2)}) collective-permute-start(bf16[128,512]{1,0:T(8,128)(2,1)S(1)} %get-tuple-element.44), channel_id=1, source_target_pairs={{0,128},{32,160},{64,192},{96,224},{128,0},{160,32},{192,64},{224,... | collective-permute-start | bytes 393224 | tf_op jit(solution)/shard_map/ppermute | solution.py:222
  42.3 6.1 %collective-permute-start.7 = (bf16[128,512]{1,0:T(8,128)(2,1)S(1)}, bf16[128,512]{1,0:T(8,128)(2,1)S(1)}, u32[]{:S(2)}, u32[]{:S(2)}) collective-permute-start(bf16[128,512]{1,0:T(8,128)(2,1)S(1)} %get-tuple-element.45), channel_id=1, source_target_pairs={{0,192},{32,224},{64,0},{96,32},{128,64},{160,96},{192,128},{224,1... | collective-permute-start | bytes 393224 | tf_op jit(solution)/shard_map/ppermute | solution.py:222
  78.3 8.5 %collective-permute-start.11 = (bf16[136,512]{1,0:T(8,128)(2,1)S(1)}, bf16[136,512]{1,0:T(8,128)(2,1)S(1)}, u32[]{:S(2)}, u32[]{:S(2)}) collective-permute-start(bf16[136,512]{1,0:T(8,128)(2,1)S(1)} %unpack.1.own_ref.a0), channel_id=1, source_target_pairs={{0,192},{32,224},{64,0},{96,32},{128,64},{160,96},{192,128},{224,1... | collective-permute-start | bytes 417800 | tf_op jit(solution)/shard_map/ppermute | solution.py:222
  81.1 8.1 %collective-permute-start.10 = (bf16[136,512]{1,0:T(8,128)(2,1)S(1)}, bf16[136,512]{1,0:T(8,128)(2,1)S(1)}, u32[]{:S(2)}, u32[]{:S(2)}) collective-permute-start(bf16[136,512]{1,0:T(8,128)(2,1)S(1)} %unpack.1.own_ref.a0), channel_id=1, source_target_pairs={{0,128},{32,160},{64,192},{96,224},{128,0},{160,32},{192,64},{224,... | collective-permute-start | bytes 417800 | tf_op jit(solution)/shard_map/ppermute | solution.py:222
  82.6 9.1 %collective-permute-start.9 = (bf16[136,512]{1,0:T(8,128)(2,1)S(1)}, bf16[136,512]{1,0:T(8,128)(2,1)S(1)}, u32[]{:S(2)}, u32[]{:S(2)}) collective-permute-start(bf16[136,512]{1,0:T(8,128)(2,1)S(1)} %unpack.1.own_ref.a0), channel_id=1, source_target_pairs={{0,64},{32,96},{64,128},{96,160},{128,192},{160,224},{192,0},{224,... | collective-permute-start | bytes 417800 | tf_op jit(solution)/shard_map/ppermute | solution.py:222
  82.6 11.6 %collective-permute-start.12 = (bf16[136,512]{1,0:T(8,128)(2,1)S(1)}, bf16[136,512]{1,0:T(8,128)(2,1)S(1)}, u32[]{:S(2)}, u32[]{:S(2)}) collective-permute-start(bf16[136,512]{1,0:T(8,128)(2,1)S(1)} %unpack.1.own_ref.a0), channel_id=1, source_target_pairs={{0,32},{32,0},{64,96},{96,64},{128,160},{160,128},{192,224},{224,1... | collective-permute-start | bytes 417800 | tf_op jit(solution)/shard_map/ppermute | solution.py:218
  86.8 7.4 %collective-permute-start.15 = (bf16[136,512]{1,0:T(8,128)(2,1)S(1)}, bf16[136,512]{1,0:T(8,128)(2,1)S(1)}, u32[]{:S(2)}, u32[]{:S(2)}) collective-permute-start(bf16[136,512]{1,0:T(8,128)(2,1)S(1)} %collective-permute-done.11.r3_ref.a3), channel_id=1, source_target_pairs={{0,32},{32,0},{64,96},{96,64},{128,160},{160,128},{192,224},{224,1... | collective-permute-start | bytes 417800 | tf_op jit(solution)/shard_map/ppermute | solution.py:218
  89.2 5.0 %collective-permute-start.14 = (bf16[136,512]{1,0:T(8,128)(2,1)S(1)}, bf16[136,512]{1,0:T(8,128)(2,1)S(1)}, u32[]{:S(2)}, u32[]{:S(2)}) collective-permute-start(bf16[136,512]{1,0:T(8,128)(2,1)S(1)} %collective-permute-done.10.r2_ref.a2), channel_id=1, source_target_pairs={{0,32},{32,0},{64,96},{96,64},{128,160},{160,128},{192,224},{224,1... | collective-permute-start | bytes 417800 | tf_op jit(solution)/shard_map/ppermute | solution.py:218
  91.7 2.5 %collective-permute-start.13 = (bf16[136,512]{1,0:T(8,128)(2,1)S(1)}, bf16[136,512]{1,0:T(8,128)(2,1)S(1)}, u32[]{:S(2)}, u32[]{:S(2)}) collective-permute-start(bf16[136,512]{1,0:T(8,128)(2,1)S(1)} %collective-permute-done.9.r1_ref.a1), channel_id=1, source_target_pairs={{0,32},{32,0},{64,96},{96,64},{128,160},{160,128},{192,224},{224,1... | collective-permute-start | bytes 417800 | tf_op jit(solution)/shard_map/ppermute | solution.py:218

commit v4 on v3

v4 whole, which is shorter than its diff:
```python
import functools

import jax
import jax.numpy as jnp
from jax import lax
from jax.experimental import pallas as pl
from jax.experimental.pallas import tpu as pltpu
from jax.sharding import Mesh
from jax.sharding import PartitionSpec as P

BF = jnp.bfloat16
F32 = jnp.float32
I32 = jnp.int32
PACK = 8
HUB = 4
NY, NX, NZ = 4, 4, 8


def dot(a, b, ca=1, cb=0):
    return lax.dot_general(a, b, (((ca,), (cb,)), ((), ())), preferred_element_type=F32)


def call(kernel, outs, name, flops=1 << 22, nbytes=1 << 20, smem=(), hbm=(), hbm_out=False, scratch=(), alias=None):
    outs = [jax.ShapeDtypeStruct(s, d) for s, d in outs]
    vector = pl.BlockSpec(memory_space=pltpu.VMEM)
    scalar = pl.BlockSpec(memory_space=pltpu.SMEM)
    main = pl.BlockSpec(memory_space=pltpu.HBM)

    def run(*args):
        return pl.pallas_call(
            kernel,
            out_shape=outs,
            in_specs=[scalar if i in smem else main if i in hbm else vector for i in range(len(args))],
            out_specs=[main if hbm_out else vector] * len(outs),
            scratch_shapes=list(scratch),
            input_output_aliases=alias or {},
            name=name,
            compiler_params=pltpu.CompilerParams(vmem_limit_bytes=32 << 20),
            cost_estimate=pl.CostEstimate(flops=flops, bytes_accessed=nbytes, transcendentals=0),
        )(*args)

    return run


def place():
    return lax.axis_index("y"), lax.axis_index("c")


def iota(shape, dim):
    return lax.broadcasted_iota(I32, shape, dim)


def outgoing_kernel(sel_ref, feat_ref, r1_ref, r2_ref, r3_ref, out_ref):
    rows = dot(sel_ref[...], feat_ref[...])
    k = lax.rem(iota(rows.shape, 0), PACK)
    for i, ref in ((1, r1_ref), (2, r2_ref), (3, r3_ref)):
        rows = jnp.where(k == HUB + i, ref[...].astype(F32)[:1], rows)
    out_ref[...] = rows.astype(BF).reshape(out_ref.shape)


def packed_index(nb, verts, packed, hubs):
    y, c = place()
    h = nb - verts
    p, dom = lax.rem(h, 32), h // 32
    row = p * PACK + HUB + lax.rem(y - dom // 2 + NY, NY)
    hub = verts + row + jnp.where(lax.rem(dom, 2) == c, 0, packed)
    b = nb - verts - hubs
    bound = verts + (b // 4) * PACK + lax.rem(b, 4)
    far = jnp.where(nb < verts + hubs, hub, jnp.where(b < packed // 2, bound, -1))
    return jnp.where(nb < verts, nb, far)


def count_tile(index, at, step=128):
    slots, verts = index.shape
    index = jnp.clip(index - at, -1, step).astype(F32).astype(BF)
    rows = iota((step, verts), 0).astype(F32).astype(BF)
    one, zero = jnp.ones((), BF), jnp.zeros((), BF)
    acc = jnp.zeros((step, verts), BF)
    for j in range(slots):
        acc = acc + jnp.where(index[j : j + 1, :] == rows, one, zero)
    return acc


def count_kernel(slot_ref, nbt_ref, route_ref, count_ref, ct_ref, c_ref, deg_ref, index_ref, sel_ref, *, hubs, table):
    packed, verts = sel_ref.shape
    cap, peers = route_ref.shape
    live = iota((cap, peers), 0) < count_ref[...]
    routes = jnp.where(live, route_ref[...], -1).astype(F32).astype(BF)
    owner = (iota((packed, peers), 0) // PACK == iota((packed, peers), 1)).astype(BF)
    every = dot(owner, routes, 1, 1)
    k = lax.rem(iota((packed, cap), 0), PACK)
    pick = jnp.sum(jnp.where(k == iota((packed, cap), 1), every, 0.0), axis=1, keepdims=True).astype(I32)
    k = lax.rem(iota((packed, 1), 0), PACK)
    pick = jnp.where(k < cap, pick, jnp.where(k == HUB, slot_ref[0], -1))
    sel_ref[...] = (pick == iota((packed, verts), 1)).astype(BF)

    nbt = nbt_ref[...]
    degree = jnp.sum((nbt < table).astype(F32), axis=0, keepdims=True)
    deg_ref[...] = jnp.broadcast_to(degree, (8, verts)).T[:, :1]
    index = packed_index(nbt, verts, packed, hubs)
    index_ref[...] = index
    for t in range(0, verts + packed, 128):
        acc = count_tile(index, t)
        ct_ref[t : t + 128, :] = acc
        c_ref[:, t : t + 128] = acc.astype(F32).T.astype(BF)


def local_kernel(feat_ref, ws_ref, c_ref, index_ref, ct2_ref, c2_ref, zs_ref, s1_ref):
    feat = feat_ref[...]
    verts = feat.shape[0]
    zs_ref[...] = dot(feat, ws_ref[...])
    s1_ref[...] = dot(c_ref[:, :verts], feat)
    index = index_ref[...]
    for t in range(0, c2_ref.shape[1], 128):
        acc = count_tile(index, c_ref.shape[1] + t)
        ct2_ref[t : t + 128, :] = acc
        c2_ref[:, t : t + 128] = acc.astype(F32).T.astype(BF)


def forward_kernel(
    feat_ref, cot_ref, wn_ref, c_ref, c2_ref, deg_ref, zs_ref, s1_ref, got_ref, other_ref,
    hid_ref, dz_ref, send_ref, keep_ref,
):
    verts, width = feat_ref.shape
    _, c = place()
    got = got_ref[...].reshape(-1, width)
    other = other_ref[...].reshape(-1, width)
    sums = s1_ref[...] + dot(c_ref[:, verts:], got) + dot(c2_ref[...], other)
    agg = (sums / deg_ref[...]).astype(BF)
    z = zs_ref[...] + dot(agg, wn_ref[...])
    sig = jax.nn.sigmoid(z)
    hid_ref[...] = (z * sig).astype(BF)
    dz = (cot_ref[...].astype(F32) * sig * (1.0 + z * (1.0 - sig))).astype(BF)
    dz_ref[...] = dz
    feat = feat_ref[...]
    first = c == 0
    send_ref[...] = dot(jnp.where(first, agg, feat), dz, 0, 0).astype(BF)
    keep_ref[...] = dot(jnp.where(first, feat, agg), dz, 0, 0)


def backward_kernel(dz_ref, wn_ref, ws_ref, deg_ref, ct_ref, ct2_ref, base_ref, mine_ref, other_ref):
    verts, width = dz_ref.shape
    dz = dz_ref[...]
    edge = (dot(dz, wn_ref[...], 1, 1) / deg_ref[...]).astype(BF)
    other_ref[...] = dot(ct2_ref[...], edge).astype(BF)
    mine_ref[...] = dot(ct_ref[verts:, :], edge)
    base_ref[...] = dot(dz, ws_ref[...], 1, 1) + dot(ct_ref[:verts, :], edge)


def half_kernel(keep_ref, got_ref, out_ref):
    out_ref[...] = (keep_ref[...] + got_ref[...].astype(F32)).astype(BF).reshape(out_ref.shape)


def pair_kernel(mine_ref, got_ref, own_ref, s1_ref, s2_ref, s3_ref):
    x = lax.axis_index("x")
    for k, ref in enumerate((own_ref, s1_ref, s2_ref, s3_ref)):
        j = lax.rem(x + k, NX)
        ref[...] = (mine_ref[j] + got_ref[j].astype(F32)).astype(BF)


def join(a, b):
    return jnp.concatenate([a[:, :HUB], b[:, :HUB]], axis=1)


def packs(ref):
    return ref[...].astype(F32).reshape(-1, PACK, ref.shape[-1])


def pack_kernel(got_ref, own_ref, r1_ref, r2_ref, r3_ref, out_ref):
    rows = got_ref.shape[1]
    total = jnp.sum(got_ref[...].astype(F32), axis=0).astype(BF)
    out_ref[:, :rows, :] = jnp.broadcast_to(total[None], (NZ,) + total.shape)
    own, r1, r2, r3 = (packs(r) for r in (own_ref, r1_ref, r2_ref, r3_ref))
    k = iota(own.shape, 1)
    first = jnp.where(k < HUB, own, own + r1 + r2 + r3)
    out_ref[:, rows : rows + PACK, :] = first.astype(BF)
    out_ref[:, rows + PACK : rows + 2 * PACK, :] = join(r1, r2).astype(BF)
    out_ref[:, rows + 2 * PACK :, :] = join(r3, jnp.zeros_like(r3)).astype(BF)


def unpack_kernel(got_ref, out_ref, hub_ref):
    rows = out_ref.shape[1]
    total = jnp.sum(got_ref[:, :rows, :].astype(F32), axis=0).astype(BF)
    out_ref[...] = jnp.broadcast_to(total[None], out_ref.shape)
    hub_ref[...] = jnp.sum(got_ref[:, rows : rows + PACK, :].astype(F32), axis=0).astype(BF)


def grad_kernel(slot_ref, base_ref, sel_ref, got_ref, r1_ref, r2_ref, r3_ref, out_ref):
    verts, width = base_ref.shape
    x = lax.axis_index("x")
    rows = got_ref.shape[1] - 3 * PACK
    block = NZ * PACK
    own = sel_ref[x]
    b1, b2, b3 = (sel_ref[lax.rem(x - k + NX, NX)].astype(F32).reshape(NZ, PACK, verts) for k in (1, 2, 3))
    pair = join(b1, b2).reshape(block, verts).astype(BF)
    last = join(b3, jnp.zeros_like(b3)).reshape(block, verts).astype(BF)
    out = base_ref[...]
    for i, sel in enumerate((own, pair, last)):
        at = rows + i * PACK
        out = out + dot(sel, got_ref[:, at : at + PACK, :].reshape(block, width), 0, 0)
    hub = jnp.zeros((1, width), F32)
    for i, ref in ((3, r1_ref), (2, r2_ref), (1, r3_ref)):
        hub = hub + ref[...].astype(F32)[HUB + i : HUB + i + 1]
    out_ref[...] = out + jnp.where(iota((verts, width), 0) == slot_ref[0], hub, 0.0)


def weight_kernel(mine_ref, other_ref, self_ref, neigh_ref):
    _, c = place()
    first = c == 0
    mine, other = mine_ref[...].astype(F32), other_ref[...].astype(F32)
    self_ref[...] = jnp.where(first, mine, other)
    neigh_ref[...] = jnp.where(first, other, mine)


def swap_core(v):
    return lax.ppermute(v, "c", [(0, 1), (1, 0)])


def shift(v, axis, k):
    return lax.ppermute(v, axis, [(i, (i + k) % 4) for i in range(4)])


def exchange(v, axes):
    return lax.all_to_all(v, axes, split_axis=0, concat_axis=0, tiled=True)


def body(features, w_self, w_neigh, cotangent, neighbours, hub_slots, send_rows, send_counts):
    verts, width = features.shape
    peers, cap = send_rows.shape[1:]
    hubs = 256
    packed = peers * PACK
    table = verts + hubs + peers * cap
    rows = verts + packed

    hub_row = lax.dynamic_slice(features, (hub_slots[0].astype(jnp.uint32), jnp.uint32(0)), (1, width))
    hub_in = [shift(hub_row, "y", k) for k in (1, 2, 3)]
    ct, cm, degree, index, sel = call(
        functools.partial(count_kernel, hubs=hubs, table=table),
        [
            ((rows, verts), BF),
            ((verts, rows), BF),
            ((verts, 1), F32),
            (neighbours.shape[::-1], I32),
            ((packed, verts), BF),
        ],
        "count",
        flops=1 << 28,
        smem=(0,),
    )(hub_slots, neighbours.T, send_rows[0].T, send_counts)
    outgoing = call(outgoing_kernel, [((peers, PACK, width), BF)], "outgoing")(sel, features, *hub_in)[0]
    first = exchange(outgoing, ("x", "z"))
    first_other = swap_core(first)
    ct2, cm2, z_self, s_local = call(
        local_kernel,
        [((packed, verts), BF), ((verts, packed), BF), ((verts, width), F32), ((verts, width), F32)],
        "local",
    )(features, w_self, cm, index)

    hidden, dz, w_send, w_keep = call(
        forward_kernel,
        [((verts, width), BF), ((verts, width), BF), ((width, width), BF), ((width, width), F32)],
        "forward",
    )(features, cotangent, w_neigh, cm, cm2, degree, z_self, s_local, first, first_other)

    w_got = swap_core(w_send)
    base, mine, other = call(
        backward_kernel,
        [((verts, width), F32), ((packed, width), F32), ((packed, width), BF)],
        "backward",
    )(dz, w_neigh, w_self, degree, ct, ct2)

    part = width // (NY * NX)
    other_got = swap_core(other)
    w_keep, mine = lax.optimization_barrier((w_keep, mine))
    blocks = call(half_kernel, [((NY * NX, part, width), BF)], "half")(w_keep, w_got)[0]
    second = exchange(blocks, ("y", "x"))

    split = (NX, NZ * PACK, width)
    b_own, *b_out = call(pair_kernel, [(split[1:], BF)] * 4, "pair")(
        mine.reshape(split), other_got.reshape(split)
    )
    b_in = [shift(b_out[k - 1], "x", k) for k in (1, 2, 3)]
    pack = call(pack_kernel, [((NZ, part + 3 * PACK, width), BF)], "pack")(second, b_own, *b_in)[0]
    third = exchange(pack, "z")
    copies, hub = call(unpack_kernel, [((NY * NX, part, width), BF), ((PACK, width), BF)], "unpack")(third)
    fourth = exchange(copies, ("y", "x")).reshape(width, width)
    hub_back = [shift(hub, "y", k) for k in (1, 2, 3)]
    fourth, hub_back = lax.optimization_barrier((fourth, hub_back))
    grad_features = call(grad_kernel, [((verts, width), F32)], "grad", smem=(0,))(
        hub_slots, base, sel.reshape(NX, NZ * PACK, verts), third, *hub_back
    )[0]
    grad_self, grad_neigh = call(weight_kernel, [((width, width), F32)] * 2, "weights")(fourth, swap_core(fourth))
    return (hidden, grad_features, grad_self, grad_neigh)


def solution(mesh):
    every = ("y", "c", "x", "z")
    fine = Mesh(mesh.devices.reshape(NY, 2, NX, NZ), every)
    vertex = P(every, None)
    return jax.shard_map(
        body,
        mesh=fine,
        in_specs=(vertex, P(), P(), vertex, vertex, P(every), P(every, None, None), vertex),
        out_specs=(vertex, vertex, P(), P()),
        check_vma=False,
    )
```

time: 96.1 us -> 94.6 us (0.984)
  blocking collectives: 49.9 us -> 35.7 us
  waiting for transfers between devices: 5.73 us -> 12.5 us
  starting transfers between devices: 27.8 us -> 33.5 us
    all_to_all x3 -> x2, blocking collectives: 49.9 us -> 35.7 us  [exchange(): return lax.all_to_all(v, axes, split_axis=0, concat_axis=0, tiled=True)]
    all_to_all x0 -> x2, starting transfers between devices: none -> 10 us  [exchange(): return lax.all_to_all(v, axes, split_axis=0, concat_axis=0, tiled=True)]
    ppermute x16 -> x13, waiting for transfers between devices: 5.73 us -> 11 us  [the longest x9 8.28 us: shift(): return lax.ppermute(v, axis, [(i, (i + k) % 4) for i in range(4)])]
    ppermute x16 -> x13, starting transfers between devices: 27.8 us -> 23.4 us  [the longest x9 13.6 us: shift(): return lax.ppermute(v, axis, [(i, (i + k) % 4) for i in range(4)])]
    all_to_all x0 -> x2, waiting for transfers between devices: none -> 1.57 us  [exchange(): return lax.all_to_all(v, axes, split_axis=0, concat_axis=0, tiled=True)]
  transfers between devices with their start and end apart: 16 -> 15, of which waited for: 4 -> 10; matrix products, arithmetic and copies ran while one was open for 0% -> 0% of each run, Pallas kernels for 5% -> 4%
where the time goes in v4:
time: 94.6 us; the launch traced here: 94.1 us
  blocking collectives  35.7 us (38%)
  starting transfers between devices  33.5 us (35%)
  waiting for transfers between devices  12.5 us (13%)
  Pallas kernels  8.91 us (9%)
  local copies, waits for them, and re-layouts  2.13 us (2%)
  between operations  1.36 us (1%)
    all_to_all x2, blocking collectives, exchange(): return lax.all_to_all(v, axes, split_axis=0, concat_axis=0, tiled=True)  35.7 us
    ppermute x9, starting transfers between devices, shift(): return lax.ppermute(v, axis, [(i, (i + k) % 4) for i in range(4)])  13.6 us
    all_to_all x2, starting transfers between devices, exchange(): return lax.all_to_all(v, axes, split_axis=0, concat_axis=0, tiled=True)  10 us
    ppermute x4, starting transfers between devices, swap_core(): return lax.ppermute(v, 'c', [(0, 1), (1, 0)])  9.88 us
    pallas_call x11, Pallas kernels, run(): pl.pallas_call(kernel, out_shape=outs, in_specs=[scalar if i in smem else...  8.91 us
    ppermute x9, waiting for transfers between devices, shift(): return lax.ppermute(v, axis, [(i, (i + k) % 4) for i in range(4)])  8.28 us
    ppermute x4, waiting for transfers between devices, swap_core(): return lax.ppermute(v, 'c', [(0, 1), (1, 0)])  2.68 us
  transfers between devices with their start and end apart: 15, of which 10 were waited for; matrix products, arithmetic and copies ran while one was open for 0% of the time, Pallas kernels for 4%

profile of v4, /device:TPU:1, one launch (start us, length us, event | category | flops | bytes accessed | tf_op | source)
XLA Modules:
  0.0 94.1 jit_solution(14113771143420929514)
XLA Ops:
  2.0 3.6 %collective-permute-start.2 = (bf16[1,512]{1,0:T(2,128)(2,1)S(1)}, bf16[1,512]{1,0:T(2,128)(2,1)S(1)}, u32[]{:S(2)}, u32[]{:S(2)}) collective-permute-start(bf16[1,512]{1,0:T(2,128)(2,1)S(1)} %constant_dynamic-slice_fusion), channel_id=1, source_target_pairs={{0,192},{64,0},{128,64},{192,128},{1,193},{65,1},{129,65},{193,129... | collective-permute-start | bytes 3080 | tf_op jit(solution)/shard_map/ppermute | solution.py:220
  7.2 0.8 copy-done.4
  8.0 1.2 %count.1 = (bf16[512,256]{1,0:T(8,128)(2,1)S(1)}, bf16[256,512]{1,0:T(8,128)(2,1)S(1)}, f32[256,1]{1,0:T(8,128)S(1)}, s32[32,256]{1,0:T(8,128)S(1)}, bf16[256,256]{1,0:T(8,128)(2,1)S(1)}) custom-call(s32[1]{0:T(128)S(6)} %copy.12.slot_ref, s32[32,256]{1,0:T(8,128)S(1)} %bitcast.14, s32[4,32]{1,0:T(4,128)S(1)} %bitcast.15, s32[1,32]{1,0:T(1,128)S(1)} %copy-done.6), custom_call_target="tpu_custom_call" | custom-call | flops 268435456 | bytes 1048576 | tf_op jit(solution)/shard_map/count/pallas_call | solution.py:30
  9.8 20.5 %all_to_all.20.got_ref = bf16[32,8,512]{2,1,0:T(8,128)(2,1)S(1)} all-to-all(bf16[32,8,512]{2,1,0:T(8,128)(2,1)S(1)} %outgoing.1), channel_id=1, replica_groups=mesh['y'=4,'c'=2,'x'=4,'z'=8] {'x','z'}, dimensions={0} | all-to-all | bytes 524288 | tf_op jit(solution)/shard_map/all_to_all | solution.py:224
  30.3 4.5 %collective-permute-start.3 = (bf16[32,8,512]{2,1,0:T(8,128)(2,1)S(1)}, bf16[32,8,512]{2,1,0:T(8,128)(2,1)S(1)}, u32[]{:S(2)}, u32[]{:S(2)}) collective-permute-start(bf16[32,8,512]{2,1,0:T(8,128)(2,1)S(1)} %all_to_all.20.got_ref), channel_id=1, source_target_pairs={{0,32},{32,0},{1,33},{33,1},{2,34},{34,2},{3,35},{35,3},{4,36},{36... | collective-permute-start | bytes 786440 | tf_op jit(solution)/shard_map/ppermute | solution.py:216
  36.0 1.4 %forward.1 = (bf16[256,512]{1,0:T(8,128)(2,1)}, bf16[256,512]{1,0:T(8,128)(2,1)S(1)}, bf16[512,512]{1,0:T(8,128)(2,1)S(1)}, f32[512,512]{1,0:T(8,128)S(1)}) custom-call(bf16[256,512]{1,0:T(8,128)(2,1)S(1)} %copy-done, bf16[256,512]{1,0:T(8,128)(2,1)S(1)} %copy-done.3, bf16[512,512]{1,0:T(8,128)(2,1)S(1)} %copy-done.2, ...), custom_call_target="tpu_custom_call" | custom-call | flops 4194304 | bytes 1048576 | tf_op jit(solution)/shard_map/forward/pallas_call | solution.py:30
  37.7 0.8 backward.1
  39.3 0.9 half.1
  40.2 3.6 %all-to-all-start.1 = ((bf16[16,32,512]{2,1,0:T(8,128)(2,1)}), bf16[16,32,512]{2,1,0:T(8,128)(2,1)S(1)}, u32[]{:S(2)}, u32[]{:S(2)}) async-start(bf16[16,32,512]{2,1,0:T(8,128)(2,1)} %half.1), calls=%async_computation.1 | async-start | bytes 1048576 | tf_op jit(solution)/shard_map/all_to_all | solution.py:224
  44.6 1.2 %collective-permute-done.5 = bf16[256,512]{1,0:T(8,128)(2,1)S(1)} collective-permute-done((bf16[256,512]{1,0:T(8,128)(2,1)S(1)}, bf16[256,512]{1,0:T(8,128)(2,1)S(1)}, u32[]{:S(2)}, u32[]{:S(2)}) %collective-permute-start.5) | collective-permute-done | bytes 262176 | tf_op jit(solution)/shard_map/ppermute | solution.py:216
  45.8 1.6 %collective-permute-start.6 = (bf16[64,512]{1,0:T(8,128)(2,1)S(1)}, bf16[64,512]{1,0:T(8,128)(2,1)S(1)}, u32[]{:S(2)}, u32[]{:S(2)}) collective-permute-start(bf16[64,512]{1,0:T(8,128)(2,1)S(1)} %get-tuple-element.53), channel_id=1, source_target_pairs={{0,8},{8,16},{16,24},{24,0},{1,9},{9,17},{17,25},{25,1},{2,10},{10... | collective-permute-start | bytes 196616 | tf_op jit(solution)/shard_map/ppermute | solution.py:220
  47.4 2.4 %collective-permute-start.7 = (bf16[64,512]{1,0:T(8,128)(2,1)S(1)}, bf16[64,512]{1,0:T(8,128)(2,1)S(1)}, u32[]{:S(2)}, u32[]{:S(2)}) collective-permute-start(bf16[64,512]{1,0:T(8,128)(2,1)S(1)} %get-tuple-element.54), channel_id=1, source_target_pairs={{0,16},{8,24},{16,0},{24,8},{1,17},{9,25},{17,1},{25,9},{2,18},{10... | collective-permute-start | bytes 196616 | tf_op jit(solution)/shard_map/ppermute | solution.py:220
  49.8 1.2 %collective-permute-start.8 = (bf16[64,512]{1,0:T(8,128)(2,1)S(1)}, bf16[64,512]{1,0:T(8,128)(2,1)S(1)}, u32[]{:S(2)}, u32[]{:S(2)}) collective-permute-start(bf16[64,512]{1,0:T(8,128)(2,1)S(1)} %get-tuple-element.55), channel_id=1, source_target_pairs={{0,24},{8,0},{16,8},{24,16},{1,25},{9,1},{17,9},{25,17},{2,26},{10... | collective-permute-start | bytes 196616 | tf_op jit(solution)/shard_map/ppermute | solution.py:220
  51.0 3.1 %collective-permute-done.6.r1_ref = bf16[64,512]{1,0:T(8,128)(2,1)S(1)} collective-permute-done((bf16[64,512]{1,0:T(8,128)(2,1)S(1)}, bf16[64,512]{1,0:T(8,128)(2,1)S(1)}, u32[]{:S(2)}, u32[]{:S(2)}) %collective-permute-start.6) | collective-permute-done | bytes 65568 | tf_op jit(solution)/shard_map/ppermute | solution.py:220
  54.1 1.1 %collective-permute-done.7.r2_ref = bf16[64,512]{1,0:T(8,128)(2,1)S(1)} collective-permute-done((bf16[64,512]{1,0:T(8,128)(2,1)S(1)}, bf16[64,512]{1,0:T(8,128)(2,1)S(1)}, u32[]{:S(2)}, u32[]{:S(2)}) %collective-permute-start.7) | collective-permute-done | bytes 65568 | tf_op jit(solution)/shard_map/ppermute | solution.py:220
  55.4 15.2 %all_to_all.21.got_ref = bf16[8,56,512]{2,1,0:T(8,128)(2,1)S(1)} all-to-all(bf16[8,56,512]{2,1,0:T(8,128)(2,1)S(1)} %pack.1), channel_id=1, replica_groups=mesh['y'=4,'c'=2,'x'=4,'z'=8] {'z'}, dimensions={0} | all-to-all | bytes 917504 | tf_op jit(solution)/shard_map/all_to_all | solution.py:224
  70.5 0.9 unpack.1
  71.4 6.4 %all-to-all-start.3 = ((bf16[16,32,512]{2,1,0:T(8,128)(2,1)}), bf16[16,32,512]{2,1,0:T(8,128)(2,1)S(1)}, u32[]{:S(2)}, u32[]{:S(2)}) async-start(bf16[16,32,512]{2,1,0:T(8,128)(2,1)} %get-tuple-element.56), calls=%async_computation.3 | async-start | bytes 1048576 | tf_op jit(solution)/shard_map/all_to_all | solution.py:224
  77.8 2.6 %collective-permute-start.11 = (bf16[8,512]{1,0:T(8,128)(2,1)S(1)}, bf16[8,512]{1,0:T(8,128)(2,1)S(1)}, u32[]{:S(2)}, u32[]{:S(2)}) collective-permute-start(bf16[8,512]{1,0:T(8,128)(2,1)S(1)} %get-tuple-element.57), channel_id=1, source_target_pairs={{0,192},{64,0},{128,64},{192,128},{1,193},{65,1},{129,65},{193,129... | collective-permute-start | bytes 24584 | tf_op jit(solution)/shard_map/ppermute | solution.py:220
  81.6 3.7 %collective-permute-done.10.r2_ref = bf16[8,512]{1,0:T(8,128)(2,1)S(1)} collective-permute-done((bf16[8,512]{1,0:T(8,128)(2,1)S(1)}, bf16[8,512]{1,0:T(8,128)(2,1)S(1)}, u32[]{:S(2)}, u32[]{:S(2)}) %collective-permute-start.10) | collective-permute-done | bytes 8224 | tf_op jit(solution)/shard_map/ppermute | solution.py:220
  85.2 1.6 %all-to-all-done.3 = bf16[16,32,512]{2,1,0:T(8,128)(2,1)S(1)} async-done(((bf16[16,32,512]{2,1,0:T(8,128)(2,1)}), bf16[16,32,512]{2,1,0:T(8,128)(2,1)S(1)}, u32[]{:S(2)}, u32[]{:S(2)}) %all-to-all-start.3) | async-done | bytes 524320 | tf_op jit(solution)/shard_map/all_to_all | solution.py:224
  86.8 4.2 %collective-permute-start.12 = (bf16[512,512]{1,0:T(8,128)(2,1)S(1)}, bf16[512,512]{1,0:T(8,128)(2,1)S(1)}, u32[]{:S(2)}, u32[]{:S(2)}) collective-permute-start(bf16[512,512]{1,0:T(8,128)(2,1)S(1)} %bitcast.9), channel_id=1, source_target_pairs={{0,32},{32,0},{1,33},{33,1},{2,34},{34,2},{3,35},{35,3},{4,36},{36... | collective-permute-start | bytes 1572872 | tf_op jit(solution)/shard_map/ppermute | solution.py:216
  91.1 1.2 %grad.1 = f32[256,512]{1,0:T(8,128)} custom-call(s32[1]{0:T(128)S(6)} %copy.12.slot_ref, f32[256,512]{1,0:T(8,128)S(1)} %get-tuple-element.45.base_ref, bf16[4,64,256]{2,1,0:T(8,128)(2,1)S(1)} %bitcast.11, bf16[8,56,512]{2,1,0:T(8,128)(2,1)S(1)} %all_to_all.21.got_ref, bf16[8,512]{1,0:T(8,128)(2,1)S(1)} %collective-permute-done.9.r1_ref, ...), custom_call_target="tpu_custom_call" | custom-call | flops 4194304 | bytes 1048576 | tf_op jit(solution)/shard_map/grad/pallas_call | solution.py:30
  92.6 1.5 %weights.1 = (f32[512,512]{1,0:T(8,128)}, f32[512,512]{1,0:T(8,128)}) custom-call(bf16[512,512]{1,0:T(8,128)(2,1)S(1)} %bitcast.10, bf16[512,512]{1,0:T(8,128)(2,1)S(1)} %collective-permute-done.12.other_ref), custom_call_target="tpu_custom_call" | custom-call | flops 4194304 | bytes 1048576 | tf_op jit(solution)/shard_map/weights/pallas_call | solution.py:30
  (34 shorter events, 7.7 us)
Async XLA Ops:
  2.0 4.6 %copy-start.5 = (s32[1,32,4]{1,2,0:T(4,128)S(1)}, s32[1,32,4]{1,2,0:T(4,128)}, u32[]{:S(2)}) copy-start(s32[1,32,4]{1,2,0:T(4,128)} %param.14) | copy-start | bytes 1540
  2.0 7.2 %collective-permute-start.2 = (bf16[1,512]{1,0:T(2,128)(2,1)S(1)}, bf16[1,512]{1,0:T(2,128)(2,1)S(1)}, u32[]{:S(2)}, u32[]{:S(2)}) collective-permute-start(bf16[1,512]{1,0:T(2,128)(2,1)S(1)} %constant_dynamic-slice_fusion), channel_id=1, source_target_pairs={{0,192},{64,0},{128,64},{192,128},{1,193},{65,1},{129,65},{193,129... | collective-permute-start | bytes 3080 | tf_op jit(solution)/shard_map/ppermute | solution.py:220
  5.5 3.9 %collective-permute-start.1 = (bf16[1,512]{1,0:T(2,128)(2,1)S(1)}, bf16[1,512]{1,0:T(2,128)(2,1)S(1)}, u32[]{:S(2)}, u32[]{:S(2)}) collective-permute-start(bf16[1,512]{1,0:T(2,128)(2,1)S(1)} %constant_dynamic-slice_fusion), channel_id=1, source_target_pairs={{0,128},{64,192},{128,0},{192,64},{1,129},{65,193},{129,1},{193,65... | collective-permute-start | bytes 3080 | tf_op jit(solution)/shard_map/ppermute | solution.py:220
  5.9 3.6 %collective-permute-start = (bf16[1,512]{1,0:T(2,128)(2,1)S(1)}, bf16[1,512]{1,0:T(2,128)(2,1)S(1)}, u32[]{:S(2)}, u32[]{:S(2)}) collective-permute-start(bf16[1,512]{1,0:T(2,128)(2,1)S(1)} %constant_dynamic-slice_fusion), channel_id=1, source_target_pairs={{0,64},{64,128},{128,192},{192,0},{1,65},{65,129},{129,193},{193,1... | collective-permute-start | bytes 3080 | tf_op jit(solution)/shard_map/ppermute | solution.py:220
  6.6 0.7 copy-start.6
  7.2 0.8 copy-start.4
  8.0 1.5 %copy-start = (bf16[256,512]{1,0:T(8,128)(2,1)S(1)}, bf16[256,512]{1,0:T(8,128)(2,1)}, u32[]{:S(2)}) copy-start(bf16[256,512]{1,0:T(8,128)(2,1)} %feat_ref.5) | copy-start | bytes 786436
  9.5 25.3 %copy-start.1 = (bf16[512,512]{1,0:T(8,128)(2,1)S(1)}, bf16[512,512]{1,0:T(8,128)(2,1)}, u32[]{:S(2)}) copy-start(bf16[512,512]{1,0:T(8,128)(2,1)} %ws_ref.3) | copy-start | bytes 1572868
  30.3 5.7 %collective-permute-start.3 = (bf16[32,8,512]{2,1,0:T(8,128)(2,1)S(1)}, bf16[32,8,512]{2,1,0:T(8,128)(2,1)S(1)}, u32[]{:S(2)}, u32[]{:S(2)}) collective-permute-start(bf16[32,8,512]{2,1,0:T(8,128)(2,1)S(1)} %all_to_all.20.got_ref), channel_id=1, source_target_pairs={{0,32},{32,0},{1,33},{33,1},{2,34},{34,2},{3,35},{35,3},{4,36},{36... | collective-permute-start | bytes 786440 | tf_op jit(solution)/shard_map/ppermute | solution.py:216
  34.8 1.2 %copy-start.2 = (bf16[512,512]{1,0:T(8,128)(2,1)S(1)}, bf16[512,512]{1,0:T(8,128)(2,1)}, u32[]{:S(2)}) copy-start(bf16[512,512]{1,0:T(8,128)(2,1)} %wn_ref.3) | copy-start | bytes 1572868
  34.8 1.2 %copy-start.3 = (bf16[256,512]{1,0:T(8,128)(2,1)S(1)}, bf16[256,512]{1,0:T(8,128)(2,1)}, u32[]{:S(2)}) copy-start(bf16[256,512]{1,0:T(8,128)(2,1)} %cot_ref.1) | copy-start | bytes 786436
  37.4 1.9 %collective-permute-start.4 = (bf16[512,512]{1,0:T(8,128)(2,1)S(1)}, bf16[512,512]{1,0:T(8,128)(2,1)S(1)}, u32[]{:S(2)}, u32[]{:S(2)}) collective-permute-start(bf16[512,512]{1,0:T(8,128)(2,1)S(1)} %get-tuple-element.49), channel_id=1, source_target_pairs={{0,32},{32,0},{1,33},{33,1},{2,34},{34,2},{3,35},{35,3},{4,36},{36... | collective-permute-start | bytes 1572872 | tf_op jit(solution)/shard_map/ppermute | solution.py:216
  40.2 15.1 %all-to-all-start.1 = ((bf16[16,32,512]{2,1,0:T(8,128)(2,1)}), bf16[16,32,512]{2,1,0:T(8,128)(2,1)S(1)}, u32[]{:S(2)}, u32[]{:S(2)}) async-start(bf16[16,32,512]{2,1,0:T(8,128)(2,1)} %half.1), calls=%async_computation.1 | async-start | bytes 1048576 | tf_op jit(solution)/shard_map/all_to_all | solution.py:224
  43.8 1.9 %collective-permute-start.5 = (bf16[256,512]{1,0:T(8,128)(2,1)S(1)}, bf16[256,512]{1,0:T(8,128)(2,1)S(1)}, u32[]{:S(2)}, u32[]{:S(2)}) collective-permute-start(bf16[256,512]{1,0:T(8,128)(2,1)S(1)} %get-tuple-element.51), channel_id=1, source_target_pairs={{0,32},{32,0},{1,33},{33,1},{2,34},{34,2},{3,35},{35,3},{4,36},{36... | collective-permute-start | bytes 786440 | tf_op jit(solution)/shard_map/ppermute | solution.py:216
  45.8 8.3 %collective-permute-start.6 = (bf16[64,512]{1,0:T(8,128)(2,1)S(1)}, bf16[64,512]{1,0:T(8,128)(2,1)S(1)}, u32[]{:S(2)}, u32[]{:S(2)}) collective-permute-start(bf16[64,512]{1,0:T(8,128)(2,1)S(1)} %get-tuple-element.53), channel_id=1, source_target_pairs={{0,8},{8,16},{16,24},{24,0},{1,9},{9,17},{17,25},{25,1},{2,10},{10... | collective-permute-start | bytes 196616 | tf_op jit(solution)/shard_map/ppermute | solution.py:220
  47.4 7.8 %collective-permute-start.7 = (bf16[64,512]{1,0:T(8,128)(2,1)S(1)}, bf16[64,512]{1,0:T(8,128)(2,1)S(1)}, u32[]{:S(2)}, u32[]{:S(2)}) collective-permute-start(bf16[64,512]{1,0:T(8,128)(2,1)S(1)} %get-tuple-element.54), channel_id=1, source_target_pairs={{0,16},{8,24},{16,0},{24,8},{1,17},{9,25},{17,1},{25,9},{2,18},{10... | collective-permute-start | bytes 196616 | tf_op jit(solution)/shard_map/ppermute | solution.py:220
  49.8 5.4 %collective-permute-start.8 = (bf16[64,512]{1,0:T(8,128)(2,1)S(1)}, bf16[64,512]{1,0:T(8,128)(2,1)S(1)}, u32[]{:S(2)}, u32[]{:S(2)}) collective-permute-start(bf16[64,512]{1,0:T(8,128)(2,1)S(1)} %get-tuple-element.55), channel_id=1, source_target_pairs={{0,24},{8,0},{16,8},{24,16},{1,25},{9,1},{17,9},{25,17},{2,26},{10... | collective-permute-start | bytes 196616 | tf_op jit(solution)/shard_map/ppermute | solution.py:220
  71.4 15.4 %all-to-all-start.3 = ((bf16[16,32,512]{2,1,0:T(8,128)(2,1)}), bf16[16,32,512]{2,1,0:T(8,128)(2,1)S(1)}, u32[]{:S(2)}, u32[]{:S(2)}) async-start(bf16[16,32,512]{2,1,0:T(8,128)(2,1)} %get-tuple-element.56), calls=%async_computation.3 | async-start | bytes 1048576 | tf_op jit(solution)/shard_map/all_to_all | solution.py:224
  77.8 3.7 %collective-permute-start.11 = (bf16[8,512]{1,0:T(8,128)(2,1)S(1)}, bf16[8,512]{1,0:T(8,128)(2,1)S(1)}, u32[]{:S(2)}, u32[]{:S(2)}) collective-permute-start(bf16[8,512]{1,0:T(8,128)(2,1)S(1)} %get-tuple-element.57), channel_id=1, source_target_pairs={{0,192},{64,0},{128,64},{192,128},{1,193},{65,1},{129,65},{193,129... | collective-permute-start | bytes 24584 | tf_op jit(solution)/shard_map/ppermute | solution.py:220
  80.4 4.9 %collective-permute-start.10 = (bf16[8,512]{1,0:T(8,128)(2,1)S(1)}, bf16[8,512]{1,0:T(8,128)(2,1)S(1)}, u32[]{:S(2)}, u32[]{:S(2)}) collective-permute-start(bf16[8,512]{1,0:T(8,128)(2,1)S(1)} %get-tuple-element.57), channel_id=1, source_target_pairs={{0,128},{64,192},{128,0},{192,64},{1,129},{65,193},{129,1},{193,65... | collective-permute-start | bytes 24584 | tf_op jit(solution)/shard_map/ppermute | solution.py:220
  81.0 4.3 %collective-permute-start.9 = (bf16[8,512]{1,0:T(8,128)(2,1)S(1)}, bf16[8,512]{1,0:T(8,128)(2,1)S(1)}, u32[]{:S(2)}, u32[]{:S(2)}) collective-permute-start(bf16[8,512]{1,0:T(8,128)(2,1)S(1)} %get-tuple-element.57), channel_id=1, source_target_pairs={{0,64},{64,128},{128,192},{192,0},{1,65},{65,129},{129,193},{193,1... | collective-permute-start | bytes 24584 | tf_op jit(solution)/shard_map/ppermute | solution.py:220
  86.8 5.8 %collective-permute-start.12 = (bf16[512,512]{1,0:T(8,128)(2,1)S(1)}, bf16[512,512]{1,0:T(8,128)(2,1)S(1)}, u32[]{:S(2)}, u32[]{:S(2)}) collective-permute-start(bf16[512,512]{1,0:T(8,128)(2,1)S(1)} %bitcast.9), channel_id=1, source_target_pairs={{0,32},{32,0},{1,33},{33,1},{2,34},{34,2},{3,35},{35,3},{4,36},{36... | collective-permute-start | bytes 1572872 | tf_op jit(solution)/shard_map/ppermute | solution.py:216

commit v5 on v4

--- a/solution.py
+++ b/solution.py
@@ -50,8 +50,20 @@
     return lax.broadcasted_iota(I32, shape, dim)
 
 
-def outgoing_kernel(sel_ref, feat_ref, r1_ref, r2_ref, r3_ref, out_ref):
-    rows = dot(sel_ref[...], feat_ref[...])
+def outgoing_kernel(slot_ref, route_ref, count_ref, feat_ref, r1_ref, r2_ref, r3_ref, out_ref, sel_ref):
+    packed, verts = sel_ref.shape
+    cap, peers = route_ref.shape
+    live = iota((cap, peers), 0) < count_ref[...]
+    routes = jnp.where(live, route_ref[...], -1).astype(F32).astype(BF)
+    owner = (iota((packed, peers), 0) // PACK == iota((packed, peers), 1)).astype(BF)
+    every = dot(owner, routes, 1, 1)
+    k = lax.rem(iota((packed, cap), 0), PACK)
+    pick = jnp.sum(jnp.where(k == iota((packed, cap), 1), every, 0.0), axis=1, keepdims=True).astype(I32)
+    k = lax.rem(iota((packed, 1), 0), PACK)
+    pick = jnp.where(k < cap, pick, jnp.where(k == HUB, slot_ref[0], -1))
+    sel = (pick == iota((packed, verts), 1)).astype(BF)
+    sel_ref[...] = sel
+    rows = dot(sel, feat_ref[...])
     k = lax.rem(iota(rows.shape, 0), PACK)
     for i, ref in ((1, r1_ref), (2, r2_ref), (3, r3_ref)):
         rows = jnp.where(k == HUB + i, ref[...].astype(F32)[:1], rows)
@@ -81,19 +93,8 @@
     return acc
 
 
-def count_kernel(slot_ref, nbt_ref, route_ref, count_ref, ct_ref, c_ref, deg_ref, index_ref, sel_ref, *, hubs, table):
-    packed, verts = sel_ref.shape
-    cap, peers = route_ref.shape
-    live = iota((cap, peers), 0) < count_ref[...]
-    routes = jnp.where(live, route_ref[...], -1).astype(F32).astype(BF)
-    owner = (iota((packed, peers), 0) // PACK == iota((packed, peers), 1)).astype(BF)
-    every = dot(owner, routes, 1, 1)
-    k = lax.rem(iota((packed, cap), 0), PACK)
-    pick = jnp.sum(jnp.where(k == iota((packed, cap), 1), every, 0.0), axis=1, keepdims=True).astype(I32)
-    k = lax.rem(iota((packed, 1), 0), PACK)
-    pick = jnp.where(k < cap, pick, jnp.where(k == HUB, slot_ref[0], -1))
-    sel_ref[...] = (pick == iota((packed, verts), 1)).astype(BF)
-
+def count_kernel(nbt_ref, ct_ref, c_ref, deg_ref, index_ref, *, packed, hubs, table):
+    verts = nbt_ref.shape[1]
     nbt = nbt_ref[...]
     degree = jnp.sum((nbt < table).astype(F32), axis=0, keepdims=True)
     deg_ref[...] = jnp.broadcast_to(degree, (8, verts)).T[:, :1]
@@ -204,12 +205,26 @@
     out_ref[...] = out + jnp.where(iota((verts, width), 0) == slot_ref[0], hub, 0.0)
 
 
-def weight_kernel(mine_ref, other_ref, self_ref, neigh_ref):
+def weight_kernel(*refs, own):
+    got_ref = refs[0]
+    self_ref, neigh_ref, buf, sem = refs[1 if own else 3 :]
     _, c = place()
-    first = c == 0
-    mine, other = mine_ref[...].astype(F32), other_ref[...].astype(F32)
-    self_ref[...] = jnp.where(first, mine, other)
-    neigh_ref[...] = jnp.where(first, other, mine)
+    half = got_ref.shape[0] // 2
+    to_self = (c == 0) if own else (c != 0)
+
+    def write(ref):
+        copies = []
+        for i in range(2):
+            rows = pl.ds(i * half, half)
+            buf[rows, :] = got_ref[rows, :].astype(F32)
+            copy = pltpu.make_async_copy(buf.at[rows, :], ref.at[rows, :], sem.at[i])
+            copy.start()
+            copies.append(copy)
+        for copy in copies:
+            copy.wait()
+
+    pl.when(to_self)(lambda: write(self_ref))
+    pl.when(jnp.logical_not(to_self))(lambda: write(neigh_ref))
 
 
 def swap_core(v):
@@ -234,20 +249,16 @@
 
     hub_row = lax.dynamic_slice(features, (hub_slots[0].astype(jnp.uint32), jnp.uint32(0)), (1, width))
     hub_in = [shift(hub_row, "y", k) for k in (1, 2, 3)]
-    ct, cm, degree, index, sel = call(
-        functools.partial(count_kernel, hubs=hubs, table=table),
-        [
-            ((rows, verts), BF),
-            ((verts, rows), BF),
-            ((verts, 1), F32),
-            (neighbours.shape[::-1], I32),
-            ((packed, verts), BF),
-        ],
+    ct, cm, degree, index = call(
+        functools.partial(count_kernel, packed=packed, hubs=hubs, table=table),
+        [((rows, verts), BF), ((verts, rows), BF), ((verts, 1), F32), (neighbours.shape[::-1], I32)],
         "count",
         flops=1 << 28,
-        smem=(0,),
-    )(hub_slots, neighbours.T, send_rows[0].T, send_counts)
-    outgoing = call(outgoing_kernel, [((peers, PACK, width), BF)], "outgoing")(sel, features, *hub_in)[0]
+    )(neighbours.T)
+    hub_in, ct, cm = lax.optimization_barrier((hub_in, ct, cm))
+    outgoing, sel = call(
+        outgoing_kernel, [((peers, PACK, width), BF), ((packed, verts), BF)], "outgoing", smem=(0,)
+    )(hub_slots, send_rows[0].T, send_counts, features, *hub_in)
     first = exchange(outgoing, ("x", "z"))
     first_other = swap_core(first)
     ct2, cm2, z_self, s_local = call(
@@ -285,11 +296,20 @@
     copies, hub = call(unpack_kernel, [((NY * NX, part, width), BF), ((PACK, width), BF)], "unpack")(third)
     fourth = exchange(copies, ("y", "x")).reshape(width, width)
     hub_back = [shift(hub, "y", k) for k in (1, 2, 3)]
-    fourth, hub_back = lax.optimization_barrier((fourth, hub_back))
     grad_features = call(grad_kernel, [((verts, width), F32)], "grad", smem=(0,))(
         hub_slots, base, sel.reshape(NX, NZ * PACK, verts), third, *hub_back
     )[0]
-    grad_self, grad_neigh = call(weight_kernel, [((width, width), F32)] * 2, "weights")(fourth, swap_core(fourth))
+    fourth, grad_features = lax.optimization_barrier((fourth, grad_features))
+    other = swap_core(fourth)
+    scratch = (pltpu.VMEM((width, width), F32), pltpu.SemaphoreType.DMA((2,)))
+    shapes = [((width, width), F32)] * 2
+    partial = call(
+        functools.partial(weight_kernel, own=True), shapes, "mine", hbm_out=True, scratch=scratch
+    )(fourth)
+    grad_self, grad_neigh = call(
+        functools.partial(weight_kernel, own=False), shapes, "other", hbm=(1, 2), hbm_out=True, scratch=scratch,
+        alias={1: 0, 2: 1},
+    )(other, *partial)
     return (hidden, grad_features, grad_self, grad_neigh)
 
 

time: 94.6 us -> 94.5 us (level)
    all_to_all x2, waiting for transfers between devices: 1.57 us -> 0.38 us  [exchange(): return lax.all_to_all(v, axes, split_axis=0, concat_axis=0, tiled=True)]
    pallas_call x11 -> x12, Pallas kernels: 8.91 us -> 9.58 us  [run(): pl.pallas_call(kernel, out_shape=outs, in_specs=[scalar if i in smem else...]
  transfers between devices with their start and end apart: 15 -> 15, of which waited for: 10 -> 10; matrix products, arithmetic and copies ran while one was open for 0% -> 0% of each run, Pallas kernels for 4% -> 5%
where the time goes in v5:
time: 94.5 us; the launch traced here: 94 us
  blocking collectives  35.7 us (38%)
  starting transfers between devices  33.7 us (36%)
  waiting for transfers between devices  12.2 us (13%)
  Pallas kernels  9.58 us (10%)
  local copies, waits for them, and re-layouts  1.49 us (2%)
  between operations  1.37 us (1%)
    all_to_all x2, blocking collectives, exchange(): return lax.all_to_all(v, axes, split_axis=0, concat_axis=0, tiled=True)  35.7 us
    ppermute x9, starting transfers between devices, shift(): return lax.ppermute(v, axis, [(i, (i + k) % 4) for i in range(4)])  13.6 us
    ppermute x4, starting transfers between devices, swap_core(): return lax.ppermute(v, 'c', [(0, 1), (1, 0)])  10.1 us
    all_to_all x2, starting transfers between devices, exchange(): return lax.all_to_all(v, axes, split_axis=0, concat_axis=0, tiled=True)  10 us
    pallas_call x12, Pallas kernels, run(): pl.pallas_call(kernel, out_shape=outs, in_specs=[scalar if i in smem else...  9.58 us
    ppermute x9, waiting for transfers between devices, shift(): return lax.ppermute(v, axis, [(i, (i + k) % 4) for i in range(4)])  9.02 us
    ppermute x4, waiting for transfers between devices, swap_core(): return lax.ppermute(v, 'c', [(0, 1), (1, 0)])  2.85 us
  transfers between devices with their start and end apart: 15, of which 10 were waited for; matrix products, arithmetic and copies ran while one was open for 0% of the time, Pallas kernels for 5%

profile of v5, /device:TPU:1, one launch (start us, length us, event | category | flops | bytes accessed | tf_op | source)
XLA Modules:
  0.0 94.0 jit_solution(3955234434281637025)
XLA Ops:
  2.0 3.6 %collective-permute-start.2 = (bf16[1,512]{1,0:T(2,128)(2,1)S(1)}, bf16[1,512]{1,0:T(2,128)(2,1)S(1)}, u32[]{:S(2)}, u32[]{:S(2)}) collective-permute-start(bf16[1,512]{1,0:T(2,128)(2,1)S(1)} %constant_dynamic-slice_fusion), channel_id=1, source_target_pairs={{0,192},{64,0},{128,64},{192,128},{1,193},{65,1},{129,65},{193,129... | collective-permute-start | bytes 3080 | tf_op jit(solution)/shard_map/ppermute | solution.py:235
  7.4 1.1 %count.1 = (bf16[512,256]{1,0:T(8,128)(2,1)S(1)}, bf16[256,512]{1,0:T(8,128)(2,1)S(1)}, f32[256,1]{1,0:T(8,128)S(1)}, s32[32,256]{1,0:T(8,128)S(1)}) custom-call(s32[32,256]{1,0:T(8,128)S(1)} %bitcast.15), custom_call_target="tpu_custom_call" | custom-call | flops 268435456 | bytes 1048576 | tf_op jit(solution)/shard_map/count/pallas_call | solution.py:30
  8.5 1.0 %collective-permute-done.1.r2_ref = bf16[1,512]{1,0:T(2,128)(2,1)S(1)} collective-permute-done((bf16[1,512]{1,0:T(2,128)(2,1)S(1)}, bf16[1,512]{1,0:T(2,128)(2,1)S(1)}, u32[]{:S(2)}, u32[]{:S(2)}) %collective-permute-start.1) | collective-permute-done | bytes 1056 | tf_op jit(solution)/shard_map/ppermute | solution.py:235
  10.0 20.5 %all_to_all.20.got_ref = bf16[32,8,512]{2,1,0:T(8,128)(2,1)S(1)} all-to-all(bf16[32,8,512]{2,1,0:T(8,128)(2,1)S(1)} %get-tuple-element.51), channel_id=1, replica_groups=mesh['y'=4,'c'=2,'x'=4,'z'=8] {'x','z'}, dimensions={0} | all-to-all | bytes 524288 | tf_op jit(solution)/shard_map/all_to_all | solution.py:239
  30.5 4.5 %collective-permute-start.3 = (bf16[32,8,512]{2,1,0:T(8,128)(2,1)S(1)}, bf16[32,8,512]{2,1,0:T(8,128)(2,1)S(1)}, u32[]{:S(2)}, u32[]{:S(2)}) collective-permute-start(bf16[32,8,512]{2,1,0:T(8,128)(2,1)S(1)} %all_to_all.20.got_ref), channel_id=1, source_target_pairs={{0,32},{32,0},{1,33},{33,1},{2,34},{34,2},{3,35},{35,3},{4,36},{36... | collective-permute-start | bytes 786440 | tf_op jit(solution)/shard_map/ppermute | solution.py:231
  36.2 1.4 %forward.1 = (bf16[256,512]{1,0:T(8,128)(2,1)}, bf16[256,512]{1,0:T(8,128)(2,1)S(1)}, bf16[512,512]{1,0:T(8,128)(2,1)S(1)}, f32[512,512]{1,0:T(8,128)S(1)}) custom-call(bf16[256,512]{1,0:T(8,128)(2,1)S(1)} %copy-done, bf16[256,512]{1,0:T(8,128)(2,1)S(1)} %copy-done.3, bf16[512,512]{1,0:T(8,128)(2,1)S(1)} %copy-done.2, ...), custom_call_target="tpu_custom_call" | custom-call | flops 4194304 | bytes 1048576 | tf_op jit(solution)/shard_map/forward/pallas_call | solution.py:30
  37.9 0.8 backward.1
  39.5 0.9 half.1
  40.4 3.6 %all-to-all-start.1 = ((bf16[16,32,512]{2,1,0:T(8,128)(2,1)}), bf16[16,32,512]{2,1,0:T(8,128)(2,1)S(1)}, u32[]{:S(2)}, u32[]{:S(2)}) async-start(bf16[16,32,512]{2,1,0:T(8,128)(2,1)} %half.1), calls=%async_computation.1 | async-start | bytes 1048576 | tf_op jit(solution)/shard_map/all_to_all | solution.py:239
  44.7 1.2 %collective-permute-done.5 = bf16[256,512]{1,0:T(8,128)(2,1)S(1)} collective-permute-done((bf16[256,512]{1,0:T(8,128)(2,1)S(1)}, bf16[256,512]{1,0:T(8,128)(2,1)S(1)}, u32[]{:S(2)}, u32[]{:S(2)}) %collective-permute-start.5) | collective-permute-done | bytes 262176 | tf_op jit(solution)/shard_map/ppermute | solution.py:231
  46.0 1.6 %collective-permute-start.6 = (bf16[64,512]{1,0:T(8,128)(2,1)S(1)}, bf16[64,512]{1,0:T(8,128)(2,1)S(1)}, u32[]{:S(2)}, u32[]{:S(2)}) collective-permute-start(bf16[64,512]{1,0:T(8,128)(2,1)S(1)} %get-tuple-element.63), channel_id=1, source_target_pairs={{0,8},{8,16},{16,24},{24,0},{1,9},{9,17},{17,25},{25,1},{2,10},{10... | collective-permute-start | bytes 196616 | tf_op jit(solution)/shard_map/ppermute | solution.py:235
  47.6 2.4 %collective-permute-start.7 = (bf16[64,512]{1,0:T(8,128)(2,1)S(1)}, bf16[64,512]{1,0:T(8,128)(2,1)S(1)}, u32[]{:S(2)}, u32[]{:S(2)}) collective-permute-start(bf16[64,512]{1,0:T(8,128)(2,1)S(1)} %get-tuple-element.64), channel_id=1, source_target_pairs={{0,16},{8,24},{16,0},{24,8},{1,17},{9,25},{17,1},{25,9},{2,18},{10... | collective-permute-start | bytes 196616 | tf_op jit(solution)/shard_map/ppermute | solution.py:235
  50.0 1.2 %collective-permute-start.8 = (bf16[64,512]{1,0:T(8,128)(2,1)S(1)}, bf16[64,512]{1,0:T(8,128)(2,1)S(1)}, u32[]{:S(2)}, u32[]{:S(2)}) collective-permute-start(bf16[64,512]{1,0:T(8,128)(2,1)S(1)} %get-tuple-element.65), channel_id=1, source_target_pairs={{0,24},{8,0},{16,8},{24,16},{1,25},{9,1},{17,9},{25,17},{2,26},{10... | collective-permute-start | bytes 196616 | tf_op jit(solution)/shard_map/ppermute | solution.py:235
  51.2 3.1 %collective-permute-done.6.r1_ref = bf16[64,512]{1,0:T(8,128)(2,1)S(1)} collective-permute-done((bf16[64,512]{1,0:T(8,128)(2,1)S(1)}, bf16[64,512]{1,0:T(8,128)(2,1)S(1)}, u32[]{:S(2)}, u32[]{:S(2)}) %collective-permute-start.6) | collective-permute-done | bytes 65568 | tf_op jit(solution)/shard_map/ppermute | solution.py:235
  54.3 1.1 %collective-permute-done.7.r2_ref = bf16[64,512]{1,0:T(8,128)(2,1)S(1)} collective-permute-done((bf16[64,512]{1,0:T(8,128)(2,1)S(1)}, bf16[64,512]{1,0:T(8,128)(2,1)S(1)}, u32[]{:S(2)}, u32[]{:S(2)}) %collective-permute-start.7) | collective-permute-done | bytes 65568 | tf_op jit(solution)/shard_map/ppermute | solution.py:235
  55.6 15.2 %all_to_all.21.got_ref = bf16[8,56,512]{2,1,0:T(8,128)(2,1)S(1)} all-to-all(bf16[8,56,512]{2,1,0:T(8,128)(2,1)S(1)} %pack.1), channel_id=1, replica_groups=mesh['y'=4,'c'=2,'x'=4,'z'=8] {'z'}, dimensions={0} | all-to-all | bytes 917504 | tf_op jit(solution)/shard_map/all_to_all | solution.py:239
  70.7 0.9 unpack.1
  71.6 6.4 %all-to-all-start.3 = ((bf16[16,32,512]{2,1,0:T(8,128)(2,1)}), bf16[16,32,512]{2,1,0:T(8,128)(2,1)S(1)}, u32[]{:S(2)}, u32[]{:S(2)}) async-start(bf16[16,32,512]{2,1,0:T(8,128)(2,1)} %get-tuple-element.66), calls=%async_computation.3 | async-start | bytes 1048576 | tf_op jit(solution)/shard_map/all_to_all | solution.py:239
  78.0 2.6 %collective-permute-start.11 = (bf16[8,512]{1,0:T(8,128)(2,1)S(1)}, bf16[8,512]{1,0:T(8,128)(2,1)S(1)}, u32[]{:S(2)}, u32[]{:S(2)}) collective-permute-start(bf16[8,512]{1,0:T(8,128)(2,1)S(1)} %get-tuple-element.69), channel_id=1, source_target_pairs={{0,192},{64,0},{128,64},{192,128},{1,193},{65,1},{129,65},{193,129... | collective-permute-start | bytes 24584 | tf_op jit(solution)/shard_map/ppermute | solution.py:235
  81.8 3.7 %collective-permute-done.10.r2_ref = bf16[8,512]{1,0:T(8,128)(2,1)S(1)} collective-permute-done((bf16[8,512]{1,0:T(8,128)(2,1)S(1)}, bf16[8,512]{1,0:T(8,128)(2,1)S(1)}, u32[]{:S(2)}, u32[]{:S(2)}) %collective-permute-start.10) | collective-permute-done | bytes 8224 | tf_op jit(solution)/shard_map/ppermute | solution.py:235
  85.5 1.2 %grad.1 = f32[256,512]{1,0:T(8,128)} custom-call(s32[1]{0:T(128)S(6)} %copy.16.slot_ref, f32[256,512]{1,0:T(8,128)S(1)} %get-tuple-element.67.base_ref, bf16[4,64,256]{2,1,0:T(8,128)(2,1)S(1)} %bitcast.13, bf16[8,56,512]{2,1,0:T(8,128)(2,1)S(1)} %all_to_all.21.got_ref, bf16[8,512]{1,0:T(8,128)(2,1)S(1)} %collective-permute-done.9.r1_ref, ...), custom_call_target="tpu_custom_call" | custom-call | flops 4194304 | bytes 1048576 | tf_op jit(solution)/shard_map/grad/pallas_call | solution.py:30
  87.0 4.4 %collective-permute-start.12 = (bf16[512,512]{1,0:T(8,128)(2,1)S(1)}, bf16[512,512]{1,0:T(8,128)(2,1)S(1)}, u32[]{:S(2)}, u32[]{:S(2)}) collective-permute-start(bf16[512,512]{1,0:T(8,128)(2,1)S(1)} %bitcast.9), channel_id=1, source_target_pairs={{0,32},{32,0},{1,33},{33,1},{2,34},{34,2},{3,35},{35,3},{4,36},{36... | collective-permute-start | bytes 1572872 | tf_op jit(solution)/shard_map/ppermute | solution.py:231
  91.5 1.0 %mine.1 = (f32[512,512]{1,0:T(8,128)}, f32[512,512]{1,0:T(8,128)}) custom-call(bf16[512,512]{1,0:T(8,128)(2,1)S(1)} %bitcast.10), custom_call_target="tpu_custom_call" | custom-call | flops 4194304 | bytes 1048576 | tf_op jit(solution)/shard_map/mine/pallas_call | solution.py:30
  93.0 1.0 %other.1 = (f32[512,512]{1,0:T(8,128)}, f32[512,512]{1,0:T(8,128)}) custom-call(bf16[512,512]{1,0:T(8,128)(2,1)S(1)} %collective-permute-done.12.refs_0_, f32[512,512]{1,0:T(8,128)} %get-tuple-element.72.refs_1_, f32[512,512]{1,0:T(8,128)} %get-tuple-element.73.refs_2_), custom_call_target="tpu_custom_call", output_to_operand_aliasing={{0}: (1, {}), {1}: (2, {})} | custom-call | flops 4194304 | bytes 1048576 | tf_op jit(solution)/shard_map/other/pallas_call | solution.py:30
  (35 shorter events, 8.2 us)
Async XLA Ops:
  2.0 6.5 %collective-permute-start.2 = (bf16[1,512]{1,0:T(2,128)(2,1)S(1)}, bf16[1,512]{1,0:T(2,128)(2,1)S(1)}, u32[]{:S(2)}, u32[]{:S(2)}) collective-permute-start(bf16[1,512]{1,0:T(2,128)(2,1)S(1)} %constant_dynamic-slice_fusion), channel_id=1, source_target_pairs={{0,192},{64,0},{128,64},{192,128},{1,193},{65,1},{129,65},{193,129... | collective-permute-start | bytes 3080 | tf_op jit(solution)/shard_map/ppermute | solution.py:235
  5.5 3.9 %collective-permute-start.1 = (bf16[1,512]{1,0:T(2,128)(2,1)S(1)}, bf16[1,512]{1,0:T(2,128)(2,1)S(1)}, u32[]{:S(2)}, u32[]{:S(2)}) collective-permute-start(bf16[1,512]{1,0:T(2,128)(2,1)S(1)} %constant_dynamic-slice_fusion), channel_id=1, source_target_pairs={{0,128},{64,192},{128,0},{192,64},{1,129},{65,193},{129,1},{193,65... | collective-permute-start | bytes 3080 | tf_op jit(solution)/shard_map/ppermute | solution.py:235
  5.9 3.6 %collective-permute-start = (bf16[1,512]{1,0:T(2,128)(2,1)S(1)}, bf16[1,512]{1,0:T(2,128)(2,1)S(1)}, u32[]{:S(2)}, u32[]{:S(2)}) collective-permute-start(bf16[1,512]{1,0:T(2,128)(2,1)S(1)} %constant_dynamic-slice_fusion), channel_id=1, source_target_pairs={{0,64},{64,128},{128,192},{192,0},{1,65},{65,129},{129,193},{193,1... | collective-permute-start | bytes 3080 | tf_op jit(solution)/shard_map/ppermute | solution.py:235
  6.6 0.8 copy-start.6
  7.3 2.2 %copy-start = (bf16[256,512]{1,0:T(8,128)(2,1)S(1)}, bf16[256,512]{1,0:T(8,128)(2,1)}, u32[]{:S(2)}) copy-start(bf16[256,512]{1,0:T(8,128)(2,1)} %feat_ref.5) | copy-start | bytes 786436
  7.3 2.2 %copy-start.4 = (s32[1,32,4]{1,2,0:T(4,128)S(1)}, s32[1,32,4]{1,2,0:T(4,128)}, u32[]{:S(2)}) copy-start(s32[1,32,4]{1,2,0:T(4,128)} %param.14) | copy-start | bytes 1540
  7.4 2.2 %copy-start.5 = (s32[1,32]{1,0:T(1,128)S(1)}, s32[1,32]{1,0:T(1,128)}, u32[]{:S(2)}) copy-start(s32[1,32]{1,0:T(1,128)} %count_ref.1) | copy-start | bytes 388
  8.5 26.5 %copy-start.1 = (bf16[512,512]{1,0:T(8,128)(2,1)S(1)}, bf16[512,512]{1,0:T(8,128)(2,1)}, u32[]{:S(2)}) copy-start(bf16[512,512]{1,0:T(8,128)(2,1)} %ws_ref.3) | copy-start | bytes 1572868
  30.5 5.7 %collective-permute-start.3 = (bf16[32,8,512]{2,1,0:T(8,128)(2,1)S(1)}, bf16[32,8,512]{2,1,0:T(8,128)(2,1)S(1)}, u32[]{:S(2)}, u32[]{:S(2)}) collective-permute-start(bf16[32,8,512]{2,1,0:T(8,128)(2,1)S(1)} %all_to_all.20.got_ref), channel_id=1, source_target_pairs={{0,32},{32,0},{1,33},{33,1},{2,34},{34,2},{3,35},{35,3},{4,36},{36... | collective-permute-start | bytes 786440 | tf_op jit(solution)/shard_map/ppermute | solution.py:231
  35.0 1.2 %copy-start.2 = (bf16[512,512]{1,0:T(8,128)(2,1)S(1)}, bf16[512,512]{1,0:T(8,128)(2,1)}, u32[]{:S(2)}) copy-start(bf16[512,512]{1,0:T(8,128)(2,1)} %wn_ref.3) | copy-start | bytes 1572868
  35.0 1.2 %copy-start.3 = (bf16[256,512]{1,0:T(8,128)(2,1)S(1)}, bf16[256,512]{1,0:T(8,128)(2,1)}, u32[]{:S(2)}) copy-start(bf16[256,512]{1,0:T(8,128)(2,1)} %cot_ref.1) | copy-start | bytes 786436
  37.6 1.9 %collective-permute-start.4 = (bf16[512,512]{1,0:T(8,128)(2,1)S(1)}, bf16[512,512]{1,0:T(8,128)(2,1)S(1)}, u32[]{:S(2)}, u32[]{:S(2)}) collective-permute-start(bf16[512,512]{1,0:T(8,128)(2,1)S(1)} %get-tuple-element.59), channel_id=1, source_target_pairs={{0,32},{32,0},{1,33},{33,1},{2,34},{34,2},{3,35},{35,3},{4,36},{36... | collective-permute-start | bytes 1572872 | tf_op jit(solution)/shard_map/ppermute | solution.py:231
  40.4 15.1 %all-to-all-start.1 = ((bf16[16,32,512]{2,1,0:T(8,128)(2,1)}), bf16[16,32,512]{2,1,0:T(8,128)(2,1)S(1)}, u32[]{:S(2)}, u32[]{:S(2)}) async-start(bf16[16,32,512]{2,1,0:T(8,128)(2,1)} %half.1), calls=%async_computation.1 | async-start | bytes 1048576 | tf_op jit(solution)/shard_map/all_to_all | solution.py:239
  44.0 1.9 %collective-permute-start.5 = (bf16[256,512]{1,0:T(8,128)(2,1)S(1)}, bf16[256,512]{1,0:T(8,128)(2,1)S(1)}, u32[]{:S(2)}, u32[]{:S(2)}) collective-permute-start(bf16[256,512]{1,0:T(8,128)(2,1)S(1)} %get-tuple-element.61), channel_id=1, source_target_pairs={{0,32},{32,0},{1,33},{33,1},{2,34},{34,2},{3,35},{35,3},{4,36},{36... | collective-permute-start | bytes 786440 | tf_op jit(solution)/shard_map/ppermute | solution.py:231
  46.0 8.3 %collective-permute-start.6 = (bf16[64,512]{1,0:T(8,128)(2,1)S(1)}, bf16[64,512]{1,0:T(8,128)(2,1)S(1)}, u32[]{:S(2)}, u32[]{:S(2)}) collective-permute-start(bf16[64,512]{1,0:T(8,128)(2,1)S(1)} %get-tuple-element.63), channel_id=1, source_target_pairs={{0,8},{8,16},{16,24},{24,0},{1,9},{9,17},{17,25},{25,1},{2,10},{10... | collective-permute-start | bytes 196616 | tf_op jit(solution)/shard_map/ppermute | solution.py:235
  47.6 7.8 %collective-permute-start.7 = (bf16[64,512]{1,0:T(8,128)(2,1)S(1)}, bf16[64,512]{1,0:T(8,128)(2,1)S(1)}, u32[]{:S(2)}, u32[]{:S(2)}) collective-permute-start(bf16[64,512]{1,0:T(8,128)(2,1)S(1)} %get-tuple-element.64), channel_id=1, source_target_pairs={{0,16},{8,24},{16,0},{24,8},{1,17},{9,25},{17,1},{25,9},{2,18},{10... | collective-permute-start | bytes 196616 | tf_op jit(solution)/shard_map/ppermute | solution.py:235
  50.0 5.4 %collective-permute-start.8 = (bf16[64,512]{1,0:T(8,128)(2,1)S(1)}, bf16[64,512]{1,0:T(8,128)(2,1)S(1)}, u32[]{:S(2)}, u32[]{:S(2)}) collective-permute-start(bf16[64,512]{1,0:T(8,128)(2,1)S(1)} %get-tuple-element.65), channel_id=1, source_target_pairs={{0,24},{8,0},{16,8},{24,16},{1,25},{9,1},{17,9},{25,17},{2,26},{10... | collective-permute-start | bytes 196616 | tf_op jit(solution)/shard_map/ppermute | solution.py:235
  71.6 15.4 %all-to-all-start.3 = ((bf16[16,32,512]{2,1,0:T(8,128)(2,1)}), bf16[16,32,512]{2,1,0:T(8,128)(2,1)S(1)}, u32[]{:S(2)}, u32[]{:S(2)}) async-start(bf16[16,32,512]{2,1,0:T(8,128)(2,1)} %get-tuple-element.66), calls=%async_computation.3 | async-start | bytes 1048576 | tf_op jit(solution)/shard_map/all_to_all | solution.py:239
  78.0 3.7 %collective-permute-start.11 = (bf16[8,512]{1,0:T(8,128)(2,1)S(1)}, bf16[8,512]{1,0:T(8,128)(2,1)S(1)}, u32[]{:S(2)}, u32[]{:S(2)}) collective-permute-start(bf16[8,512]{1,0:T(8,128)(2,1)S(1)} %get-tuple-element.69), channel_id=1, source_target_pairs={{0,192},{64,0},{128,64},{192,128},{1,193},{65,1},{129,65},{193,129... | collective-permute-start | bytes 24584 | tf_op jit(solution)/shard_map/ppermute | solution.py:235
  80.6 4.9 %collective-permute-start.10 = (bf16[8,512]{1,0:T(8,128)(2,1)S(1)}, bf16[8,512]{1,0:T(8,128)(2,1)S(1)}, u32[]{:S(2)}, u32[]{:S(2)}) collective-permute-start(bf16[8,512]{1,0:T(8,128)(2,1)S(1)} %get-tuple-element.69), channel_id=1, source_target_pairs={{0,128},{64,192},{128,0},{192,64},{1,129},{65,193},{129,1},{193,65... | collective-permute-start | bytes 24584 | tf_op jit(solution)/shard_map/ppermute | solution.py:235
  81.2 4.3 %collective-permute-start.9 = (bf16[8,512]{1,0:T(8,128)(2,1)S(1)}, bf16[8,512]{1,0:T(8,128)(2,1)S(1)}, u32[]{:S(2)}, u32[]{:S(2)}) collective-permute-start(bf16[8,512]{1,0:T(8,128)(2,1)S(1)} %get-tuple-element.69), channel_id=1, source_target_pairs={{0,64},{64,128},{128,192},{192,0},{1,65},{65,129},{129,193},{193,1... | collective-permute-start | bytes 24584 | tf_op jit(solution)/shard_map/ppermute | solution.py:235
  87.0 6.0 %collective-permute-start.12 = (bf16[512,512]{1,0:T(8,128)(2,1)S(1)}, bf16[512,512]{1,0:T(8,128)(2,1)S(1)}, u32[]{:S(2)}, u32[]{:S(2)}) collective-permute-start(bf16[512,512]{1,0:T(8,128)(2,1)S(1)} %bitcast.9), channel_id=1, source_target_pairs={{0,32},{32,0},{1,33},{33,1},{2,34},{34,2},{3,35},{35,3},{4,36},{36... | collective-permute-start | bytes 1572872 | tf_op jit(solution)/shard_map/ppermute | solution.py:231

commit v6 on v5

--- a/solution.py
+++ b/solution.py
@@ -31,7 +31,7 @@
             kernel,
             out_shape=outs,
             in_specs=[scalar if i in smem else main if i in hbm else vector for i in range(len(args))],
-            out_specs=[main if hbm_out else vector] * len(outs),
+            out_specs=[main if hbm_out is True or (hbm_out and i in hbm_out) else vector for i in range(len(outs))],
             scratch_shapes=list(scratch),
             input_output_aliases=alias or {},
             name=name,
@@ -148,8 +148,20 @@
     base_ref[...] = dot(dz, ws_ref[...], 1, 1) + dot(ct_ref[:verts, :], edge)
 
 
-def half_kernel(keep_ref, got_ref, out_ref):
-    out_ref[...] = (keep_ref[...] + got_ref[...].astype(F32)).astype(BF).reshape(out_ref.shape)
+def half_kernel(keep_ref, got_ref, out_ref, buf, sem):
+    blocks, part, _ = buf.shape
+    step = blocks // 4
+    copies = []
+    for i in range(4):
+        rows = slice(i * step * part, (i + 1) * step * part)
+        total = (keep_ref[rows, :] + got_ref[rows, :].astype(F32)).astype(BF)
+        span = pl.ds(i * step, step)
+        buf[span] = total.reshape(step, part, total.shape[1])
+        copy = pltpu.make_async_copy(buf.at[span], out_ref.at[span], sem.at[i])
+        copy.start()
+        copies.append(copy)
+    for copy in copies:
+        copy.wait()
 
 
 def pair_kernel(mine_ref, got_ref, own_ref, s1_ref, s2_ref, s3_ref):
@@ -179,11 +191,15 @@
     out_ref[:, rows + 2 * PACK :, :] = join(r3, jnp.zeros_like(r3)).astype(BF)
 
 
-def unpack_kernel(got_ref, out_ref, hub_ref):
-    rows = out_ref.shape[1]
-    total = jnp.sum(got_ref[:, :rows, :].astype(F32), axis=0).astype(BF)
-    out_ref[...] = jnp.broadcast_to(total[None], out_ref.shape)
+def unpack_kernel(got_ref, out_ref, hub_ref, buf, sem):
+    rows = buf.shape[0]
+    buf[...] = jnp.sum(got_ref[:, :rows, :].astype(F32), axis=0).astype(BF)
+    copies = [pltpu.make_async_copy(buf, out_ref.at[i], sem.at[i]) for i in range(out_ref.shape[0])]
+    for copy in copies:
+        copy.start()
     hub_ref[...] = jnp.sum(got_ref[:, rows : rows + PACK, :].astype(F32), axis=0).astype(BF)
+    for copy in copies:
+        copy.wait()
 
 
 def grad_kernel(slot_ref, base_ref, sel_ref, got_ref, r1_ref, r2_ref, r3_ref, out_ref):
@@ -283,7 +299,9 @@
     part = width // (NY * NX)
     other_got = swap_core(other)
     w_keep, mine = lax.optimization_barrier((w_keep, mine))
-    blocks = call(half_kernel, [((NY * NX, part, width), BF)], "half")(w_keep, w_got)[0]
+    blocks = call(half_kernel, [((NY * NX, part, width), BF)], "half", hbm_out=True,
+        scratch=(pltpu.VMEM((NY * NX, part, width), BF), pltpu.SemaphoreType.DMA((4,))),
+    )(w_keep, w_got)[0]
     second = exchange(blocks, ("y", "x"))
 
     split = (NX, NZ * PACK, width)
@@ -293,7 +311,9 @@
     b_in = [shift(b_out[k - 1], "x", k) for k in (1, 2, 3)]
     pack = call(pack_kernel, [((NZ, part + 3 * PACK, width), BF)], "pack")(second, b_own, *b_in)[0]
     third = exchange(pack, "z")
-    copies, hub = call(unpack_kernel, [((NY * NX, part, width), BF), ((PACK, width), BF)], "unpack")(third)
+    copies, hub = call(unpack_kernel, [((NY * NX, part, width), BF), ((PACK, width), BF)], "unpack", hbm_out=(0,),
+        scratch=(pltpu.VMEM((part, width), BF), pltpu.SemaphoreType.DMA((NY * NX,))),
+    )(third)
     fourth = exchange(copies, ("y", "x")).reshape(width, width)
     hub_back = [shift(hub, "y", k) for k in (1, 2, 3)]
     grad_features = call(grad_kernel, [((verts, width), F32)], "grad", smem=(0,))(

time: 94.5 us -> 94.6 us (level)
  no operation moved by 1% of the time
where the time goes in v6:
time: 94.6 us; the launch traced here: 94.1 us
  blocking collectives  35.7 us (38%)
  starting transfers between devices  33.7 us (36%)
  waiting for transfers between devices  12.2 us (13%)
  Pallas kernels  9.64 us (10%)
  local copies, waits for them, and re-layouts  1.49 us (2%)
  between operations  1.39 us (1%)
    all_to_all x2, blocking collectives, exchange(): return lax.all_to_all(v, axes, split_axis=0, concat_axis=0, tiled=True)  35.7 us
    ppermute x9, starting transfers between devices, shift(): return lax.ppermute(v, axis, [(i, (i + k) % 4) for i in range(4)])  13.6 us
    ppermute x4, starting transfers between devices, swap_core(): return lax.ppermute(v, 'c', [(0, 1), (1, 0)])  10.1 us
    all_to_all x2, starting transfers between devices, exchange(): return lax.all_to_all(v, axes, split_axis=0, concat_axis=0, tiled=True)  10.1 us
    pallas_call x12, Pallas kernels, run(): pl.pallas_call(kernel, out_shape=outs, in_specs=[scalar if i in smem else...  9.64 us
    ppermute x9, waiting for transfers between devices, shift(): return lax.ppermute(v, axis, [(i, (i + k) % 4) for i in range(4)])  9.02 us
    ppermute x4, waiting for transfers between devices, swap_core(): return lax.ppermute(v, 'c', [(0, 1), (1, 0)])  2.85 us
  transfers between devices with their start and end apart: 15, of which 10 were waited for; matrix products, arithmetic and copies ran while one was open for 0% of the time, Pallas kernels for 5%

profile of v6, /device:TPU:1, one launch (start us, length us, event | category | flops | bytes accessed | tf_op | source)
XLA Modules:
  0.0 94.1 jit_solution(14977186663766280323)
XLA Ops:
  2.0 3.6 %collective-permute-start.2 = (bf16[1,512]{1,0:T(2,128)(2,1)S(1)}, bf16[1,512]{1,0:T(2,128)(2,1)S(1)}, u32[]{:S(2)}, u32[]{:S(2)}) collective-permute-start(bf16[1,512]{1,0:T(2,128)(2,1)S(1)} %constant_dynamic-slice_fusion), channel_id=1, source_target_pairs={{0,192},{64,0},{128,64},{192,128},{1,193},{65,1},{129,65},{193,129... | collective-permute-start | bytes 3080 | tf_op jit(solution)/shard_map/ppermute | solution.py:251
  7.4 1.1 %count.1 = (bf16[512,256]{1,0:T(8,128)(2,1)S(1)}, bf16[256,512]{1,0:T(8,128)(2,1)S(1)}, f32[256,1]{1,0:T(8,128)S(1)}, s32[32,256]{1,0:T(8,128)S(1)}) custom-call(s32[32,256]{1,0:T(8,128)S(1)} %bitcast.15), custom_call_target="tpu_custom_call" | custom-call | flops 268435456 | bytes 1048576 | tf_op jit(solution)/shard_map/count/pallas_call | solution.py:30
  8.5 1.0 %collective-permute-done.1.r2_ref = bf16[1,512]{1,0:T(2,128)(2,1)S(1)} collective-permute-done((bf16[1,512]{1,0:T(2,128)(2,1)S(1)}, bf16[1,512]{1,0:T(2,128)(2,1)S(1)}, u32[]{:S(2)}, u32[]{:S(2)}) %collective-permute-start.1) | collective-permute-done | bytes 1056 | tf_op jit(solution)/shard_map/ppermute | solution.py:251
  10.0 20.5 %all_to_all.20.got_ref = bf16[32,8,512]{2,1,0:T(8,128)(2,1)S(1)} all-to-all(bf16[32,8,512]{2,1,0:T(8,128)(2,1)S(1)} %get-tuple-element.51), channel_id=1, replica_groups=mesh['y'=4,'c'=2,'x'=4,'z'=8] {'x','z'}, dimensions={0} | all-to-all | bytes 524288 | tf_op jit(solution)/shard_map/all_to_all | solution.py:255
  30.5 4.5 %collective-permute-start.3 = (bf16[32,8,512]{2,1,0:T(8,128)(2,1)S(1)}, bf16[32,8,512]{2,1,0:T(8,128)(2,1)S(1)}, u32[]{:S(2)}, u32[]{:S(2)}) collective-permute-start(bf16[32,8,512]{2,1,0:T(8,128)(2,1)S(1)} %all_to_all.20.got_ref), channel_id=1, source_target_pairs={{0,32},{32,0},{1,33},{33,1},{2,34},{34,2},{3,35},{35,3},{4,36},{36... | collective-permute-start | bytes 786440 | tf_op jit(solution)/shard_map/ppermute | solution.py:247
  36.2 1.4 %forward.1 = (bf16[256,512]{1,0:T(8,128)(2,1)}, bf16[256,512]{1,0:T(8,128)(2,1)S(1)}, bf16[512,512]{1,0:T(8,128)(2,1)S(1)}, f32[512,512]{1,0:T(8,128)S(1)}) custom-call(bf16[256,512]{1,0:T(8,128)(2,1)S(1)} %copy-done, bf16[256,512]{1,0:T(8,128)(2,1)S(1)} %copy-done.3, bf16[512,512]{1,0:T(8,128)(2,1)S(1)} %copy-done.2, ...), custom_call_target="tpu_custom_call" | custom-call | flops 4194304 | bytes 1048576 | tf_op jit(solution)/shard_map/forward/pallas_call | solution.py:30
  37.9 0.8 backward.1
  39.5 0.8 half.1
  40.3 3.7 %all-to-all-start.1 = ((bf16[16,32,512]{2,1,0:T(8,128)(2,1)}), bf16[16,32,512]{2,1,0:T(8,128)(2,1)S(1)}, u32[]{:S(2)}, u32[]{:S(2)}) async-start(bf16[16,32,512]{2,1,0:T(8,128)(2,1)} %half.1), calls=%async_computation.1 | async-start | bytes 1048576 | tf_op jit(solution)/shard_map/all_to_all | solution.py:255
  44.7 1.2 %collective-permute-done.5 = bf16[256,512]{1,0:T(8,128)(2,1)S(1)} collective-permute-done((bf16[256,512]{1,0:T(8,128)(2,1)S(1)}, bf16[256,512]{1,0:T(8,128)(2,1)S(1)}, u32[]{:S(2)}, u32[]{:S(2)}) %collective-permute-start.5) | collective-permute-done | bytes 262176 | tf_op jit(solution)/shard_map/ppermute | solution.py:247
  45.9 1.6 %collective-permute-start.6 = (bf16[64,512]{1,0:T(8,128)(2,1)S(1)}, bf16[64,512]{1,0:T(8,128)(2,1)S(1)}, u32[]{:S(2)}, u32[]{:S(2)}) collective-permute-start(bf16[64,512]{1,0:T(8,128)(2,1)S(1)} %get-tuple-element.63), channel_id=1, source_target_pairs={{0,8},{8,16},{16,24},{24,0},{1,9},{9,17},{17,25},{25,1},{2,10},{10... | collective-permute-start | bytes 196616 | tf_op jit(solution)/shard_map/ppermute | solution.py:251
  47.6 2.4 %collective-permute-start.7 = (bf16[64,512]{1,0:T(8,128)(2,1)S(1)}, bf16[64,512]{1,0:T(8,128)(2,1)S(1)}, u32[]{:S(2)}, u32[]{:S(2)}) collective-permute-start(bf16[64,512]{1,0:T(8,128)(2,1)S(1)} %get-tuple-element.64), channel_id=1, source_target_pairs={{0,16},{8,24},{16,0},{24,8},{1,17},{9,25},{17,1},{25,9},{2,18},{10... | collective-permute-start | bytes 196616 | tf_op jit(solution)/shard_map/ppermute | solution.py:251
  50.0 1.2 %collective-permute-start.8 = (bf16[64,512]{1,0:T(8,128)(2,1)S(1)}, bf16[64,512]{1,0:T(8,128)(2,1)S(1)}, u32[]{:S(2)}, u32[]{:S(2)}) collective-permute-start(bf16[64,512]{1,0:T(8,128)(2,1)S(1)} %get-tuple-element.65), channel_id=1, source_target_pairs={{0,24},{8,0},{16,8},{24,16},{1,25},{9,1},{17,9},{25,17},{2,26},{10... | collective-permute-start | bytes 196616 | tf_op jit(solution)/shard_map/ppermute | solution.py:251
  51.2 3.1 %collective-permute-done.6.r1_ref = bf16[64,512]{1,0:T(8,128)(2,1)S(1)} collective-permute-done((bf16[64,512]{1,0:T(8,128)(2,1)S(1)}, bf16[64,512]{1,0:T(8,128)(2,1)S(1)}, u32[]{:S(2)}, u32[]{:S(2)}) %collective-permute-start.6) | collective-permute-done | bytes 65568 | tf_op jit(solution)/shard_map/ppermute | solution.py:251
  54.3 1.1 %collective-permute-done.7.r2_ref = bf16[64,512]{1,0:T(8,128)(2,1)S(1)} collective-permute-done((bf16[64,512]{1,0:T(8,128)(2,1)S(1)}, bf16[64,512]{1,0:T(8,128)(2,1)S(1)}, u32[]{:S(2)}, u32[]{:S(2)}) %collective-permute-start.7) | collective-permute-done | bytes 65568 | tf_op jit(solution)/shard_map/ppermute | solution.py:251
  55.6 15.2 %all_to_all.21.got_ref = bf16[8,56,512]{2,1,0:T(8,128)(2,1)S(1)} all-to-all(bf16[8,56,512]{2,1,0:T(8,128)(2,1)S(1)} %pack.1), channel_id=1, replica_groups=mesh['y'=4,'c'=2,'x'=4,'z'=8] {'z'}, dimensions={0} | all-to-all | bytes 917504 | tf_op jit(solution)/shard_map/all_to_all | solution.py:255
  70.7 1.0 %unpack.1 = (bf16[16,32,512]{2,1,0:T(8,128)(2,1)}, bf16[8,512]{1,0:T(8,128)(2,1)S(1)}) custom-call(bf16[8,56,512]{2,1,0:T(8,128)(2,1)S(1)} %all_to_all.21.got_ref), custom_call_target="tpu_custom_call" | custom-call | flops 4194304 | bytes 1048576 | tf_op jit(solution)/shard_map/unpack/pallas_call | solution.py:30
  71.7 6.4 %all-to-all-start.3 = ((bf16[16,32,512]{2,1,0:T(8,128)(2,1)}), bf16[16,32,512]{2,1,0:T(8,128)(2,1)S(1)}, u32[]{:S(2)}, u32[]{:S(2)}) async-start(bf16[16,32,512]{2,1,0:T(8,128)(2,1)} %get-tuple-element.66), calls=%async_computation.3 | async-start | bytes 1048576 | tf_op jit(solution)/shard_map/all_to_all | solution.py:255
  78.1 2.6 %collective-permute-start.11 = (bf16[8,512]{1,0:T(8,128)(2,1)S(1)}, bf16[8,512]{1,0:T(8,128)(2,1)S(1)}, u32[]{:S(2)}, u32[]{:S(2)}) collective-permute-start(bf16[8,512]{1,0:T(8,128)(2,1)S(1)} %get-tuple-element.69), channel_id=1, source_target_pairs={{0,192},{64,0},{128,64},{192,128},{1,193},{65,1},{129,65},{193,129... | collective-permute-start | bytes 24584 | tf_op jit(solution)/shard_map/ppermute | solution.py:251
  81.8 3.7 %collective-permute-done.10.r2_ref = bf16[8,512]{1,0:T(8,128)(2,1)S(1)} collective-permute-done((bf16[8,512]{1,0:T(8,128)(2,1)S(1)}, bf16[8,512]{1,0:T(8,128)(2,1)S(1)}, u32[]{:S(2)}, u32[]{:S(2)}) %collective-permute-start.10) | collective-permute-done | bytes 8224 | tf_op jit(solution)/shard_map/ppermute | solution.py:251
  85.5 1.2 %grad.1 = f32[256,512]{1,0:T(8,128)} custom-call(s32[1]{0:T(128)S(6)} %copy.16.slot_ref, f32[256,512]{1,0:T(8,128)S(1)} %get-tuple-element.67.base_ref, bf16[4,64,256]{2,1,0:T(8,128)(2,1)S(1)} %bitcast.13, bf16[8,56,512]{2,1,0:T(8,128)(2,1)S(1)} %all_to_all.21.got_ref, bf16[8,512]{1,0:T(8,128)(2,1)S(1)} %collective-permute-done.9.r1_ref, ...), custom_call_target="tpu_custom_call" | custom-call | flops 4194304 | bytes 1048576 | tf_op jit(solution)/shard_map/grad/pallas_call | solution.py:30
  87.1 4.4 %collective-permute-start.12 = (bf16[512,512]{1,0:T(8,128)(2,1)S(1)}, bf16[512,512]{1,0:T(8,128)(2,1)S(1)}, u32[]{:S(2)}, u32[]{:S(2)}) collective-permute-start(bf16[512,512]{1,0:T(8,128)(2,1)S(1)} %bitcast.9), channel_id=1, source_target_pairs={{0,32},{32,0},{1,33},{33,1},{2,34},{34,2},{3,35},{35,3},{4,36},{36... | collective-permute-start | bytes 1572872 | tf_op jit(solution)/shard_map/ppermute | solution.py:247
  91.6 1.0 %mine.1 = (f32[512,512]{1,0:T(8,128)}, f32[512,512]{1,0:T(8,128)}) custom-call(bf16[512,512]{1,0:T(8,128)(2,1)S(1)} %bitcast.10), custom_call_target="tpu_custom_call" | custom-call | flops 4194304 | bytes 1048576 | tf_op jit(solution)/shard_map/mine/pallas_call | solution.py:30
  93.1 1.0 %other.1 = (f32[512,512]{1,0:T(8,128)}, f32[512,512]{1,0:T(8,128)}) custom-call(bf16[512,512]{1,0:T(8,128)(2,1)S(1)} %collective-permute-done.12.refs_0_, f32[512,512]{1,0:T(8,128)} %get-tuple-element.72.refs_1_, f32[512,512]{1,0:T(8,128)} %get-tuple-element.73.refs_2_), custom_call_target="tpu_custom_call", output_to_operand_aliasing={{0}: (1, {}), {1}: (2, {})} | custom-call | flops 4194304 | bytes 1048576 | tf_op jit(solution)/shard_map/other/pallas_call | solution.py:30
  (35 shorter events, 8.2 us)
Async XLA Ops:
  2.0 6.5 %collective-permute-start.2 = (bf16[1,512]{1,0:T(2,128)(2,1)S(1)}, bf16[1,512]{1,0:T(2,128)(2,1)S(1)}, u32[]{:S(2)}, u32[]{:S(2)}) collective-permute-start(bf16[1,512]{1,0:T(2,128)(2,1)S(1)} %constant_dynamic-slice_fusion), channel_id=1, source_target_pairs={{0,192},{64,0},{128,64},{192,128},{1,193},{65,1},{129,65},{193,129... | collective-permute-start | bytes 3080 | tf_op jit(solution)/shard_map/ppermute | solution.py:251
  5.5 3.9 %collective-permute-start.1 = (bf16[1,512]{1,0:T(2,128)(2,1)S(1)}, bf16[1,512]{1,0:T(2,128)(2,1)S(1)}, u32[]{:S(2)}, u32[]{:S(2)}) collective-permute-start(bf16[1,512]{1,0:T(2,128)(2,1)S(1)} %constant_dynamic-slice_fusion), channel_id=1, source_target_pairs={{0,128},{64,192},{128,0},{192,64},{1,129},{65,193},{129,1},{193,65... | collective-permute-start | bytes 3080 | tf_op jit(solution)/shard_map/ppermute | solution.py:251
  5.9 3.6 %collective-permute-start = (bf16[1,512]{1,0:T(2,128)(2,1)S(1)}, bf16[1,512]{1,0:T(2,128)(2,1)S(1)}, u32[]{:S(2)}, u32[]{:S(2)}) collective-permute-start(bf16[1,512]{1,0:T(2,128)(2,1)S(1)} %constant_dynamic-slice_fusion), channel_id=1, source_target_pairs={{0,64},{64,128},{128,192},{192,0},{1,65},{65,129},{129,193},{193,1... | collective-permute-start | bytes 3080 | tf_op jit(solution)/shard_map/ppermute | solution.py:251
  6.6 0.8 copy-start.6
  7.3 2.2 %copy-start = (bf16[256,512]{1,0:T(8,128)(2,1)S(1)}, bf16[256,512]{1,0:T(8,128)(2,1)}, u32[]{:S(2)}) copy-start(bf16[256,512]{1,0:T(8,128)(2,1)} %feat_ref.5) | copy-start | bytes 786436
  7.3 2.2 %copy-start.4 = (s32[1,32,4]{1,2,0:T(4,128)S(1)}, s32[1,32,4]{1,2,0:T(4,128)}, u32[]{:S(2)}) copy-start(s32[1,32,4]{1,2,0:T(4,128)} %param.14) | copy-start | bytes 1540
  7.4 2.2 %copy-start.5 = (s32[1,32]{1,0:T(1,128)S(1)}, s32[1,32]{1,0:T(1,128)}, u32[]{:S(2)}) copy-start(s32[1,32]{1,0:T(1,128)} %count_ref.1) | copy-start | bytes 388
  8.5 26.5 %copy-start.1 = (bf16[512,512]{1,0:T(8,128)(2,1)S(1)}, bf16[512,512]{1,0:T(8,128)(2,1)}, u32[]{:S(2)}) copy-start(bf16[512,512]{1,0:T(8,128)(2,1)} %ws_ref.3) | copy-start | bytes 1572868
  30.5 5.7 %collective-permute-start.3 = (bf16[32,8,512]{2,1,0:T(8,128)(2,1)S(1)}, bf16[32,8,512]{2,1,0:T(8,128)(2,1)S(1)}, u32[]{:S(2)}, u32[]{:S(2)}) collective-permute-start(bf16[32,8,512]{2,1,0:T(8,128)(2,1)S(1)} %all_to_all.20.got_ref), channel_id=1, source_target_pairs={{0,32},{32,0},{1,33},{33,1},{2,34},{34,2},{3,35},{35,3},{4,36},{36... | collective-permute-start | bytes 786440 | tf_op jit(solution)/shard_map/ppermute | solution.py:247
  35.0 1.2 %copy-start.2 = (bf16[512,512]{1,0:T(8,128)(2,1)S(1)}, bf16[512,512]{1,0:T(8,128)(2,1)}, u32[]{:S(2)}) copy-start(bf16[512,512]{1,0:T(8,128)(2,1)} %wn_ref.3) | copy-start | bytes 1572868
  35.0 1.2 %copy-start.3 = (bf16[256,512]{1,0:T(8,128)(2,1)S(1)}, bf16[256,512]{1,0:T(8,128)(2,1)}, u32[]{:S(2)}) copy-start(bf16[256,512]{1,0:T(8,128)(2,1)} %cot_ref.1) | copy-start | bytes 786436
  37.6 1.9 %collective-permute-start.4 = (bf16[512,512]{1,0:T(8,128)(2,1)S(1)}, bf16[512,512]{1,0:T(8,128)(2,1)S(1)}, u32[]{:S(2)}, u32[]{:S(2)}) collective-permute-start(bf16[512,512]{1,0:T(8,128)(2,1)S(1)} %get-tuple-element.59), channel_id=1, source_target_pairs={{0,32},{32,0},{1,33},{33,1},{2,34},{34,2},{3,35},{35,3},{4,36},{36... | collective-permute-start | bytes 1572872 | tf_op jit(solution)/shard_map/ppermute | solution.py:247
  40.3 15.1 %all-to-all-start.1 = ((bf16[16,32,512]{2,1,0:T(8,128)(2,1)}), bf16[16,32,512]{2,1,0:T(8,128)(2,1)S(1)}, u32[]{:S(2)}, u32[]{:S(2)}) async-start(bf16[16,32,512]{2,1,0:T(8,128)(2,1)} %half.1), calls=%async_computation.1 | async-start | bytes 1048576 | tf_op jit(solution)/shard_map/all_to_all | solution.py:255
  44.0 1.9 %collective-permute-start.5 = (bf16[256,512]{1,0:T(8,128)(2,1)S(1)}, bf16[256,512]{1,0:T(8,128)(2,1)S(1)}, u32[]{:S(2)}, u32[]{:S(2)}) collective-permute-start(bf16[256,512]{1,0:T(8,128)(2,1)S(1)} %get-tuple-element.61), channel_id=1, source_target_pairs={{0,32},{32,0},{1,33},{33,1},{2,34},{34,2},{3,35},{35,3},{4,36},{36... | collective-permute-start | bytes 786440 | tf_op jit(solution)/shard_map/ppermute | solution.py:247
  45.9 8.3 %collective-permute-start.6 = (bf16[64,512]{1,0:T(8,128)(2,1)S(1)}, bf16[64,512]{1,0:T(8,128)(2,1)S(1)}, u32[]{:S(2)}, u32[]{:S(2)}) collective-permute-start(bf16[64,512]{1,0:T(8,128)(2,1)S(1)} %get-tuple-element.63), channel_id=1, source_target_pairs={{0,8},{8,16},{16,24},{24,0},{1,9},{9,17},{17,25},{25,1},{2,10},{10... | collective-permute-start | bytes 196616 | tf_op jit(solution)/shard_map/ppermute | solution.py:251
  47.6 7.8 %collective-permute-start.7 = (bf16[64,512]{1,0:T(8,128)(2,1)S(1)}, bf16[64,512]{1,0:T(8,128)(2,1)S(1)}, u32[]{:S(2)}, u32[]{:S(2)}) collective-permute-start(bf16[64,512]{1,0:T(8,128)(2,1)S(1)} %get-tuple-element.64), channel_id=1, source_target_pairs={{0,16},{8,24},{16,0},{24,8},{1,17},{9,25},{17,1},{25,9},{2,18},{10... | collective-permute-start | bytes 196616 | tf_op jit(solution)/shard_map/ppermute | solution.py:251
  50.0 5.4 %collective-permute-start.8 = (bf16[64,512]{1,0:T(8,128)(2,1)S(1)}, bf16[64,512]{1,0:T(8,128)(2,1)S(1)}, u32[]{:S(2)}, u32[]{:S(2)}) collective-permute-start(bf16[64,512]{1,0:T(8,128)(2,1)S(1)} %get-tuple-element.65), channel_id=1, source_target_pairs={{0,24},{8,0},{16,8},{24,16},{1,25},{9,1},{17,9},{25,17},{2,26},{10... | collective-permute-start | bytes 196616 | tf_op jit(solution)/shard_map/ppermute | solution.py:251
  71.7 15.4 %all-to-all-start.3 = ((bf16[16,32,512]{2,1,0:T(8,128)(2,1)}), bf16[16,32,512]{2,1,0:T(8,128)(2,1)S(1)}, u32[]{:S(2)}, u32[]{:S(2)}) async-start(bf16[16,32,512]{2,1,0:T(8,128)(2,1)} %get-tuple-element.66), calls=%async_computation.3 | async-start | bytes 1048576 | tf_op jit(solution)/shard_map/all_to_all | solution.py:255
  78.1 3.7 %collective-permute-start.11 = (bf16[8,512]{1,0:T(8,128)(2,1)S(1)}, bf16[8,512]{1,0:T(8,128)(2,1)S(1)}, u32[]{:S(2)}, u32[]{:S(2)}) collective-permute-start(bf16[8,512]{1,0:T(8,128)(2,1)S(1)} %get-tuple-element.69), channel_id=1, source_target_pairs={{0,192},{64,0},{128,64},{192,128},{1,193},{65,1},{129,65},{193,129... | collective-permute-start | bytes 24584 | tf_op jit(solution)/shard_map/ppermute | solution.py:251
  80.7 4.9 %collective-permute-start.10 = (bf16[8,512]{1,0:T(8,128)(2,1)S(1)}, bf16[8,512]{1,0:T(8,128)(2,1)S(1)}, u32[]{:S(2)}, u32[]{:S(2)}) collective-permute-start(bf16[8,512]{1,0:T(8,128)(2,1)S(1)} %get-tuple-element.69), channel_id=1, source_target_pairs={{0,128},{64,192},{128,0},{192,64},{1,129},{65,193},{129,1},{193,65... | collective-permute-start | bytes 24584 | tf_op jit(solution)/shard_map/ppermute | solution.py:251
  81.3 4.3 %collective-permute-start.9 = (bf16[8,512]{1,0:T(8,128)(2,1)S(1)}, bf16[8,512]{1,0:T(8,128)(2,1)S(1)}, u32[]{:S(2)}, u32[]{:S(2)}) collective-permute-start(bf16[8,512]{1,0:T(8,128)(2,1)S(1)} %get-tuple-element.69), channel_id=1, source_target_pairs={{0,64},{64,128},{128,192},{192,0},{1,65},{65,129},{129,193},{193,1... | collective-permute-start | bytes 24584 | tf_op jit(solution)/shard_map/ppermute | solution.py:251
  87.1 6.0 %collective-permute-start.12 = (bf16[512,512]{1,0:T(8,128)(2,1)S(1)}, bf16[512,512]{1,0:T(8,128)(2,1)S(1)}, u32[]{:S(2)}, u32[]{:S(2)}) collective-permute-start(bf16[512,512]{1,0:T(8,128)(2,1)S(1)} %bitcast.9), channel_id=1, source_target_pairs={{0,32},{32,0},{1,33},{33,1},{2,34},{34,2},{3,35},{35,3},{4,36},{36... | collective-permute-start | bytes 1572872 | tf_op jit(solution)/shard_map/ppermute | solution.py:247
